TPU v7x, 256 devices: a whole 4x4x8 slice. The times are simulated.
256 devices in a mesh: member: 2 (over y_lo), lat: 4 (over x), lon: 32 (over z, y_hi, core).
Axes of the slice: x: 4, y: 4 (y_hi: 2, y_lo: 2; y = y_hi * 2 + y_lo), z: 8, core: 2. Of those that a mesh axis runs over, the one named last changes fastest.
Arguments:
- features: bfloat16 [2, 720, 1440, 128], P('member', 'lat', 'lon'), may hold values from -6 to 6
- present_condition: bfloat16 [2, 720, 1440, 80], P('member', 'lat', 'lon'), may hold values from -6 to 6
- target: bfloat16 [720, 1440, 80], P('lat', 'lon'), may hold values from -8 to 8
- filter_weights_tensor: bfloat16 [3, 3, 128, 80], replicated, may hold values from -0.1875 to 0.1875
Outputs:
- predicted_outputs: bfloat16 [2, 720, 1440, 80], P('member', 'lat', 'lon')
- objective_mean: float32 [], replicated
- hidden_state_slope: bfloat16 [2, 720, 1440, 128], P('member', 'lat', 'lon')
- filter_weights_slope: float32 [3, 3, 128, 80], replicated
All inputs are finite; a program needn't handle non-finite values.
Results may differ from a plain program's by a relative error of at most 0.0095.
Values may be sent and summed in bfloat16 or wider, within the bound.
No kernel may reach another device: no remote copies, remote signals or barrier semaphores. Data moves between devices by JAX's collectives and lax.ppermute only.
A program may use at most 128 MiB of HBM per device.

v0:
```python
import math

import jax
import jax.numpy as jnp
from jax import lax
from jax.sharding import PartitionSpec as P

epsilon = 1e-06


def padded(block, sides, width, periodic):
    for axis, dim in sides:
        count = lax.axis_size(axis)
        forward = [(i, i + 1) for i in range(count - 1)]
        if periodic:
            forward.append((count - 1, 0))
        backward = [(target, source) for source, target in forward]
        low = lax.ppermute(
            lax.slice_in_dim(block, block.shape[dim] - width, None, axis=dim), axis, forward
        )
        high = lax.ppermute(lax.slice_in_dim(block, 0, width, axis=dim), axis, backward)
        block = jnp.concatenate([low, block, high], axis=dim)
    return block


def partner(value, axis, distance):
    mask = 2**distance
    pairs = [(source, source ^ mask) for source in range(lax.axis_size(axis))]
    return lax.ppermute(value, axis, pairs)


def stencil_filter_step(haloed_grid_array, weights_hwio):
    result = lax.conv_general_dilated(
        haloed_grid_array[None],
        weights_hwio,
        (1, 1),
        "VALID",
        dimension_numbers=("NHWC", "HWIO", "NHWC"),
        preferred_element_type=jnp.float32,
    )
    return result[0]


def latitude_weights(row_index, total_rows):
    scale = math.pi / total_rows
    angles = 0.5 * math.pi - (row_index.astype(jnp.float32) + 0.5) * scale
    every_row = (
        0.5 * math.pi - (jnp.arange(total_rows, dtype=jnp.int32).astype(jnp.float32) + 0.5) * scale
    )
    return jnp.cos(angles) / jnp.mean(jnp.cos(every_row))


def tap_products(haloed_grid_array, cotangent):
    lat_rows, lon_cols, channels = cotangent.shape
    inputs = haloed_grid_array.shape[2]
    flat_grad = cotangent.reshape(lat_rows * lon_cols, channels)
    stacked = []
    for row_tap in range(3):
        across = []
        for col_tap in range(3):
            window = haloed_grid_array[
                row_tap : row_tap + lat_rows, col_tap : col_tap + lon_cols
            ].reshape(lat_rows * lon_cols, inputs)
            across.append(
                lax.dot_general(
                    window, flat_grad, (((0,), (0,)), ((), ())), preferred_element_type=jnp.float32
                )
            )
        stacked.append(jnp.stack(across))
    return jnp.stack(stacked)


def extend_features(field):
    widened = padded(field, (("lon", 1),), 1, True)
    return padded(widened, (("lat", 0),), 1, False)


def extend_cotangent(field):
    widened = padded(field, (("lon", 1),), 1, True)
    return padded(widened, (("lat", 0),), 1, False)


def local(features, present_condition, target, filter_weights_tensor):
    lat_rows = features.shape[1]
    lon_cols = features.shape[2]
    total_rows = lat_rows * lax.axis_size("lat")
    total_cols = lon_cols * lax.axis_size("lon")
    haloed_grid_array = extend_features(features[0])
    predicted_outputs = (
        present_condition[0].astype(jnp.float32)
        + stencil_filter_step(haloed_grid_array, filter_weights_tensor)
    ).astype(jnp.bfloat16)
    companion_sample = partner(predicted_outputs, "member", 0)
    truth = target.astype(jnp.float32)
    energy_metrics = predicted_outputs.astype(jnp.float32)
    misfit = energy_metrics - truth
    errors = jnp.sqrt(jnp.sum(misfit * misfit, axis=-1) + epsilon)
    spread = energy_metrics - companion_sample.astype(jnp.float32)
    pair = jnp.sqrt(jnp.sum(spread * spread, axis=-1) + epsilon)
    row_index = lax.axis_index("lat") * lat_rows + jnp.arange(lat_rows, dtype=jnp.int32)
    weights = latitude_weights(row_index, total_rows)[:, None]
    local_total = jnp.sum(weights * (0.5 * errors - 0.25 * pair))
    cotangent = (
        weights[..., None] * (0.5 * misfit / errors[..., None] - 0.5 * spread / pair[..., None])
    ).astype(jnp.bfloat16)
    flipped = jnp.transpose(filter_weights_tensor[::-1, ::-1], (0, 1, 3, 2))
    hidden_state_slope = stencil_filter_step(extend_cotangent(cotangent), flipped).astype(
        jnp.bfloat16
    )
    partial_grad = tap_products(haloed_grid_array, cotangent)
    summed_grad, total = lax.psum((partial_grad, local_total), ("member", "lat", "lon"))
    objective_mean = total / (total_rows * total_cols)
    filter_weights_slope = summed_grad / math.sqrt(2.0 * total_rows * total_cols)
    return (predicted_outputs[None], objective_mean, hidden_state_slope[None], filter_weights_slope)


def solution(mesh):
    in_specs = (
        P("member", "lat", "lon", None),
        P("member", "lat", "lon", None),
        P("lat", "lon", None),
        P(),
    )
    out_specs = (P("member", "lat", "lon", None), P(), P("member", "lat", "lon", None), P())
    return jax.shard_map(local, mesh=mesh, in_specs=in_specs, out_specs=out_specs, check_vma=False)
```

profile of v0, /device:TPU:1, one launch (start us, length us, event | category | flops | bytes accessed | tf_op | source)
XLA Modules:
  0.0 395.3 jit_solution(8616252345672613163)
XLA Ops:
  7.2 1.0 fusion.76
  8.2 4.4 %collective-permute-start = (bf16[180,1,128]{2,0,1:T(8,128)(2,1)S(1)}, bf16[180,1,128]{2,0,1:T(8,128)(2,1)S(1)}, u32[]{:S(2)}, u32[]{:S(2)}) collective-permute-start(bf16[180,1,128]{2,0,1:T(8,128)(2,1)S(1)} %get-tuple-element.10), channel_id=1, source_target_pairs={{0,1},{1,2},{2,3},{3,4},{4,5},{5,6},{6,7},{7,8},{8,9},{9,10},{10,1... | collective-permute-start | bytes 138248 | tf_op jit(solution)/shard_map/ppermute | solution.py:18
  12.6 1.2 collective-permute-done
  13.7 3.8 collective-permute-done.1
  17.6 1.0 pad_maximum_fusion.5
  18.6 3.1 collective-permute-start.2
  21.7 1.3 collective-permute-start.3
  23.0 3.3 collective-permute-done.3
  26.3 1.0 maximum_bitcast_fusion
  28.3 6.8 %broadcast_select_fusion = f32[180,8,6,80]{3,1,2,0:T(8,128)} fusion(pred[8,6]{0,1:T(8,128)(4,1)S(1)} %copy-done.10, bf16[3,3,128,80]{2,3,1,0:T(8,128)(2,1)S(1)} %copy-done, bf16[182,1,7,2,128]{4,2,3,0,1:T(8,128)(2,1)S(1)} %slice.78, bf16[182,1,8,6,128]{4,2,3,0,1:T(8,128)(2,1)S(1)} %copy.17), kind=kOutput, calls=%fused_computation.28 | convolution fusion | flops 1602161664 | bytes 5837872 | tf_op jit(solution)/shard_map/conv_general_dilated | solution.py:33
  35.1 6.2 %copy.18 = f32[180,8,6,80]{0,3,2,1:T(8,128)} copy(f32[180,8,6,80]{3,1,2,0:T(8,128)} %broadcast_select_fusion) | data formatting | bytes 5529600 | tf_op jit(solution)/shard_map/conv_general_dilated | solution.py:33
  41.3 4.4 %fusion.3 = bf16[1,180,45,80]{1,3,2,0:T(8,128)(2,1)} fusion(f32[180,1,48,80]{0,3,2,1:T(8,128)} %bitcast.83, bf16[1,180,45,80]{1,3,2,0:T(8,128)(2,1)} %param.5), kind=kLoop, calls=%fused_computation.9 | loop fusion | flops 1944000 | bytes 5184000 | tf_op jit(solution)/shard_map/convert_element_type | solution.py:92
  46.1 1.7 copy.27
  47.8 4.2 %reshape_squeeze.3 = bf16[8100,128]{1,0:T(8,128)(2,1)} reshape(bf16[1,180,45,128]{3,2,1,0:T(8,128)(2,1)} %copy.27) | data formatting | bytes 4147200 | tf_op jit(solution)/shard_map/reshape;squeeze | solution.py:63
  52.0 0.6 cosine_reduce_fusion
  53.4 4.4 %maximum_maximum_fusion = (bf16[181,47,128]{2,0,1:T(8,128)(2,1)}, bf16[181,47,128]{2,0,1:T(8,128)(2,1)}) fusion(bf16[180,1,128]{2,0,1:T(8,128)(2,1)S(1)} %collective-permute-done.1, bf16[180,45,128]{2,0,1:T(8,128)(2,1)S(1)} %bitcast.80, bf16[180,1,128]{2,0,1:T(8,128)(2,1)S(1)} %collective-permute-done, bf16[1,47,128]{2,0,1:T(2,128)(2,1)S(1)} %collective-permute-done.2, ...), kind=kLoop, calls=%fused_computation.26 | loop fusion | flops 17422336 | bytes 6545408 | tf_op jit(solution)/shard_map/concatenate | solution.py:22
  57.8 26.6 %collective-permute-done.4 = bf16[180,45,80]{0,2,1:T(8,128)(2,1)} collective-permute-done((bf16[180,45,80]{0,2,1:T(8,128)(2,1)}, bf16[180,45,80]{0,2,1:T(8,128)(2,1)}, u32[]{:S(2)}, u32[]{:S(2)}) %collective-permute-start.4) | collective-permute-done | bytes 1296032 | tf_op jit(solution)/shard_map/ppermute | solution.py:29
  84.3 3.6 multiply_reduce_fusion
  87.9 0.6 add_sqrt_fusion.1
  88.6 4.8 %multiply_convert_fusion = bf16[180,45,80]{0,2,1:T(8,128)(2,1)} fusion(bf16[180,45,80]{0,2,1:T(8,128)(2,1)S(1)} %copy-done.5, bf16[180,45,80]{0,2,1:T(8,128)(2,1)} %collective-permute-done.4, f32[180,45]{0,1:T(8,128)S(1)} %get-tuple-element.18, f32[180,45]{0,1:T(8,128)S(1)} %get-tuple-element.16, f32[180]{0:T(256)S(1)} %cosine_divide_fusion, ...), kind=kLoop, calls=%fused_computation.10 | loop fusion | flops 7776000 | bytes 5249520 | tf_op jit(solution)/shard_map/convert_element_type | solution.py:105
  93.4 4.7 %copy.26 = bf16[180,45,80]{2,1,0:T(8,128)(2,1)} copy(bf16[180,45,80]{0,2,1:T(8,128)(2,1)} %multiply_convert_fusion) | data formatting | bytes 2592000 | tf_op jit(solution)/shard_map/convert_element_type | solution.py:105
  98.1 3.0 fusion.44
  101.5 0.8 fusion.47
  102.2 0.8 fusion.50
  103.0 0.8 copy-done.6
  103.9 1.3 fusion.53
  105.1 1.3 fusion.56
  106.4 1.3 fusion.59
  107.7 4.3 %reshape.50 = bf16[8100,80]{1,0:T(8,128)(2,1)} reshape(bf16[180,45,80]{2,1,0:T(8,128)(2,1)} %copy.26) | data formatting | bytes 2592000 | tf_op jit(solution)/shard_map/reshape | solution.py:56
  112.0 5.5 %collective-permute-start.5 = (bf16[180,1,80]{0,2,1:T(8,128)(2,1)S(1)}, bf16[180,1,80]{0,2,1:T(8,128)(2,1)S(1)}, u32[]{:S(2)}, u32[]{:S(2)}) collective-permute-start(bf16[180,1,80]{0,2,1:T(8,128)(2,1)S(1)} %get-tuple-element.14), channel_id=1, source_target_pairs={{0,1},{1,2},{2,3},{3,4},{4,5},{5,6},{6,7},{7,8},{8,9},{9,10},{10,1... | collective-permute-start | bytes 86408 | tf_op jit(solution)/shard_map/ppermute | solution.py:18
  117.5 2.9 convolution_bitcast_fusion
  120.4 0.8 fusion.62
  121.2 0.8 fusion.65
  122.4 0.6 copy-done.8
  123.4 1.4 fusion.77
  124.8 1.6 copy.19
  126.4 3.2 collective-permute-start.7
  130.1 1.3 collective-permute-start.8
  131.4 0.8 pad_maximum_fusion.2
  132.2 81.6 %psum.14 = f32[]{:T(128)} all-reduce(f32[]{:T(128)} %get-tuple-element.17), channel_id=1, replica_groups=mesh['member'=2,'lat'=4,'lon'=32] {'member','lat','lon'}, use_global_device_ids=true, to_apply=%region_4.0 | all-reduce | flops 1 | bytes 8 | tf_op jit(solution)/shard_map/psum | solution.py:111
  215.0 1.4 copy.22
  216.3 2.4 maximum_bitcast_fusion.1
  219.1 3.4 copy.24
  222.5 1.3 slice.84
  223.8 7.1 %select_convert_fusion = bf16[180,8,6,128]{3,1,2,0:T(8,128)(2,1)S(1)} fusion(pred[8,6]{0,1:T(8,128)(4,1)S(1)} %copy-done.11, bf16[3,3,128,80]{2,3,1,0:T(8,128)(2,1)S(1)} %copy-done, bf16[182,1,7,2,80]{4,2,3,0,1:T(8,128)(2,1)S(1)} %slice.84, bf16[182,1,8,6,80]{4,2,3,0,1:T(8,128)(2,1)} %copy.24), kind=kOutput, calls=%fused_computation.6 | convolution fusion | flops 1600327680 | bytes 4201648 | tf_op jit(solution)/shard_map/conv_general_dilated | solution.py:33
  231.6 1.5 slice_bitcast_fusion.1
  233.1 152.1 %all-reduce.2.cloned.1.call-done = f32[3,3,128,80]{2,3,1,0:T(8,128)} async-done(((f32[3,3,128,80]{2,3,1,0:T(8,128)}), f32[3,3,128,80]{2,3,1,0:T(8,128)}) %all-reduce.2.cloned.1.call-update) | async-done | bytes 368656 | tf_op jit(solution)/shard_map/psum | solution.py:111
  385.2 1.8 broadcast_multiply_fusion
  (44 shorter events, 4.4 us)
Async XLA Ops:
  7.2 21.1 %copy-start = (bf16[3,3,128,80]{2,3,1,0:T(8,128)(2,1)S(1)}, bf16[3,3,128,80]{2,3,1,0:T(8,128)(2,1)}, u32[]{:S(2)}) copy-start(bf16[3,3,128,80]{2,3,1,0:T(8,128)(2,1)} %param.7) | copy-start | bytes 552964
  7.2 19.1 %copy-start.1 = (bf16[1,180,45,128]{3,1,2,0:T(8,128)(2,1)S(1)}, bf16[1,180,45,128]{3,1,2,0:T(8,128)(2,1)}, u32[]{:S(2)}) copy-start(bf16[1,180,45,128]{3,1,2,0:T(8,128)(2,1)} %param.4) | copy-start | bytes 6220804
  7.2 378.0 %all-reduce.2.cloned.1.call-start = ((), (), s32[]{:S(2)}) async-start(), calls=%async_computation | async-start | bytes 737280 | tf_op jit(solution)/shard_map/psum | solution.py:111
  8.2 5.5 %collective-permute-start = (bf16[180,1,128]{2,0,1:T(8,128)(2,1)S(1)}, bf16[180,1,128]{2,0,1:T(8,128)(2,1)S(1)}, u32[]{:S(2)}, u32[]{:S(2)}) collective-permute-start(bf16[180,1,128]{2,0,1:T(8,128)(2,1)S(1)} %get-tuple-element.10), channel_id=1, source_target_pairs={{0,1},{1,2},{2,3},{3,4},{4,5},{5,6},{6,7},{7,8},{8,9},{9,10},{10,1... | collective-permute-start | bytes 138248 | tf_op jit(solution)/shard_map/ppermute | solution.py:18
  12.6 5.0 %collective-permute-start.1 = (bf16[180,1,128]{2,0,1:T(8,128)(2,1)S(1)}, bf16[180,1,128]{2,0,1:T(8,128)(2,1)S(1)}, u32[]{:S(2)}, u32[]{:S(2)}) collective-permute-start(bf16[180,1,128]{2,0,1:T(8,128)(2,1)S(1)} %get-tuple-element.11), channel_id=1, source_target_pairs={{1,0},{2,1},{3,2},{4,3},{5,4},{6,5},{7,6},{8,7},{9,8},{10,9},{11,1... | collective-permute-start | bytes 138248 | tf_op jit(solution)/shard_map/ppermute | solution.py:21
  18.6 4.4 %collective-permute-start.2 = (bf16[1,47,128]{2,0,1:T(2,128)(2,1)S(1)}, bf16[1,47,128]{2,0,1:T(2,128)(2,1)S(1)}, u32[]{:S(2)}, u32[]{:S(2)}) collective-permute-start(bf16[1,47,128]{2,0,1:T(2,128)(2,1)S(1)} %get-tuple-element.8), channel_id=1, source_target_pairs={{0,32},{32,64},{64,96},{1,33},{33,65},{65,97},{2,34},{34,66},{66,9... | collective-permute-start | bytes 36104 | tf_op jit(solution)/shard_map/ppermute | solution.py:18
  21.7 4.6 %collective-permute-start.3 = (bf16[1,47,128]{2,0,1:T(2,128)(2,1)S(1)}, bf16[1,47,128]{2,0,1:T(2,128)(2,1)S(1)}, u32[]{:S(2)}, u32[]{:S(2)}) collective-permute-start(bf16[1,47,128]{2,0,1:T(2,128)(2,1)S(1)} %get-tuple-element.9), channel_id=1, source_target_pairs={{32,0},{64,32},{96,64},{33,1},{65,33},{97,65},{34,2},{66,34},{98,6... | collective-permute-start | bytes 36104 | tf_op jit(solution)/shard_map/ppermute | solution.py:21
  27.5 0.8 copy-start.10
  45.7 38.6 %collective-permute-start.4 = (bf16[180,45,80]{0,2,1:T(8,128)(2,1)}, bf16[180,45,80]{0,2,1:T(8,128)(2,1)}, u32[]{:S(2)}, u32[]{:S(2)}) collective-permute-start(bf16[180,45,80]{0,2,1:T(8,128)(2,1)} %bitcast.6), channel_id=1, source_target_pairs={{0,128},{128,0},{1,129},{129,1},{2,130},{130,2},{3,131},{131,3},{4... | collective-permute-start | bytes 3888008 | tf_op jit(solution)/shard_map/ppermute | solution.py:29
  53.4 31.0 %copy-start.5 = (bf16[180,45,80]{0,2,1:T(8,128)(2,1)S(1)}, bf16[180,45,80]{0,2,1:T(8,128)(2,1)}, u32[]{:S(2)}) copy-start(bf16[180,45,80]{0,2,1:T(8,128)(2,1)} %param.6) | copy-start | bytes 3888004
  98.1 3.0 copy-start.2
  98.1 3.4 copy-start.7
  102.2 1.6 copy-start.6
  112.0 8.4 %copy-start.3 = (bf16[180,45,80]{0,2,1:T(8,128)(2,1)S(1)}, bf16[180,45,80]{0,2,1:T(8,128)(2,1)}, u32[]{:S(2)}) copy-start(bf16[180,45,80]{0,2,1:T(8,128)(2,1)} %multiply_convert_fusion) | copy-start | bytes 3888004
  112.0 10.1 %collective-permute-start.5 = (bf16[180,1,80]{0,2,1:T(8,128)(2,1)S(1)}, bf16[180,1,80]{0,2,1:T(8,128)(2,1)S(1)}, u32[]{:S(2)}, u32[]{:S(2)}) collective-permute-start(bf16[180,1,80]{0,2,1:T(8,128)(2,1)S(1)} %get-tuple-element.14), channel_id=1, source_target_pairs={{0,1},{1,2},{2,3},{3,4},{4,5},{5,6},{6,7},{7,8},{8,9},{9,10},{10,1... | collective-permute-start | bytes 86408 | tf_op jit(solution)/shard_map/ppermute | solution.py:18
  117.5 4.9 %collective-permute-start.6 = (bf16[180,1,80]{0,2,1:T(8,128)(2,1)S(1)}, bf16[180,1,80]{0,2,1:T(8,128)(2,1)S(1)}, u32[]{:S(2)}, u32[]{:S(2)}) collective-permute-start(bf16[180,1,80]{0,2,1:T(8,128)(2,1)S(1)} %get-tuple-element.15), channel_id=1, source_target_pairs={{1,0},{2,1},{3,2},{4,3},{5,4},{6,5},{7,6},{8,7},{9,8},{10,9},{11,1... | collective-permute-start | bytes 86408 | tf_op jit(solution)/shard_map/ppermute | solution.py:21
  122.4 0.6 copy-start.8
  126.4 90.0 %copy-start.4 = (bf16[180,45,80]{0,2,1:T(8,128)(2,1)S(1)}, bf16[180,45,80]{0,2,1:T(8,128)(2,1)}, u32[]{:S(2)}) copy-start(bf16[180,45,80]{0,2,1:T(8,128)(2,1)} %multiply_convert_fusion) | copy-start | bytes 3888004
  126.4 90.0 %copy-start.9 = (bf16[180,1,80]{0,2,1:T(8,128)(2,1)S(1)}, bf16[180,1,80]{0,2,1:T(8,128)(2,1)}, u32[]{:S(2)}) copy-start(bf16[180,1,80]{0,2,1:T(8,128)(2,1)} %copy-done.8) | copy-start | bytes 86404
  126.4 88.1 %collective-permute-start.7 = (bf16[1,47,80]{2,1,0:T(8,128)(2,1)S(1)}, bf16[1,47,80]{2,1,0:T(8,128)(2,1)S(1)}, u32[]{:S(2)}, u32[]{:S(2)}) collective-permute-start(bf16[1,47,80]{2,1,0:T(8,128)(2,1)S(1)} %copy.19), channel_id=1, source_target_pairs={{0,32},{32,64},{64,96},{1,33},{33,65},{65,97},{2,34},{34,66},{66,9... | collective-permute-start | bytes 22568 | tf_op jit(solution)/shard_map/ppermute | solution.py:18
  130.1 84.9 %collective-permute-start.8 = (bf16[1,47,80]{2,1,0:T(8,128)(2,1)S(1)}, bf16[1,47,80]{2,1,0:T(8,128)(2,1)S(1)}, u32[]{:S(2)}, u32[]{:S(2)}) collective-permute-start(bf16[1,47,80]{2,1,0:T(8,128)(2,1)S(1)} %copy.20), channel_id=1, source_target_pairs={{32,0},{64,32},{96,64},{33,1},{65,33},{97,65},{34,2},{66,34},{98,6... | collective-permute-start | bytes 22568 | tf_op jit(solution)/shard_map/ppermute | solution.py:21
  219.1 4.7 %copy-start.11 = (pred[8,6]{0,1:T(8,128)(4,1)S(1)}, pred[8,6]{0,1:T(8,128)(4,1)}, u32[]{:S(2)}) copy-start(pred[8,6]{0,1:T(8,128)(4,1)} %constant.45) | copy-start | bytes 148
Sparse Core Ops, SparseCore 0:
  132.3 252.8 all-reduce.1
where the time goes:
time: 403 us; the launch traced here: 395 us
  waiting for transfers between devices  187 us (46%)
  blocking collectives  81.6 us (20%)
  local copies, waits for them, and re-layouts  37.2 us (9%)
  matrix products  26.9 us (7%)
  other arithmetic  25.9 us (6%)
  starting transfers between devices  19.2 us (5%)
  between operations  17.1 us (4%)
    psum x1, waiting for transfers between devices, local(): lax.psum((partial_grad, local_total), ('member', 'lat', 'lon'))  152 us
    psum x1, blocking collectives, local(): lax.psum((partial_grad, local_total), ('member', 'lat', 'lon'))  81.6 us
    ppermute x1, waiting for transfers between devices, partner(): return lax.ppermute(value, axis, pairs)  26.6 us
    ppermute x4, starting transfers between devices, padded(): lax.ppermute(lax.slice_in_dim(block, block.shape[dim] - width, None, axis...  16.2 us
    conv_general_dilated x2, matrix products, stencil_filter_step(): lax.conv_general_dilated(haloed_grid_array[None], weights_hwio, (1, 1), '...  14 us
    dot_general x9, matrix products, tap_products(): lax.dot_general(window, flat_grad, (((0,), (0,)), ((), ())), preferred_el...  12.9 us
    conv_general_dilated x5, local copies, waits for them, and re-layouts, stencil_filter_step(): lax.conv_general_dilated(haloed_grid_array[None], weights_hwio, (1, 1), '...  11.6 us
  transfers between devices with their start and end apart: 10, of which 6 were waited for; matrix products, arithmetic and copies ran while one was open for 9% of the time, Pallas kernels for 0%

commit v1 on v0

v1 whole, which is shorter than its diff:
```python
import functools
import math

import jax
import jax.numpy as jnp
from jax import lax
from jax.experimental import pallas as pl
from jax.experimental.pallas import tpu as pltpu
from jax.sharding import PartitionSpec as P

epsilon = 1e-06
RING = 256
LANES = 128
AXES = ("member", "lat", "lon")
VMEM = pl.BlockSpec(memory_space=pltpu.VMEM)
ANY = pl.BlockSpec(memory_space=pl.ANY)


def latitude_weights(row_index, total_rows):
    scale = math.pi / total_rows
    angles = 0.5 * math.pi - (row_index.astype(jnp.float32) + 0.5) * scale
    every_row = (
        0.5 * math.pi - (jnp.arange(total_rows, dtype=jnp.int32).astype(jnp.float32) + 0.5) * scale
    )
    return jnp.cos(angles) / jnp.mean(jnp.cos(every_row))


def neighbour(value, north, east):
    bands, sectors = lax.axis_size("lat"), lax.axis_size("lon")
    pairs = []
    for band in range(bands):
        for sector in range(sectors):
            to = band + north
            if 0 <= to < bands:
                pairs.append((band * sectors + sector, to * sectors + (sector + east) % sectors))
    return lax.ppermute(value, ("lat", "lon"), pairs)


def extend(columns):
    count, rows, channels = columns.shape
    first, last = columns[:, :1], columns[:, rows - 1 :]
    west = neighbour(columns[count - 1 :], 0, 1)
    east = neighbour(columns[:1], 0, -1)
    above = neighbour(last, 1, 0)
    below = neighbour(first, -1, 0)
    above_west = neighbour(last[count - 1 :], 1, 1)
    above_east = neighbour(last[:1], 1, -1)
    below_west = neighbour(first[count - 1 :], -1, 1)
    below_east = neighbour(first[:1], -1, -1)
    wide = jnp.concatenate([west, columns, east], axis=0)
    top = jnp.concatenate([above_west, above, above_east], axis=0)
    bottom = jnp.concatenate([below_west, below, below_east], axis=0)
    gap = jnp.zeros((count + 2, RING - rows - 2, channels), columns.dtype)
    return jnp.concatenate([wide, bottom, gap, top], axis=1)


def window(slab_ref, column):
    return jnp.concatenate([slab_ref[column + b] for b in range(3)], axis=1)


def forward_kernel(start, count, *refs):
    if start:
        slab_ref, present_ref, weights_ref, _, pred_out, packed_out, pred_v, sem = refs
    else:
        slab_ref, present_ref, weights_ref, pred_out, packed_out, pred_v, sem = refs
    outputs, rows = present_ref.shape[1:]

    def one(j):
        y = lax.dot_general(
            weights_ref[...],
            window(slab_ref, start + j),
            (((1,), (1,)), ((), ())),
            preferred_element_type=jnp.float32,
        )
        increment = (
            pltpu.roll(y[:outputs], 1, 1)
            + y[outputs : 2 * outputs]
            + pltpu.roll(y[2 * outputs :], RING - 1, 1)
        )
        head = increment[:, :LANES] + present_ref[start + j, :, :LANES].astype(jnp.float32)
        tail = increment[:, LANES:rows] + present_ref[start + j, :, LANES:].astype(jnp.float32)
        head = head.astype(jnp.bfloat16)
        tail = tail.astype(jnp.bfloat16)
        pred_v[j, :, :LANES] = head
        pred_v[j, :, LANES:] = tail
        packed_out[j] = head
        return tail

    half = LANES // 2

    def pair(t, carry):
        low = one(2 * t)
        high = one(2 * t + 1)
        packed_out[count + t, :, : rows - LANES] = low
        packed_out[count + t, :, half : half + rows - LANES] = high
        return carry

    lax.fori_loop(0, count // 2, pair, 0)
    if count % 2:
        packed_out[count + count // 2, :, : rows - LANES] = one(count - 1)
    copy = pltpu.make_async_copy(pred_v, pred_out.at[pl.ds(start, count)], sem)
    copy.start()
    copy.wait()


def forward(start, count, slab, present, weights, pred):
    columns, outputs, rows = present.shape
    inputs = slab.shape[2]
    given = [slab, present, weights] + ([pred] if start else [])
    return pl.pallas_call(
        functools.partial(forward_kernel, start, count),
        out_shape=(
            jax.ShapeDtypeStruct((columns, outputs, rows), jnp.bfloat16),
            jax.ShapeDtypeStruct((count + (count + 1) // 2, outputs, LANES), jnp.bfloat16),
        ),
        in_specs=[VMEM] * 3 + ([ANY] if start else []),
        out_specs=(ANY, VMEM),
        scratch_shapes=[
            pltpu.VMEM((count, outputs, rows), jnp.bfloat16),
            pltpu.SemaphoreType.DMA,
        ],
        input_output_aliases={3: 0} if start else {},
        compiler_params=pltpu.CompilerParams(vmem_limit_bytes=24 << 20),
        cost_estimate=pl.CostEstimate(
            flops=2 * count * 9 * inputs * outputs * RING,
            bytes_accessed=count * RING * (inputs + 3 * outputs) * 2,
            transcendentals=0,
        ),
        name="forward",
    )(*given)


def score_kernel(start, count, last, *refs):
    if start:
        slab_ref, own_ref, other_ref, target_ref, weight_ref, sums_ref, turned_out, sums_out = refs[:8]
    else:
        slab_ref, own_ref, other_ref, target_ref, weight_ref, turned_out, sums_out = refs[:7]
    cot_v, acc_v = refs[-2:]
    outputs, rows = target_ref.shape[1:]
    cut = LANES // 2
    weight = weight_ref[...]
    cot_v[...] = jnp.zeros_like(cot_v)
    acc_v[...] = jnp.zeros_like(acc_v)

    def one(j, tail_block, shift, score):
        parts = []
        for ref in (own_ref, other_ref):
            head = ref[j].astype(jnp.float32)
            tail = ref[tail_block, :, shift : shift + rows - LANES].astype(jnp.float32)
            parts.append((head, tail))
        halves = []
        for side in range(2):
            lanes = slice(0, LANES) if side == 0 else slice(LANES, rows)
            value = parts[0][side]
            truth = target_ref[start + j, :, lanes].astype(jnp.float32)
            misfit = value - truth
            spread = value - parts[1][side]
            error2 = jnp.sum(misfit * misfit, axis=0, keepdims=True) + epsilon
            pair2 = jnp.sum(spread * spread, axis=0, keepdims=True) + epsilon
            error_inv = lax.rsqrt(error2)
            pair_inv = lax.rsqrt(pair2)
            scale = 0.5 * weight[:, lanes]
            cot_v[shift // cut, :outputs, lanes] = misfit * (scale * error_inv) - spread * (
                scale * pair_inv
            )
            halves.append(scale * (error2 * error_inv - 0.5 * (pair2 * pair_inv)))
        cot = cot_v[shift // cut]
        turned_out[j] = cot.T[:rows].astype(jnp.bfloat16)
        cot = cot[:outputs]
        shifted = jnp.concatenate([pltpu.roll(cot, RING - 1, 1), cot, pltpu.roll(cot, 1, 1)], axis=0)
        acc_v[...] += jnp.dot(
            shifted.astype(jnp.bfloat16),
            window(slab_ref, start + j),
            preferred_element_type=jnp.float32,
        )
        return tuple(s + h for s, h in zip(score, halves))

    def pair(t, score):
        score = one(2 * t, count + t, 0, score)
        return one(2 * t + 1, count + t, cut, score)

    score = (jnp.zeros((1, LANES), jnp.float32), jnp.zeros((1, rows - LANES), jnp.float32))
    score = lax.fori_loop(0, count // 2, pair, score)
    if count % 2:
        score = one(count - 1, count + count // 2, 0, score)
    inputs = slab_ref.shape[2]
    for a in range(3):
        for b in range(3):
            block = acc_v[a * outputs : (a + 1) * outputs, b * inputs : (b + 1) * inputs]
            place = slice((3 * a + b) * outputs, (3 * a + b + 1) * outputs)
            sums_out[place] = block + sums_ref[place] if start else block
    spare = slice(9 * outputs, sums_out.shape[0])
    total = jnp.sum(score[0], axis=1, keepdims=True) + jnp.sum(score[1], axis=1, keepdims=True)
    filler = jnp.broadcast_to(total, (sums_out.shape[0] - 9 * outputs, inputs))
    sums_out[spare] = filler + sums_ref[spare] if start else filler


def scored(start, count, last, slab, own, other, target, weight, sums, sum_rows):
    _, outputs, rows = target.shape
    inputs = slab.shape[2]
    given = [slab, own, other, target, weight] + ([sums] if start else [])
    return pl.pallas_call(
        functools.partial(score_kernel, start, count, last),
        out_shape=(
            jax.ShapeDtypeStruct((count, rows, LANES), jnp.bfloat16),
            jax.ShapeDtypeStruct((sum_rows, inputs), jnp.float32),
        ),
        in_specs=[VMEM] * len(given),
        out_specs=(VMEM, VMEM),
        scratch_shapes=[
            pltpu.VMEM((2, LANES, RING), jnp.float32),
            pltpu.VMEM((3 * outputs, 3 * inputs), jnp.float32),
        ],
        compiler_params=pltpu.CompilerParams(vmem_limit_bytes=24 << 20),
        cost_estimate=pl.CostEstimate(
            flops=2 * count * 9 * inputs * outputs * RING,
            bytes_accessed=count * RING * (inputs + 3 * outputs) * 2,
            transcendentals=2 * count * rows,
        ),
        name="score",
    )(*given)


def backward_kernel(block, slab_ref, weights_ref, slope_out):
    rows, inputs = slope_out.shape[1:]
    base = pl.program_id(0) * block
    for j in range(block):
        z = jnp.dot(
            window(slab_ref, base + j), weights_ref[...], preferred_element_type=jnp.float32
        )
        slope = (
            pltpu.roll(z[:, :inputs], 1, 0)
            + z[:, inputs : 2 * inputs]
            + pltpu.roll(z[:, 2 * inputs :], RING - 1, 0)
        )
        slope_out[j] = slope[:rows].astype(jnp.bfloat16)


def backward(slab, weights, rows):
    columns = slab.shape[0] - 2
    inputs = weights.shape[1] // 3
    block = max(n for n in range(1, 6) if columns % n == 0)
    return pl.pallas_call(
        functools.partial(backward_kernel, block),
        grid=(columns // block,),
        out_shape=jax.ShapeDtypeStruct((columns, rows, inputs), jnp.bfloat16),
        in_specs=[VMEM, VMEM],
        out_specs=pl.BlockSpec((block, rows, inputs), lambda i: (i, 0, 0)),
        compiler_params=pltpu.CompilerParams(vmem_limit_bytes=24 << 20),
        cost_estimate=pl.CostEstimate(
            flops=2 * columns * 9 * inputs * LANES * RING,
            bytes_accessed=columns * RING * (inputs + LANES) * 2,
            transcendentals=0,
        ),
        name="backward",
    )(slab, weights)


def exchange(blocks):
    return lax.all_to_all(blocks, AXES, 0, 0, tiled=True)


def split(columns):
    weights = (10, 12, 14, 9)
    edges = [0]
    for i in range(len(weights)):
        edges.append(2 * round(columns * sum(weights[: i + 1]) / sum(weights) / 2))
    edges[-1] = columns
    return [(low, high - low) for low, high in zip(edges, edges[1:]) if high > low]


def local(features, present_condition, target, filter_weights_tensor):
    lat_rows, lon_cols, inputs = features.shape[1:]
    outputs = target.shape[2]
    total_rows = lat_rows * lax.axis_size("lat")
    total_cols = lon_cols * lax.axis_size("lon")
    devices = math.prod(lax.axis_size(axis) for axis in AXES)

    taps = jnp.transpose(filter_weights_tensor, (0, 1, 3, 2))
    forward_weights = jnp.transpose(taps, (0, 2, 1, 3)).reshape(3 * outputs, 3 * inputs)
    flipped = jnp.pad(taps[::-1, ::-1], ((0, 0), (0, 0), (0, LANES - outputs), (0, 0)))
    backward_weights = jnp.transpose(flipped, (1, 2, 0, 3)).reshape(3 * LANES, 3 * inputs)
    row_index = lax.axis_index("lat") * lat_rows + jnp.arange(lat_rows, dtype=jnp.int32)
    weight = latitude_weights(row_index, total_rows)[None]

    slab = extend(jnp.transpose(features[0], (1, 0, 2)))
    present = jnp.transpose(present_condition[0], (1, 2, 0))
    truth = jnp.transpose(target, (1, 2, 0))

    chunks = split(lon_cols)
    pred = None
    packed = []
    for start, count in chunks:
        pred, own = forward(start, count, slab, present, forward_weights, pred)
        packed.append((own, lax.ppermute(own, "member", [(0, 1), (1, 0)])))

    width = -(-(9 * outputs * inputs + 1) // (devices * LANES)) * LANES
    sum_rows = devices * width // inputs
    sums = None
    turned = []
    for (start, count), (own, other) in zip(chunks, packed):
        last = start + count == lon_cols
        piece, sums = scored(start, count, last, slab, own, other, truth, weight, sums, sum_rows)
        turned.append(piece)
    share = jnp.sum(exchange(sums.reshape(devices, width)), axis=0, keepdims=True)
    whole = exchange(jnp.broadcast_to(share, (devices, width))).reshape(sum_rows, inputs)

    slope = backward(extend(jnp.concatenate(turned, axis=0)), backward_weights, lat_rows)
    objective_mean = whole[9 * outputs, 0] / (total_rows * total_cols)
    summed = whole[: 9 * outputs] / math.sqrt(2.0 * total_rows * total_cols)
    filter_weights_slope = jnp.transpose(summed.reshape(3, 3, outputs, inputs), (0, 1, 3, 2))
    return (
        jnp.transpose(pred, (2, 0, 1))[None],
        objective_mean,
        jnp.transpose(slope, (1, 0, 2))[None],
        filter_weights_slope,
    )


def solution(mesh):
    in_specs = (
        P("member", "lat", "lon", None),
        P("member", "lat", "lon", None),
        P("lat", "lon", None),
        P(),
    )
    out_specs = (P("member", "lat", "lon", None), P(), P("member", "lat", "lon", None), P())
    return jax.shard_map(local, mesh=mesh, in_specs=in_specs, out_specs=out_specs, check_vma=False)
```

time: 403 us -> 175 us (0.43); the launches traced: 395 us -> 174 us
  waiting for transfers between devices: 187 us -> 15.7 us
  blocking collectives: 81.6 us -> 0 us
  starting transfers between devices: 19.2 us -> 77.5 us
  Pallas kernels: 0 us -> 36.8 us
  matrix products: 26.9 us -> 0 us
  local copies, waits for them, and re-layouts: 37.2 us -> 21.5 us
  between operations: 17.1 us -> 3.46 us
  other arithmetic: 25.9 us -> 19.3 us
    psum x1 -> x0, waiting for transfers between devices: 152 us -> none  [local(): lax.psum((partial_grad, local_total), ('member', 'lat', 'lon'))]
    psum x1 -> x0, blocking collectives: 81.6 us -> none  [local(): lax.psum((partial_grad, local_total), ('member', 'lat', 'lon'))]
    ppermute x9 -> x20, starting transfers between devices: 19.2 us -> 58.6 us  [the longest x16 55.3 us: neighbour(): return lax.ppermute(value, ('lat', 'lon'), pairs)]
    pallas_call x0 -> x9, Pallas kernels: none -> 36.8 us  [the longest x4 15.1 us: scored(): pl.pallas_call(functools.partial(score_kernel, start, count, last), out_s...]
    ppermute x9 -> x20, waiting for transfers between devices: 35.1 us -> 14.2 us  [the longest x16 14.2 us: neighbour(): return lax.ppermute(value, ('lat', 'lon'), pairs)]
    all_to_all x0 -> x2, starting transfers between devices: none -> 18.9 us  [exchange(): return lax.all_to_all(blocks, AXES, 0, 0, tiled=True)]
    conv_general_dilated x2 -> x0, matrix products: 14 us -> none  [stencil_filter_step(): lax.conv_general_dilated(haloed_grid_array[None], weights_hwio, (1, 1), '...]
    dot_general x9 -> x0, matrix products: 12.9 us -> none  [tap_products(): lax.dot_general(window, flat_grad, (((0,), (0,)), ((), ())), preferred_el...]
  transfers between devices with their start and end apart: 10 -> 22, of which waited for: 6 -> 4; matrix products, arithmetic and copies ran while one was open for 9% -> 14% of each run, Pallas kernels for 0% -> 19%
where the time goes in v1:
time: 175 us; the launch traced here: 174 us
  starting transfers between devices  77.5 us (44%)
  Pallas kernels  36.8 us (21%)
  local copies, waits for them, and re-layouts  21.5 us (12%)
  other arithmetic  19.3 us (11%)
  waiting for transfers between devices  15.7 us (9%)
  between operations  3.46 us (2%)
    ppermute x16, starting transfers between devices, neighbour(): return lax.ppermute(value, ('lat', 'lon'), pairs)  55.3 us
    all_to_all x2, starting transfers between devices, exchange(): return lax.all_to_all(blocks, AXES, 0, 0, tiled=True)  18.9 us
    concatenate x2, other arithmetic, extend(): return jnp.concatenate([wide, bottom, gap, top], axis=1)  17.2 us
    pallas_call x4, Pallas kernels, scored(): pl.pallas_call(functools.partial(score_kernel, start, count, last), out_s...  15.1 us
    pallas_call x4, Pallas kernels, forward(): pl.pallas_call(functools.partial(forward_kernel, start, count), out_shape...  14.2 us
    ppermute x16, waiting for transfers between devices, neighbour(): return lax.ppermute(value, ('lat', 'lon'), pairs)  14.2 us
    unnamed x35, local copies, waits for them, and re-layouts  10.7 us
    pallas_call x1, Pallas kernels, backward(): pl.pallas_call(functools.partial(backward_kernel, block), grid=(columns /...  7.53 us
  transfers between devices with their start and end apart: 22, of which 4 were waited for; matrix products, arithmetic and copies ran while one was open for 14% of the time, Pallas kernels for 19%

profile of v1, /device:TPU:1, one launch (start us, length us, event | category | flops | bytes accessed | tf_op | source)
XLA Modules:
  0.0 174.3 jit_solution(16336070663428490050)
XLA Ops:
  0.6 1.0 fusion.3
  1.6 1.3 collective-permute-start.3
  2.9 4.6 %collective-permute-start.6 = (bf16[45,1,128]{2,1,0:T(2,128)(2,1)S(1)}, bf16[45,1,128]{2,1,0:T(2,128)(2,1)S(1)}, u32[]{:S(2)}, u32[]{:S(2)}) collective-permute-start(bf16[45,1,128]{2,1,0:T(2,128)(2,1)S(1)} %get-tuple-element.45), channel_id=1, source_target_pairs={{0,32},{1,33},{2,34},{3,35},{4,36},{5,37},{6,38},{7,39},{8,40},{9,... | collective-permute-start | bytes 34568 | tf_op jit(solution)/shard_map/ppermute | solution.py:36
  7.5 0.8 fusion.1
  8.3 4.3 %collective-permute-start = (bf16[1,180,128]{2,1,0:T(8,128)(2,1)S(1)}, bf16[1,180,128]{2,1,0:T(8,128)(2,1)S(1)}, u32[]{:S(2)}, u32[]{:S(2)}) collective-permute-start(bf16[1,180,128]{2,1,0:T(8,128)(2,1)S(1)} %get-tuple-element.38), channel_id=1, source_target_pairs={{0,1},{1,2},{2,3},{3,4},{4,5},{5,6},{6,7},{7,8},{8,9},{9,10},{10,1... | collective-permute-start | bytes 138248 | tf_op jit(solution)/shard_map/ppermute | solution.py:36
  13.4 1.3 collective-permute-start.2
  14.7 7.6 %collective-permute-done.2 = bf16[1,1,128]{2,1,0:T(2,128)(2,1)S(1)} collective-permute-done((bf16[1,1,128]{2,1,0:T(2,128)(2,1)S(1)}, bf16[1,1,128]{2,1,0:T(2,128)(2,1)S(1)}, u32[]{:S(2)}, u32[]{:S(2)}) %collective-permute-start.2) | collective-permute-done | bytes 288 | tf_op jit(solution)/shard_map/ppermute | solution.py:36
  22.3 8.1 %collective-permute-start.7 = (bf16[1,1,128]{2,1,0:T(2,128)(2,1)S(1)}, bf16[1,1,128]{2,1,0:T(2,128)(2,1)S(1)}, u32[]{:S(2)}, u32[]{:S(2)}) collective-permute-start(bf16[1,1,128]{2,1,0:T(2,128)(2,1)S(1)} %get-tuple-element.41), channel_id=1, source_target_pairs={{0,63},{1,32},{2,33},{3,34},{4,35},{5,36},{6,37},{7,38},{8,39},{9,... | collective-permute-start | bytes 776 | tf_op jit(solution)/shard_map/ppermute | solution.py:36
  31.1 1.3 collective-permute-start.5
  32.4 0.9 rev.3
  33.4 1.2 copy.15
  34.5 1.3 collective-permute-start.4
  36.0 5.8 %collective-permute-done.4 = bf16[1,1,128]{2,1,0:T(2,128)(2,1)S(1)} collective-permute-done((bf16[1,1,128]{2,1,0:T(2,128)(2,1)S(1)}, bf16[1,1,128]{2,1,0:T(2,128)(2,1)S(1)}, u32[]{:S(2)}, u32[]{:S(2)}) %collective-permute-start.4) | collective-permute-done | bytes 288 | tf_op jit(solution)/shard_map/ppermute | solution.py:36
  42.4 9.0 %maximum_maximum_fusion.refs_0_ = bf16[47,256,128]{2,1,0:T(8,128)(2,1)S(1)} fusion(bf16[1,1,128]{2,1,0:T(2,128)(2,1)} %copy-done.12, bf16[45,1,128]{2,1,0:T(2,128)(2,1)} %copy-done.11, bf16[1,1,128]{2,1,0:T(2,128)(2,1)} %copy-done.13, bf16[1,1,128]{2,1,0:T(2,128)(2,1)S(1)} %collective-permute-done.4, bf16[45,1,128]{2,1,0:T(2,128)(2,1)} %copy-done.10, ...), kind=kLoop, calls=%fused_computation | loop fusion | flops 30801920 | bytes 5270528 | tf_op jit(solution)/shard_map/concatenate | solution.py:54
  51.5 3.8 %forward.4 = (bf16[45,80,180]{2,1,0:T(8,128)(2,1)}, bf16[15,80,128]{2,1,0:T(8,128)(2,1)}) custom-call(bf16[47,256,128]{2,1,0:T(8,128)(2,1)S(1)} %maximum_maximum_fusion.refs_0_, bf16[45,80,180]{2,1,0:T(8,128)(2,1)S(1)} %bitcast.33, bf16[240,384]{1,0:T(8,128)(2,1)S(1)} %bitcast.41), custom_call_target="tpu_custom_call" | custom-call | flops 471859200 | bytes 1884160 | tf_op jit(solution)/shard_map/forward/pallas_call | solution.py:110
  56.5 1.2 copy.17
  57.7 0.8 copy.22
  59.8 1.5 copy-done.1
  61.3 3.5 %forward.5 = (bf16[45,80,180]{2,1,0:T(8,128)(2,1)}, bf16[18,80,128]{2,1,0:T(8,128)(2,1)S(1)}) custom-call(bf16[47,256,128]{2,1,0:T(8,128)(2,1)S(1)} %maximum_maximum_fusion.refs_0_, bf16[45,80,180]{2,1,0:T(8,128)(2,1)S(1)} %bitcast.34, bf16[240,384]{1,0:T(8,128)(2,1)S(1)} %bitcast.42, ...), custom_call_target="tpu_custom_call", output_to_operand_aliasing={{0}: (3, {})} | custom-call | flops 566231040 | bytes 2260992 | tf_op jit(solution)/shard_map/forward/pallas_call | solution.py:110
  64.8 1.2 collective-permute-start.10
  66.0 4.0 %forward.6 = (bf16[45,80,180]{2,1,0:T(8,128)(2,1)}, bf16[21,80,128]{2,1,0:T(8,128)(2,1)S(1)}) custom-call(bf16[47,256,128]{2,1,0:T(8,128)(2,1)S(1)} %maximum_maximum_fusion.refs_0_, bf16[45,80,180]{2,1,0:T(8,128)(2,1)S(1)} %bitcast.35, bf16[240,384]{1,0:T(8,128)(2,1)S(1)} %bitcast.43, ...), custom_call_target="tpu_custom_call", output_to_operand_aliasing={{0}: (3, {})} | custom-call | flops 660602880 | bytes 2637824 | tf_op jit(solution)/shard_map/forward/pallas_call | solution.py:110
  70.6 2.9 %forward.7 = (bf16[45,80,180]{2,1,0:T(8,128)(2,1)}, bf16[14,80,128]{2,1,0:T(8,128)(2,1)S(1)}) custom-call(bf16[47,256,128]{2,1,0:T(8,128)(2,1)S(1)} %maximum_maximum_fusion.refs_0_, bf16[45,80,180]{2,1,0:T(8,128)(2,1)S(1)} %bitcast.36, bf16[240,384]{1,0:T(8,128)(2,1)S(1)} %bitcast.44, ...), custom_call_target="tpu_custom_call", output_to_operand_aliasing={{0}: (3, {})} | custom-call | flops 424673280 | bytes 1695744 | tf_op jit(solution)/shard_map/forward/pallas_call | solution.py:110
  73.4 1.2 collective-permute-start.8
  74.6 4.2 %score.4 = (bf16[10,180,128]{2,1,0:T(8,128)(2,1)S(1)}, f32[768,128]{1,0:T(8,128)S(1)}) custom-call(bf16[47,256,128]{2,1,0:T(8,128)(2,1)S(1)} %maximum_maximum_fusion.refs_0_, bf16[15,80,128]{2,1,0:T(8,128)(2,1)} %get-tuple-element.27.refs_1_, bf16[15,80,128]{2,1,0:T(8,128)(2,1)} %collective-permute-done.11.refs_2_, bf16[45,80,180]{2,1,0:T(8,128)(2,1)S(1)} %bitcast.37, ...), custom_call_target="tpu_custom_call" | custom-call | flops 471859200 | bytes 1884160 | tf_op jit(solution)/shard_map/score/pallas_call | solution.py:202
  80.0 1.3 collective-permute-start.16
  81.3 14.3 %collective-permute-start.19 = (bf16[1,1,128]{2,1,0:T(2,128)(2,1)}, bf16[1,1,128]{2,1,0:T(2,128)(2,1)}, u32[]{:S(2)}, u32[]{:S(2)}) collective-permute-start(bf16[1,1,128]{2,1,0:T(2,128)(2,1)} %get-tuple-element.53), channel_id=1, source_target_pairs={{0,63},{1,32},{2,33},{3,34},{4,35},{5,36},{6,37},{7,38},{8,39},{9,... | collective-permute-start | bytes 776 | tf_op jit(solution)/shard_map/ppermute | solution.py:36
  95.5 3.8 %score.5 = (bf16[12,180,128]{2,1,0:T(8,128)(2,1)S(1)}, f32[768,128]{1,0:T(8,128)S(1)}) custom-call(bf16[47,256,128]{2,1,0:T(8,128)(2,1)S(1)} %maximum_maximum_fusion.refs_0_, bf16[18,80,128]{2,1,0:T(8,128)(2,1)S(1)} %get-tuple-element.26.refs_1_, bf16[18,80,128]{2,1,0:T(8,128)(2,1)S(1)} %collective-permute-done.10.refs_2_, ...), custom_call_target="tpu_custom_call" | custom-call | flops 566231040 | bytes 2260992 | tf_op jit(solution)/shard_map/score/pallas_call | solution.py:202
  99.3 0.8 copy-done.5
  100.1 4.4 %score.6 = (bf16[14,180,128]{2,1,0:T(8,128)(2,1)S(1)}, f32[768,128]{1,0:T(8,128)S(1)}) custom-call(bf16[47,256,128]{2,1,0:T(8,128)(2,1)S(1)} %maximum_maximum_fusion.refs_0_, bf16[21,80,128]{2,1,0:T(8,128)(2,1)S(1)} %get-tuple-element.25.refs_1_, bf16[21,80,128]{2,1,0:T(8,128)(2,1)S(1)} %collective-permute-done.9.refs_2_, bf16[45,80,180]{2,1,0:T(8,128)(2,1)S(1)} %bitcast.39, ...), custom_call_target="tpu_custom_call" | custom-call | flops 660602880 | bytes 2637824 | tf_op jit(solution)/shard_map/score/pallas_call | solution.py:202
  104.5 0.8 copy-done.3
  105.4 2.8 %score.7 = (bf16[9,180,128]{2,1,0:T(8,128)(2,1)S(1)}, f32[768,128]{1,0:T(8,128)S(1)}) custom-call(bf16[47,256,128]{2,1,0:T(8,128)(2,1)S(1)} %maximum_maximum_fusion.refs_0_, bf16[14,80,128]{2,1,0:T(8,128)(2,1)S(1)} %get-tuple-element.24.refs_1_, bf16[14,80,128]{2,1,0:T(8,128)(2,1)S(1)} %collective-permute-done.8.refs_2_, bf16[45,80,180]{2,1,0:T(8,128)(2,1)S(1)} %bitcast.40, ...), custom_call_target="tpu_custom_call" | custom-call | flops 424673280 | bytes 1695744 | tf_op jit(solution)/shard_map/score/pallas_call | solution.py:202
  108.9 3.5 %collective-permute-start.12 = (bf16[1,180,128]{2,1,0:T(8,128)(2,1)S(1)}, bf16[1,180,128]{2,1,0:T(8,128)(2,1)S(1)}, u32[]{:S(2)}, u32[]{:S(2)}) collective-permute-start(bf16[1,180,128]{2,1,0:T(8,128)(2,1)S(1)} %slice.77), channel_id=1, source_target_pairs={{0,1},{1,2},{2,3},{3,4},{4,5},{5,6},{6,7},{7,8},{8,9},{9,10},{10,1... | collective-permute-start | bytes 138248 | tf_op jit(solution)/shard_map/ppermute | solution.py:36
  112.4 8.8 %all-to-all-start = ((f32[256,1,384]{2,1,0:T(1,128)}), f32[256,1,384]{2,1,0:T(1,128)S(1)}, u32[]{:S(2)}, u32[]{:S(2)}) async-start(f32[256,1,384]{2,1,0:T(1,128)} %bitcast.45), calls=%async_computation | async-start | bytes 786432 | tf_op jit(solution)/shard_map/all_to_all | solution.py:260
  121.2 1.3 collective-permute-start.14
  123.2 0.9 constant_dynamic-update-slice_fusion.4
  124.1 2.0 %constant_dynamic-update-slice_fusion.3 = (bf16[47,180,128]{2,1,0:T(8,128)(2,1)}, bf16[45,180,128]{2,1,0:T(8,128)(2,1)S(1)}) fusion(bf16[47,180,128]{2,1,0:T(8,128)(2,1)} %get-tuple-element.50, bf16[12,180,128]{2,1,0:T(8,128)(2,1)} %copy-done.5, bf16[45,180,128]{2,1,0:T(8,128)(2,1)S(1)} %get-tuple-element.51), kind=kLoop, calls=%fused_computation.9 | loop fusion | bytes 1695744
  126.1 1.0 constant_dynamic-update-slice_fusion.2
  127.1 0.9 constant_dynamic-update-slice_fusion.1
  128.0 1.3 collective-permute-start.15
  129.3 7.5 %collective-permute-start.18 = (bf16[45,1,128]{2,1,0:T(2,128)(2,1)S(1)}, bf16[45,1,128]{2,1,0:T(2,128)(2,1)S(1)}, u32[]{:S(2)}, u32[]{:S(2)}) collective-permute-start(bf16[45,1,128]{2,1,0:T(2,128)(2,1)S(1)} %get-tuple-element.37), channel_id=1, source_target_pairs={{0,32},{1,33},{2,34},{3,35},{4,36},{5,37},{6,38},{7,39},{8,40},{9,... | collective-permute-start | bytes 34568 | tf_op jit(solution)/shard_map/ppermute | solution.py:36
  136.8 1.4 constant_dynamic-update-slice_fusion
  138.2 3.9 %collective-permute-start.17 = (bf16[1,1,128]{2,1,0:T(2,128)(2,1)S(1)}, bf16[1,1,128]{2,1,0:T(2,128)(2,1)S(1)}, u32[]{:S(2)}, u32[]{:S(2)}) collective-permute-start(bf16[1,1,128]{2,1,0:T(2,128)(2,1)S(1)} %get-tuple-element.57), channel_id=1, source_target_pairs={{0,33},{1,34},{2,35},{3,36},{4,37},{5,38},{6,39},{7,40},{8,41},{9,... | collective-permute-start | bytes 776 | tf_op jit(solution)/shard_map/ppermute | solution.py:36
  142.5 1.0 broadcast_in_dim.14
  143.5 10.1 %all-to-all-start.1 = ((f32[256,1,384]{2,1,0:T(1,128)}), f32[256,1,384]{2,1,0:T(1,128)S(1)}, u32[]{:S(2)}, u32[]{:S(2)}) async-start(f32[256,1,384]{2,1,0:T(1,128)} %broadcast_in_dim.14), calls=%async_computation.1 | async-start | bytes 786432 | tf_op jit(solution)/shard_map/all_to_all | solution.py:260
  153.7 8.1 %maximum_maximum_fusion.1.slab_ref = bf16[47,256,128]{2,1,0:T(8,128)(2,1)S(1)} fusion(bf16[1,1,128]{2,1,0:T(2,128)(2,1)} %collective-permute-done.19, bf16[45,1,128]{2,1,0:T(2,128)(2,1)S(1)} %collective-permute-done.18, bf16[1,1,128]{2,1,0:T(2,128)(2,1)S(1)} %collective-permute-done.17, bf16[1,1,128]{2,1,0:T(2,128)(2,1)} %collective-permute-done.16, ...), kind=kLoop, calls=%fused_computation.1 | loop fusion | flops 24641536 | bytes 5270528 | tf_op jit(solution)/shard_map/concatenate | solution.py:54
  161.8 7.5 %backward.1 = bf16[45,180,128]{2,1,0:T(8,128)(2,1)} custom-call(bf16[47,256,128]{2,1,0:T(8,128)(2,1)S(1)} %maximum_maximum_fusion.1.slab_ref, bf16[384,384]{1,0:T(8,128)(2,1)S(1)} %bitcast.46), custom_call_target="tpu_custom_call" | custom-call | flops 3397386240 | bytes 5898240 | tf_op jit(solution)/shard_map/backward/pallas_call | solution.py:243
  169.3 1.5 all-to-all-done.1
  172.0 1.1 slice_multiply_fusion
  (63 shorter events, 8.0 us)
Async XLA Ops:
  1.6 40.2 %collective-permute-start.3 = (bf16[45,1,128]{2,1,0:T(2,128)(2,1)S(1)}, bf16[45,1,128]{2,1,0:T(2,128)(2,1)S(1)}, u32[]{:S(2)}, u32[]{:S(2)}) collective-permute-start(bf16[45,1,128]{2,1,0:T(2,128)(2,1)S(1)} %get-tuple-element.44), channel_id=1, source_target_pairs={{32,0},{33,1},{34,2},{35,3},{36,4},{37,5},{38,6},{39,7},{40,8},{41... | collective-permute-start | bytes 34568 | tf_op jit(solution)/shard_map/ppermute | solution.py:36
  2.9 38.9 %collective-permute-start.6 = (bf16[45,1,128]{2,1,0:T(2,128)(2,1)S(1)}, bf16[45,1,128]{2,1,0:T(2,128)(2,1)S(1)}, u32[]{:S(2)}, u32[]{:S(2)}) collective-permute-start(bf16[45,1,128]{2,1,0:T(2,128)(2,1)S(1)} %get-tuple-element.45), channel_id=1, source_target_pairs={{0,32},{1,33},{2,34},{3,35},{4,36},{5,37},{6,38},{7,39},{8,40},{9,... | collective-permute-start | bytes 34568 | tf_op jit(solution)/shard_map/ppermute | solution.py:36
  8.3 33.5 %collective-permute-start = (bf16[1,180,128]{2,1,0:T(8,128)(2,1)S(1)}, bf16[1,180,128]{2,1,0:T(8,128)(2,1)S(1)}, u32[]{:S(2)}, u32[]{:S(2)}) collective-permute-start(bf16[1,180,128]{2,1,0:T(8,128)(2,1)S(1)} %get-tuple-element.38), channel_id=1, source_target_pairs={{0,1},{1,2},{2,3},{3,4},{4,5},{5,6},{6,7},{7,8},{8,9},{9,10},{10,1... | collective-permute-start | bytes 138248 | tf_op jit(solution)/shard_map/ppermute | solution.py:36
  12.7 29.8 %collective-permute-start.1 = (bf16[1,180,128]{2,1,0:T(8,128)(2,1)S(1)}, bf16[1,180,128]{2,1,0:T(8,128)(2,1)S(1)}, u32[]{:S(2)}, u32[]{:S(2)}) collective-permute-start(bf16[1,180,128]{2,1,0:T(8,128)(2,1)S(1)} %get-tuple-element.39), channel_id=1, source_target_pairs={{0,31},{1,0},{2,1},{3,2},{4,3},{5,4},{6,5},{7,6},{8,7},{9,8},{10,9... | collective-permute-start | bytes 138248 | tf_op jit(solution)/shard_map/ppermute | solution.py:36
  13.4 8.9 %collective-permute-start.2 = (bf16[1,1,128]{2,1,0:T(2,128)(2,1)S(1)}, bf16[1,1,128]{2,1,0:T(2,128)(2,1)S(1)}, u32[]{:S(2)}, u32[]{:S(2)}) collective-permute-start(bf16[1,1,128]{2,1,0:T(2,128)(2,1)S(1)} %get-tuple-element.40), channel_id=1, source_target_pairs={{32,1},{33,2},{34,3},{35,4},{36,5},{37,6},{38,7},{39,8},{40,9},{41... | collective-permute-start | bytes 776 | tf_op jit(solution)/shard_map/ppermute | solution.py:36
  22.3 8.9 %collective-permute-start.7 = (bf16[1,1,128]{2,1,0:T(2,128)(2,1)S(1)}, bf16[1,1,128]{2,1,0:T(2,128)(2,1)S(1)}, u32[]{:S(2)}, u32[]{:S(2)}) collective-permute-start(bf16[1,1,128]{2,1,0:T(2,128)(2,1)S(1)} %get-tuple-element.41), channel_id=1, source_target_pairs={{0,63},{1,32},{2,33},{3,34},{4,35},{5,36},{6,37},{7,38},{8,39},{9,... | collective-permute-start | bytes 776 | tf_op jit(solution)/shard_map/ppermute | solution.py:36
  31.1 10.7 %copy-start.12 = (bf16[1,1,128]{2,1,0:T(2,128)(2,1)}, bf16[1,1,128]{2,1,0:T(2,128)(2,1)S(1)}, u32[]{:S(2)}) copy-start(bf16[1,1,128]{2,1,0:T(2,128)(2,1)S(1)} %collective-permute-done.7) | copy-start | bytes 772
  31.1 3.4 %collective-permute-start.5 = (bf16[1,1,128]{2,1,0:T(2,128)(2,1)S(1)}, bf16[1,1,128]{2,1,0:T(2,128)(2,1)S(1)}, u32[]{:S(2)}, u32[]{:S(2)}) collective-permute-start(bf16[1,1,128]{2,1,0:T(2,128)(2,1)S(1)} %get-tuple-element.42), channel_id=1, source_target_pairs={{0,33},{1,34},{2,35},{3,36},{4,37},{5,38},{6,39},{7,40},{8,41},{9,... | collective-permute-start | bytes 776 | tf_op jit(solution)/shard_map/ppermute | solution.py:36
  33.4 18.1 %copy-start = (bf16[1,180,45,80]{1,3,2,0:T(8,128)(2,1)S(1)}, bf16[1,180,45,80]{1,3,2,0:T(8,128)(2,1)}, u32[]{:S(2)}) copy-start(bf16[1,180,45,80]{1,3,2,0:T(8,128)(2,1)} %param.5) | copy-start | bytes 3888004
  34.5 7.3 %copy-start.13 = (bf16[1,1,128]{2,1,0:T(2,128)(2,1)}, bf16[1,1,128]{2,1,0:T(2,128)(2,1)S(1)}, u32[]{:S(2)}) copy-start(bf16[1,1,128]{2,1,0:T(2,128)(2,1)S(1)} %collective-permute-done.5) | copy-start | bytes 772
  34.5 7.3 %collective-permute-start.4 = (bf16[1,1,128]{2,1,0:T(2,128)(2,1)S(1)}, bf16[1,1,128]{2,1,0:T(2,128)(2,1)S(1)}, u32[]{:S(2)}, u32[]{:S(2)}) collective-permute-start(bf16[1,1,128]{2,1,0:T(2,128)(2,1)S(1)} %get-tuple-element.43), channel_id=1, source_target_pairs={{32,31},{33,0},{34,1},{35,2},{36,3},{37,4},{38,5},{39,6},{40,7},{4... | collective-permute-start | bytes 776 | tf_op jit(solution)/shard_map/ppermute | solution.py:36
  41.8 0.6 copy-start.10
  41.8 0.6 copy-start.11
  55.3 19.4 %collective-permute-start.11 = (bf16[15,80,128]{2,1,0:T(8,128)(2,1)}, bf16[15,80,128]{2,1,0:T(8,128)(2,1)}, u32[]{:S(2)}, u32[]{:S(2)}) collective-permute-start(bf16[15,80,128]{2,1,0:T(8,128)(2,1)} %get-tuple-element.27.refs_1_), channel_id=1, source_target_pairs={{0,128},{128,0},{1,129},{129,1},{2,130},{130,2},{3,131},{131,3},{4... | collective-permute-start | bytes 921608 | tf_op jit(solution)/shard_map/ppermute | solution.py:295
  59.8 1.5 copy-start.1
  64.8 30.7 %collective-permute-start.10 = (bf16[18,80,128]{2,1,0:T(8,128)(2,1)S(1)}, bf16[18,80,128]{2,1,0:T(8,128)(2,1)S(1)}, u32[]{:S(2)}, u32[]{:S(2)}) collective-permute-start(bf16[18,80,128]{2,1,0:T(8,128)(2,1)S(1)} %get-tuple-element.26.refs_1_), channel_id=1, source_target_pairs={{0,128},{128,0},{1,129},{129,1},{2,130},{130,2},{3,131},{131,3},{4... | collective-permute-start | bytes 1105928 | tf_op jit(solution)/shard_map/ppermute | solution.py:295
  70.0 30.1 %collective-permute-start.9 = (bf16[21,80,128]{2,1,0:T(8,128)(2,1)S(1)}, bf16[21,80,128]{2,1,0:T(8,128)(2,1)S(1)}, u32[]{:S(2)}, u32[]{:S(2)}) collective-permute-start(bf16[21,80,128]{2,1,0:T(8,128)(2,1)S(1)} %get-tuple-element.25.refs_1_), channel_id=1, source_target_pairs={{0,128},{128,0},{1,129},{129,1},{2,130},{130,2},{3,131},{131,3},{4... | collective-permute-start | bytes 1290248 | tf_op jit(solution)/shard_map/ppermute | solution.py:295
  70.5 4.1 %copy-start.2 = (bf16[180,45,80]{0,2,1:T(8,128)(2,1)S(1)}, bf16[180,45,80]{0,2,1:T(8,128)(2,1)}, u32[]{:S(2)}) copy-start(bf16[180,45,80]{0,2,1:T(8,128)(2,1)} %param.6) | copy-start | bytes 3888004
  73.4 31.9 %collective-permute-start.8 = (bf16[14,80,128]{2,1,0:T(8,128)(2,1)S(1)}, bf16[14,80,128]{2,1,0:T(8,128)(2,1)S(1)}, u32[]{:S(2)}, u32[]{:S(2)}) collective-permute-start(bf16[14,80,128]{2,1,0:T(8,128)(2,1)S(1)} %get-tuple-element.24.refs_1_), channel_id=1, source_target_pairs={{0,128},{128,0},{1,129},{129,1},{2,130},{130,2},{3,131},{131,3},{4... | collective-permute-start | bytes 860168 | tf_op jit(solution)/shard_map/ppermute | solution.py:295
  80.0 58.3 %collective-permute-start.16 = (bf16[1,1,128]{2,1,0:T(2,128)(2,1)}, bf16[1,1,128]{2,1,0:T(2,128)(2,1)}, u32[]{:S(2)}, u32[]{:S(2)}) collective-permute-start(bf16[1,1,128]{2,1,0:T(2,128)(2,1)} %get-tuple-element.52), channel_id=1, source_target_pairs={{32,31},{33,0},{34,1},{35,2},{36,3},{37,4},{38,5},{39,6},{40,7},{4... | collective-permute-start | bytes 776 | tf_op jit(solution)/shard_map/ppermute | solution.py:36
  81.3 72.4 %collective-permute-start.19 = (bf16[1,1,128]{2,1,0:T(2,128)(2,1)}, bf16[1,1,128]{2,1,0:T(2,128)(2,1)}, u32[]{:S(2)}, u32[]{:S(2)}) collective-permute-start(bf16[1,1,128]{2,1,0:T(2,128)(2,1)} %get-tuple-element.53), channel_id=1, source_target_pairs={{0,63},{1,32},{2,33},{3,34},{4,35},{5,36},{6,37},{7,38},{8,39},{9,... | collective-permute-start | bytes 776 | tf_op jit(solution)/shard_map/ppermute | solution.py:36
  95.5 33.8 %collective-permute-start.13 = (bf16[1,180,128]{2,1,0:T(8,128)(2,1)}, bf16[1,180,128]{2,1,0:T(8,128)(2,1)}, u32[]{:S(2)}, u32[]{:S(2)}) collective-permute-start(bf16[1,180,128]{2,1,0:T(8,128)(2,1)} %slice.78), channel_id=1, source_target_pairs={{0,31},{1,0},{2,1},{3,2},{4,3},{5,4},{6,5},{7,6},{8,7},{9,8},{10,9... | collective-permute-start | bytes 138248 | tf_op jit(solution)/shard_map/ppermute | solution.py:36
  99.3 0.8 copy-start.5
  104.5 0.8 copy-start.3
  108.2 0.7 copy-start.8
  108.9 3.5 %copy-start.6 = (bf16[9,180,128]{2,1,0:T(8,128)(2,1)}, bf16[9,180,128]{2,1,0:T(8,128)(2,1)S(1)}, u32[]{:S(2)}) copy-start(bf16[9,180,128]{2,1,0:T(8,128)(2,1)S(1)} %get-tuple-element.32) | copy-start | bytes 1244164
  108.9 17.2 %copy-start.4 = (bf16[14,180,128]{2,1,0:T(8,128)(2,1)S(1)}, bf16[14,180,128]{2,1,0:T(8,128)(2,1)}, u32[]{:S(2)}) copy-start(bf16[14,180,128]{2,1,0:T(8,128)(2,1)} %copy-done.3) | copy-start | bytes 1935364
  108.9 13.6 %collective-permute-start.12 = (bf16[1,180,128]{2,1,0:T(8,128)(2,1)S(1)}, bf16[1,180,128]{2,1,0:T(8,128)(2,1)S(1)}, u32[]{:S(2)}, u32[]{:S(2)}) collective-permute-start(bf16[1,180,128]{2,1,0:T(8,128)(2,1)S(1)} %slice.77), channel_id=1, source_target_pairs={{0,1},{1,2},{2,3},{3,4},{4,5},{5,6},{6,7},{7,8},{8,9},{9,10},{10,1... | collective-permute-start | bytes 138248 | tf_op jit(solution)/shard_map/ppermute | solution.py:36
  112.4 14.7 %copy-start.7 = (bf16[9,180,128]{2,1,0:T(8,128)(2,1)S(1)}, bf16[9,180,128]{2,1,0:T(8,128)(2,1)}, u32[]{:S(2)}) copy-start(bf16[9,180,128]{2,1,0:T(8,128)(2,1)} %copy-done.6) | copy-start | bytes 1244164
  112.4 29.8 %all-to-all-start = ((f32[256,1,384]{2,1,0:T(1,128)}), f32[256,1,384]{2,1,0:T(1,128)S(1)}, u32[]{:S(2)}, u32[]{:S(2)}) async-start(f32[256,1,384]{2,1,0:T(1,128)} %bitcast.45), calls=%async_computation | async-start | bytes 786432 | tf_op jit(solution)/shard_map/all_to_all | solution.py:260
  121.2 32.4 %collective-permute-start.14 = (bf16[1,1,128]{2,1,0:T(2,128)(2,1)S(1)}, bf16[1,1,128]{2,1,0:T(2,128)(2,1)S(1)}, u32[]{:S(2)}, u32[]{:S(2)}) collective-permute-start(bf16[1,1,128]{2,1,0:T(2,128)(2,1)S(1)} %get-tuple-element.56), channel_id=1, source_target_pairs={{32,1},{33,2},{34,3},{35,4},{36,5},{37,6},{38,7},{39,8},{40,9},{41... | collective-permute-start | bytes 776 | tf_op jit(solution)/shard_map/ppermute | solution.py:36
  128.0 25.6 %collective-permute-start.15 = (bf16[45,1,128]{2,1,0:T(2,128)(2,1)S(1)}, bf16[45,1,128]{2,1,0:T(2,128)(2,1)S(1)}, u32[]{:S(2)}, u32[]{:S(2)}) collective-permute-start(bf16[45,1,128]{2,1,0:T(2,128)(2,1)S(1)} %get-tuple-element.36), channel_id=1, source_target_pairs={{32,0},{33,1},{34,2},{35,3},{36,4},{37,5},{38,6},{39,7},{40,8},{41... | collective-permute-start | bytes 34568 | tf_op jit(solution)/shard_map/ppermute | solution.py:36
  129.3 24.3 %collective-permute-start.18 = (bf16[45,1,128]{2,1,0:T(2,128)(2,1)S(1)}, bf16[45,1,128]{2,1,0:T(2,128)(2,1)S(1)}, u32[]{:S(2)}, u32[]{:S(2)}) collective-permute-start(bf16[45,1,128]{2,1,0:T(2,128)(2,1)S(1)} %get-tuple-element.37), channel_id=1, source_target_pairs={{0,32},{1,33},{2,34},{3,35},{4,36},{5,37},{6,38},{7,39},{8,40},{9,... | collective-permute-start | bytes 34568 | tf_op jit(solution)/shard_map/ppermute | solution.py:36
  138.2 15.4 %collective-permute-start.17 = (bf16[1,1,128]{2,1,0:T(2,128)(2,1)S(1)}, bf16[1,1,128]{2,1,0:T(2,128)(2,1)S(1)}, u32[]{:S(2)}, u32[]{:S(2)}) collective-permute-start(bf16[1,1,128]{2,1,0:T(2,128)(2,1)S(1)} %get-tuple-element.57), channel_id=1, source_target_pairs={{0,33},{1,34},{2,35},{3,36},{4,37},{5,38},{6,39},{7,40},{8,41},{9,... | collective-permute-start | bytes 776 | tf_op jit(solution)/shard_map/ppermute | solution.py:36
  143.5 18.3 %copy-start.9 = (bf16[48,8,3,128]{3,1,2,0:T(8,128)(2,1)S(1)}, bf16[48,8,3,128]{3,1,2,0:T(8,128)(2,1)}, u32[]{:S(2)}) copy-start(bf16[48,8,3,128]{3,1,2,0:T(8,128)(2,1)} %copy.22) | copy-start | bytes 884740
  143.5 27.4 %all-to-all-start.1 = ((f32[256,1,384]{2,1,0:T(1,128)}), f32[256,1,384]{2,1,0:T(1,128)S(1)}, u32[]{:S(2)}, u32[]{:S(2)}) async-start(f32[256,1,384]{2,1,0:T(1,128)} %broadcast_in_dim.14), calls=%async_computation.1 | async-start | bytes 786432 | tf_op jit(solution)/shard_map/all_to_all | solution.py:260

commit v2 on v1

v2 whole, which is shorter than its diff:
```python
import functools
import math

import jax
import jax.numpy as jnp
from jax import lax
from jax.experimental import pallas as pl
from jax.experimental.pallas import tpu as pltpu
from jax.sharding import PartitionSpec as P

epsilon = 1e-06
RING = 256
LANES = 128
TILE = 16
AXES = ("member", "lat", "lon")
VMEM = pl.BlockSpec(memory_space=pltpu.VMEM)
ANY = pl.BlockSpec(memory_space=pl.ANY)


def latitude_weights(row_index, total_rows):
    scale = math.pi / total_rows
    angles = 0.5 * math.pi - (row_index.astype(jnp.float32) + 0.5) * scale
    every_row = (
        0.5 * math.pi - (jnp.arange(total_rows, dtype=jnp.int32).astype(jnp.float32) + 0.5) * scale
    )
    return jnp.cos(angles) / jnp.mean(jnp.cos(every_row))


def swapped(first, last, axis, wraps):
    count = lax.axis_size(axis)
    even = lax.axis_index(axis) % 2 == 0
    inner = [(i, i + 1) for i in range(0, count, 2)]
    outer = [(i, (i + 1) % count) for i in range(1, count, 2) if wraps or i + 1 < count]
    both = [pairs + [(j, i) for i, j in pairs] for pairs in (inner, outer)]
    near = lax.ppermute(jnp.where(even, last, first), axis, both[0])
    far = lax.ppermute(jnp.where(even, first, last), axis, both[1])
    return jnp.where(even, far, near), jnp.where(even, near, far)


def lat_edges(columns):
    count, rows, channels = columns.shape
    body = rows - rows % TILE
    above, below = swapped(columns[:, :1], columns[:, rows - 1 :], "lat", False)
    gap = jnp.zeros((count, TILE - 1, channels), columns.dtype)
    low = jnp.concatenate([columns[:, body:], below, gap[:, : TILE - 1 - (rows - body)]], axis=1)
    return low, jnp.concatenate([gap, above], axis=1)


def lon_edges(columns, low, high):
    body = columns.shape[1] - columns.shape[1] % TILE

    def ring(part):
        gap = jnp.zeros((1, RING - body - 2 * TILE, columns.shape[2]), columns.dtype)
        return jnp.concatenate([columns[part, :body], low[part], gap, high[part]], axis=1)

    return swapped(ring(slice(0, 1)), ring(slice(-1, None)), "lon", True)


def fill(slab_v, place, field_ref, low_ref, high_ref, column):
    body = field_ref.shape[1] - field_ref.shape[1] % TILE
    slab_v[place, :body] = field_ref[column, :body]
    slab_v[place, body : body + TILE] = low_ref[column]
    gap = RING - body - 2 * TILE
    slab_v[place, body + TILE : RING - TILE] = jnp.zeros((gap, slab_v.shape[2]), slab_v.dtype)
    slab_v[place, RING - TILE :] = high_ref[column]


def fill_chunk(slab_v, start, count, wraps, field, edges):
    inside = count + 1 if wraps else count + 2

    def one(i, carry):
        fill(slab_v, i, *field, start - 1 + i)
        return carry

    lax.fori_loop(0, inside, one, 0)
    if wraps:
        west_ref, east_ref = edges
        slab_v[inside] = east_ref[0]
        slab_v[inside + 1] = west_ref[0]
        fill(slab_v, inside + 2, *field, 0)
        fill(slab_v, inside + 3, *field, 1)


def window(slab_v, place):
    return jnp.concatenate([slab_v[place + b] for b in range(3)], axis=1)


def each_column(start, count, wraps, one, carry):
    total = count + wraps

    def at(slot, odd, carry):
        return one(slot, start + slot, slot, total + slot // 2, odd, carry)

    def pair(t, carry):
        carry = one(2 * t, start + 2 * t, 2 * t, total + t, 0, carry)
        return one(2 * t + 1, start + 2 * t + 1, 2 * t + 1, total + t, 1, carry)

    carry = lax.fori_loop(0, count // 2, pair, carry)
    if count % 2:
        carry = at(count - 1, 0, carry)
    if wraps:
        carry = one(count, 0, count + 2, total + count // 2, count % 2, carry)
    return carry


def write_columns(source_v, out, start, count, wraps, sems):
    copies = [pltpu.make_async_copy(source_v.at[pl.ds(0, count)], out.at[pl.ds(start, count)], sems.at[0])]
    if wraps:
        copies.append(
            pltpu.make_async_copy(source_v.at[pl.ds(count, 1)], out.at[pl.ds(0, 1)], sems.at[1])
        )
    for copy in copies:
        copy.start()
    for copy in copies:
        copy.wait()


def forward_kernel(start, count, wraps, n_given, *refs):
    field, present_ref, taps_ref = refs[:3], refs[3], refs[4]
    edges = refs[5:7] if wraps else ()
    pred_out, packed_out, slab_v, weights_v, pred_v, sems = refs[n_given:]
    outputs, rows = present_ref.shape[1:]
    for a in range(3):
        weights_v[a * outputs : (a + 1) * outputs] = jnp.concatenate(
            [taps_ref[a, b] for b in range(3)], axis=1
        )
    fill_chunk(slab_v, start, count, wraps, field, edges)
    half = LANES // 2

    def one(slot, column, place, block, odd, carry):
        y = lax.dot_general(
            weights_v[...],
            window(slab_v, place),
            (((1,), (1,)), ((), ())),
            preferred_element_type=jnp.float32,
        )
        increment = (
            pltpu.roll(y[:outputs], 1, 1)
            + y[outputs : 2 * outputs]
            + pltpu.roll(y[2 * outputs :], RING - 1, 1)
        )
        head = increment[:, :LANES] + present_ref[column, :, :LANES].astype(jnp.float32)
        tail = increment[:, LANES:rows] + present_ref[column, :, LANES:].astype(jnp.float32)
        head = head.astype(jnp.bfloat16)
        tail = tail.astype(jnp.bfloat16)
        pred_v[slot, :, :LANES] = head
        pred_v[slot, :, LANES:] = tail
        packed_out[slot] = head
        packed_out[block, :, odd * half : odd * half + rows - LANES] = tail
        return carry

    each_column(start, count, wraps, one, 0)
    write_columns(pred_v, pred_out, start, count, wraps, sems)


def forward(start, count, wraps, field, present, taps, edges, pred):
    columns, outputs, rows = present.shape
    inputs = taps.shape[3]
    total = count + wraps
    given = [*field, present, taps] + (list(edges) if wraps else [])
    in_specs = [VMEM] * len(given)
    aliases = {}
    if pred is not None:
        aliases = {len(given): 0}
        given.append(pred)
        in_specs.append(ANY)
    return pl.pallas_call(
        functools.partial(forward_kernel, start, count, wraps, len(given)),
        out_shape=(
            jax.ShapeDtypeStruct((columns, outputs, rows), jnp.bfloat16),
            jax.ShapeDtypeStruct((total + (total + 1) // 2, outputs, LANES), jnp.bfloat16),
        ),
        in_specs=in_specs,
        out_specs=(ANY, VMEM),
        scratch_shapes=[
            pltpu.VMEM((count + 2 + 3 * wraps, RING, inputs), jnp.bfloat16),
            pltpu.VMEM((3 * outputs, 3 * inputs), jnp.bfloat16),
            pltpu.VMEM((total, outputs, rows), jnp.bfloat16),
            pltpu.SemaphoreType.DMA((2,)),
        ],
        input_output_aliases=aliases,
        compiler_params=pltpu.CompilerParams(vmem_limit_bytes=24 << 20),
        cost_estimate=pl.CostEstimate(
            flops=2 * total * 9 * inputs * outputs * RING,
            bytes_accessed=total * RING * (inputs + 3 * outputs) * 2,
            transcendentals=0,
        ),
        name="forward",
    )(*given)


def score_kernel(start, count, wraps, n_edges, adds, n_given, *refs):
    field, own_ref, other_ref, target_ref, weight_ref = refs[:3], *refs[3:7]
    edges = refs[7 : 7 + n_edges]
    sums_ref = refs[7 + n_edges] if adds else None
    turned_out, sums_out, slab_v, cot_v, acc_v, turned_v, sems = refs[n_given:]
    outputs, rows = target_ref.shape[1:]
    inputs = slab_v.shape[2]
    half = LANES // 2
    weight = weight_ref[...]
    cot_v[...] = jnp.zeros_like(cot_v)
    acc_v[...] = jnp.zeros_like(acc_v)
    fill_chunk(slab_v, start, count, wraps, field, edges)

    def one(slot, column, place, block, odd, score):
        lanes_of_tail = slice(odd * half, odd * half + rows - LANES)
        halves = []
        for side in range(2):
            lanes = slice(0, LANES) if side == 0 else slice(LANES, rows)
            if side == 0:
                value, partner = (ref[slot].astype(jnp.float32) for ref in (own_ref, other_ref))
            else:
                value, partner = (
                    ref[block, :, lanes_of_tail].astype(jnp.float32) for ref in (own_ref, other_ref)
                )
            misfit = value - target_ref[column, :, lanes].astype(jnp.float32)
            spread = value - partner
            error2 = jnp.sum(misfit * misfit, axis=0, keepdims=True) + epsilon
            pair2 = jnp.sum(spread * spread, axis=0, keepdims=True) + epsilon
            error_inv = lax.rsqrt(error2)
            pair_inv = lax.rsqrt(pair2)
            scale = 0.5 * weight[:, lanes]
            cot_v[odd, :outputs, lanes] = misfit * (scale * error_inv) - spread * (scale * pair_inv)
            halves.append(scale * (error2 * error_inv - 0.5 * (pair2 * pair_inv)))
        cot = cot_v[odd]
        turned_v[slot] = cot.T[:rows].astype(jnp.bfloat16)
        cot = cot[:outputs]
        shifted = jnp.concatenate([pltpu.roll(cot, RING - 1, 1), cot, pltpu.roll(cot, 1, 1)], axis=0)
        acc_v[...] += jnp.dot(
            shifted.astype(jnp.bfloat16), window(slab_v, place), preferred_element_type=jnp.float32
        )
        return tuple(s + h for s, h in zip(score, halves))

    score = (jnp.zeros((1, LANES), jnp.float32), jnp.zeros((1, rows - LANES), jnp.float32))
    score = each_column(start, count, wraps, one, score)
    for a in range(3):
        for b in range(3):
            block = acc_v[a * outputs : (a + 1) * outputs, b * inputs : (b + 1) * inputs]
            place = slice((3 * a + b) * outputs, (3 * a + b + 1) * outputs)
            sums_out[place] = block + sums_ref[place] if adds else block
    spare = slice(9 * outputs, sums_out.shape[0])
    total = sum(jnp.sum(part, axis=1, keepdims=True) for part in score)
    filler = jnp.broadcast_to(total, (sums_out.shape[0] - 9 * outputs, inputs))
    sums_out[spare] = filler + sums_ref[spare] if adds else filler
    write_columns(turned_v, turned_out, start, count, wraps, sems)


def scored(start, count, wraps, field, own, other, target, weight, edges, carried, sum_rows):
    columns, outputs, rows = target.shape
    inputs = field[0].shape[2]
    total = count + wraps
    edges = list(edges) if wraps else []
    given = [*field, own, other, target, weight, *edges]
    in_specs = [VMEM] * len(given)
    aliases = {}
    if carried is not None:
        turned, sums = carried
        aliases = {len(given) + 1: 0}
        given += [sums, turned]
        in_specs += [VMEM, ANY]
    return pl.pallas_call(
        functools.partial(
            score_kernel, start, count, wraps, len(edges), carried is not None, len(given)
        ),
        out_shape=(
            jax.ShapeDtypeStruct((columns, rows, LANES), jnp.bfloat16),
            jax.ShapeDtypeStruct((sum_rows, inputs), jnp.float32),
        ),
        in_specs=in_specs,
        out_specs=(ANY, VMEM),
        scratch_shapes=[
            pltpu.VMEM((count + 2 + 3 * wraps, RING, inputs), jnp.bfloat16),
            pltpu.VMEM((2, LANES, RING), jnp.float32),
            pltpu.VMEM((3 * outputs, 3 * inputs), jnp.float32),
            pltpu.VMEM((total, rows, LANES), jnp.bfloat16),
            pltpu.SemaphoreType.DMA((2,)),
        ],
        input_output_aliases=aliases,
        compiler_params=pltpu.CompilerParams(vmem_limit_bytes=24 << 20),
        cost_estimate=pl.CostEstimate(
            flops=2 * total * 9 * inputs * outputs * RING,
            bytes_accessed=total * RING * (inputs + 3 * outputs) * 2,
            transcendentals=2 * total * rows,
        ),
        name="score",
    )(*given)


def backward_kernel(block, *refs):
    field, west_ref, east_ref, taps_ref, slope_out, slab_v, weights_v = refs[:3], *refs[3:]
    rows, inputs = slope_out.shape[1:]
    columns = field[0].shape[0]
    outputs = taps_ref.shape[2]
    base = pl.program_id(0) * block

    @pl.when(pl.program_id(0) == 0)
    def _():
        spare = jnp.zeros((LANES - outputs, inputs), weights_v.dtype)
        for b in range(3):
            row = [jnp.concatenate([taps_ref[2 - a, 2 - b], spare], axis=0) for a in range(3)]
            weights_v[b * LANES : (b + 1) * LANES] = jnp.concatenate(row, axis=1)

        def one(i, carry):
            fill(slab_v, i + 1, *field, i)
            return carry

        lax.fori_loop(0, columns, one, 0)
        slab_v[0] = west_ref[0]
        slab_v[columns + 1] = east_ref[0]

    for j in range(block):
        z = jnp.dot(window(slab_v, base + j), weights_v[...], preferred_element_type=jnp.float32)
        slope = (
            pltpu.roll(z[:, :inputs], 1, 0)
            + z[:, inputs : 2 * inputs]
            + pltpu.roll(z[:, 2 * inputs :], RING - 1, 0)
        )
        slope_out[j] = slope[:rows].astype(jnp.bfloat16)


def backward(field, edges, taps):
    columns, rows = field[0].shape[:2]
    inputs = taps.shape[3]
    block = max(n for n in range(1, 6) if columns % n == 0)
    return pl.pallas_call(
        functools.partial(backward_kernel, block),
        grid=(columns // block,),
        out_shape=jax.ShapeDtypeStruct((columns, rows, inputs), jnp.bfloat16),
        in_specs=[VMEM] * 6,
        out_specs=pl.BlockSpec((block, rows, inputs), lambda i: (i, 0, 0)),
        scratch_shapes=[
            pltpu.VMEM((columns + 2, RING, LANES), jnp.bfloat16),
            pltpu.VMEM((3 * LANES, 3 * inputs), jnp.bfloat16),
        ],
        compiler_params=pltpu.CompilerParams(vmem_limit_bytes=24 << 20),
        cost_estimate=pl.CostEstimate(
            flops=2 * columns * 9 * inputs * LANES * RING,
            bytes_accessed=columns * RING * (inputs + LANES) * 2,
            transcendentals=0,
        ),
        name="backward",
    )(*field, *edges, taps)


def exchange(blocks):
    return lax.all_to_all(blocks, AXES, 0, 0, tiled=True)


def split(columns):
    shares = (8, 14, 14, 9)
    edges = [1]
    for i in range(len(shares) - 1):
        edges.append(1 + 2 * round(columns * sum(shares[: i + 1]) / sum(shares) / 2))
    edges.append(columns)
    return [(low, high - low) for low, high in zip(edges, edges[1:])]


def local(features, present_condition, target, filter_weights_tensor):
    lat_rows, lon_cols, inputs = features.shape[1:]
    outputs = target.shape[2]
    total_rows = lat_rows * lax.axis_size("lat")
    total_cols = lon_cols * lax.axis_size("lon")
    devices = math.prod(lax.axis_size(axis) for axis in AXES)

    taps = jnp.transpose(filter_weights_tensor, (0, 1, 3, 2))
    row_index = lax.axis_index("lat") * lat_rows + jnp.arange(lat_rows, dtype=jnp.int32)
    weight = latitude_weights(row_index, total_rows)[None]
    columns = jnp.transpose(features[0], (1, 0, 2))
    present = jnp.transpose(present_condition[0], (1, 2, 0))
    truth = jnp.transpose(target, (1, 2, 0))

    field = (columns, *lat_edges(columns))
    edges = lon_edges(*field)
    chunks = split(lon_cols)
    pred = None
    packed = []
    for start, count in chunks:
        wraps = int(start + count == lon_cols)
        pred, own = forward(start, count, wraps, field, present, taps, edges, pred)
        packed.append((own, lax.ppermute(own, "member", [(0, 1), (1, 0)])))

    width = -(-(9 * outputs * inputs + 1) // (devices * LANES)) * LANES
    sum_rows = devices * width // inputs
    carried = None
    for (start, count), (own, other) in zip(chunks, packed):
        wraps = int(start + count == lon_cols)
        carried = scored(
            start, count, wraps, field, own, other, truth, weight, edges, carried, sum_rows
        )
    turned, sums = carried
    share = jnp.sum(exchange(sums.reshape(devices, width)), axis=0, keepdims=True)
    whole = exchange(jnp.broadcast_to(share, (devices, width))).reshape(sum_rows, inputs)

    field = (turned, *lat_edges(turned))
    slope = backward(field, lon_edges(*field), taps)
    objective_mean = whole[9 * outputs, 0] / (total_rows * total_cols)
    summed = whole[: 9 * outputs] / math.sqrt(2.0 * total_rows * total_cols)
    filter_weights_slope = jnp.transpose(summed.reshape(3, 3, outputs, inputs), (0, 1, 3, 2))
    return (
        jnp.transpose(pred, (2, 0, 1))[None],
        objective_mean,
        jnp.transpose(slope, (1, 0, 2))[None],
        filter_weights_slope,
    )


def solution(mesh):
    in_specs = (
        P("member", "lat", "lon", None),
        P("member", "lat", "lon", None),
        P("lat", "lon", None),
        P(),
    )
    out_specs = (P("member", "lat", "lon", None), P(), P("member", "lat", "lon", None), P())
    return jax.shard_map(local, mesh=mesh, in_specs=in_specs, out_specs=out_specs, check_vma=False)
```

time: 175 us -> 129 us (0.74)
  the two profiles are of different devices: /device:TPU:1 before, /device:TPU:4 now
where the time goes in v2:
time: 129 us; the launch traced here: 128 us
  Pallas kernels  43.9 us (34%)
  starting transfers between devices  42.4 us (33%)
  waiting for transfers between devices  22.9 us (18%)
  local copies, waits for them, and re-layouts  12 us (9%)
  other arithmetic  3.72 us (3%)
  between operations  3.42 us (3%)
    pallas_call x4, Pallas kernels, scored(): pl.pallas_call(functools.partial(score_kernel, start, count, wraps, len(e...  20.5 us
    ppermute x4, starting transfers between devices, swapped(): far = lax.ppermute(jnp.where(even, first, last), axis, both[1])  19.5 us
    all_to_all x2, starting transfers between devices, exchange(): return lax.all_to_all(blocks, AXES, 0, 0, tiled=True)  17.4 us
    pallas_call x4, Pallas kernels, forward(): pl.pallas_call(functools.partial(forward_kernel, start, count, wraps, len...  15.5 us
    all_to_all x2, waiting for transfers between devices, exchange(): return lax.all_to_all(blocks, AXES, 0, 0, tiled=True)  14.5 us
    ppermute x4, waiting for transfers between devices, swapped(): far = lax.ppermute(jnp.where(even, first, last), axis, both[1])  8.41 us
    pallas_call x1, Pallas kernels, backward(): pl.pallas_call(functools.partial(backward_kernel, block), grid=(columns /...  7.97 us
    unnamed x18, local copies, waits for them, and re-layouts  6.85 us
  transfers between devices with their start and end apart: 14, of which 3 were waited for; matrix products, arithmetic and copies ran while one was open for 4% of the time, Pallas kernels for 28%

profile of v2, /device:TPU:4, one launch (start us, length us, event | category | flops | bytes accessed | tf_op | source)
XLA Modules:
  0.0 128.4 jit_solution(17019907547611660238)
XLA Ops:
  0.6 1.0 broadcast_select_fusion.14
  1.6 1.3 collective-permute-start
  2.9 3.5 %collective-permute-start.1 = (bf16[45,1,128]{2,1,0:T(2,128)(2,1)S(1)}, bf16[45,1,128]{2,1,0:T(2,128)(2,1)S(1)}, u32[]{:S(2)}, u32[]{:S(2)}) collective-permute-start(bf16[45,1,128]{2,1,0:T(2,128)(2,1)S(1)} %get-tuple-element.42), channel_id=1, source_target_pairs={{32,64},{64,32},{33,65},{65,33},{34,66},{66,34},{35,67},{67,35},{3... | collective-permute-start | bytes 34568 | tf_op jit(solution)/shard_map/ppermute | solution.py:36
  6.4 0.8 fusion.1
  7.3 0.9 slice.82
  8.2 0.1 pad.23.clone
  8.3 0.1 pad.19.clone
  8.3 0.3 collective-permute-done.1
  8.7 0.1 maximum_maximum_fusion.refs_1_
  8.9 1.6 %copy-done = bf16[1,180,45,128]{3,1,2,0:T(8,128)(2,1)S(1)} copy-done((bf16[1,180,45,128]{3,1,2,0:T(8,128)(2,1)S(1)}, bf16[1,180,45,128]{3,1,2,0:T(8,128)(2,1)}, u32[]{:S(2)}) %copy-start) | copy-done | bytes 2073624
  10.5 1.5 %copy-done.4 = bf16[1,180,45,80]{1,3,2,0:T(8,128)(2,1)S(1)} copy-done((bf16[1,180,45,80]{1,3,2,0:T(8,128)(2,1)S(1)}, bf16[1,180,45,80]{1,3,2,0:T(8,128)(2,1)}, u32[]{:S(2)}) %copy-start.4) | copy-done | bytes 1296024
  12.0 0.9 copy-done.7
  12.9 3.4 %forward.4 = (bf16[45,80,180]{2,1,0:T(8,128)(2,1)}, bf16[12,80,128]{2,1,0:T(8,128)(2,1)}) custom-call(bf16[45,180,128]{2,1,0:T(8,128)(2,1)S(1)} %bitcast.23, bf16[45,16,128]{2,1,0:T(8,128)(2,1)S(1)} %maximum_maximum_fusion.refs_1_, bf16[45,16,128]{2,1,0:T(8,128)(2,1)S(1)} %concatenate.91.refs_2_, bf16[45,80,180]{2,1,0:T(8,128)(2,1)S(1)} %bitcast.35, ...), custom_call_target="tpu_custom_call" | custom-call | flops 377487360 | bytes 1507328 | tf_op jit(solution)/shard_map/forward/pallas_call | solution.py:167
  16.2 1.7 %collective-permute-start.7 = (bf16[12,80,128]{2,1,0:T(8,128)(2,1)}, bf16[12,80,128]{2,1,0:T(8,128)(2,1)}, u32[]{:S(2)}, u32[]{:S(2)}) collective-permute-start(bf16[12,80,128]{2,1,0:T(8,128)(2,1)} %get-tuple-element.27.refs_3_), channel_id=1, source_target_pairs={{0,128},{128,0},{1,129},{129,1},{2,130},{130,2},{3,131},{131,3},{4... | collective-permute-start | bytes 737288 | tf_op jit(solution)/shard_map/ppermute | solution.py:380
  17.9 0.1 broadcast_select_fusion.6
  18.0 6.0 %collective-permute-start.2 = (bf16[1,256,128]{2,1,0:T(8,128)(2,1)S(1)}, bf16[1,256,128]{2,1,0:T(8,128)(2,1)S(1)}, u32[]{:S(2)}, u32[]{:S(2)}) collective-permute-start(bf16[1,256,128]{2,1,0:T(8,128)(2,1)S(1)} %get-tuple-element.55), channel_id=1, source_target_pairs={{1,2},{3,4},{5,6},{7,8},{9,10},{11,12},{13,14},{15,16},{17,18},{19... | collective-permute-start | bytes 196616 | tf_op jit(solution)/shard_map/ppermute | solution.py:36
  24.0 4.9 %forward.5 = (bf16[45,80,180]{2,1,0:T(8,128)(2,1)}, bf16[21,80,128]{2,1,0:T(8,128)(2,1)}) custom-call(bf16[45,180,128]{2,1,0:T(8,128)(2,1)S(1)} %bitcast.24, bf16[45,16,128]{2,1,0:T(8,128)(2,1)S(1)} %maximum_maximum_fusion.refs_1_, bf16[45,16,128]{2,1,0:T(8,128)(2,1)S(1)} %concatenate.91.refs_2_, ...), custom_call_target="tpu_custom_call", output_to_operand_aliasing={{0}: (5, {})} | custom-call | flops 660602880 | bytes 2637824 | tf_op jit(solution)/shard_map/forward/pallas_call | solution.py:167
  29.0 0.2 collective-permute-start.6
  29.2 4.2 %forward.6 = (bf16[45,80,180]{2,1,0:T(8,128)(2,1)}, bf16[21,80,128]{2,1,0:T(8,128)(2,1)S(1)}) custom-call(bf16[45,180,128]{2,1,0:T(8,128)(2,1)S(1)} %bitcast.25, bf16[45,16,128]{2,1,0:T(8,128)(2,1)S(1)} %maximum_maximum_fusion.refs_1_, bf16[45,16,128]{2,1,0:T(8,128)(2,1)S(1)} %concatenate.91.refs_2_, ...), custom_call_target="tpu_custom_call", output_to_operand_aliasing={{0}: (5, {})} | custom-call | flops 660602880 | bytes 2637824 | tf_op jit(solution)/shard_map/forward/pallas_call | solution.py:167
  33.4 2.0 %collective-permute-start.5 = (bf16[21,80,128]{2,1,0:T(8,128)(2,1)S(1)}, bf16[21,80,128]{2,1,0:T(8,128)(2,1)}, u32[]{:S(2)}, u32[]{:S(2)}) collective-permute-start(bf16[21,80,128]{2,1,0:T(8,128)(2,1)S(1)} %get-tuple-element.25.refs_3_), channel_id=1, source_target_pairs={{0,128},{128,0},{1,129},{129,1},{2,130},{130,2},{3,131},{131,3},{4... | collective-permute-start | bytes 1290248 | tf_op jit(solution)/shard_map/ppermute | solution.py:380
  35.4 3.0 %forward.7 = (bf16[45,80,180]{2,1,0:T(8,128)(2,1)}, bf16[14,80,128]{2,1,0:T(8,128)(2,1)S(1)}) custom-call(bf16[45,180,128]{2,1,0:T(8,128)(2,1)S(1)} %bitcast.26, bf16[45,16,128]{2,1,0:T(8,128)(2,1)S(1)} %maximum_maximum_fusion.refs_1_, bf16[45,16,128]{2,1,0:T(8,128)(2,1)S(1)} %concatenate.91.refs_2_, ...), custom_call_target="tpu_custom_call", output_to_operand_aliasing={{0}: (7, {})} | custom-call | flops 424673280 | bytes 1695744 | tf_op jit(solution)/shard_map/forward/pallas_call | solution.py:167
  38.4 0.3 collective-permute-start.4
  38.7 0.6 cosine_reduce_fusion
  40.0 0.1 cosine_divide_fusion.refs_6_
  40.1 1.5 %copy-done.2 = bf16[180,45,80]{0,2,1:T(8,128)(2,1)S(1)} copy-done((bf16[180,45,80]{0,2,1:T(8,128)(2,1)S(1)}, bf16[180,45,80]{0,2,1:T(8,128)(2,1)}, u32[]{:S(2)}) %copy-start.2) | copy-done | bytes 1296024
  41.5 4.0 %score.4 = (bf16[45,180,128]{2,1,0:T(8,128)(2,1)S(1)}, f32[768,128]{1,0:T(8,128)S(1)}) custom-call(bf16[45,180,128]{2,1,0:T(8,128)(2,1)S(1)} %bitcast.27, bf16[45,16,128]{2,1,0:T(8,128)(2,1)S(1)} %maximum_maximum_fusion.refs_1_, bf16[45,16,128]{2,1,0:T(8,128)(2,1)S(1)} %concatenate.91.refs_2_, bf16[12,80,128]{2,1,0:T(8,128)(2,1)} %get-tuple-element.27.refs_3_, ...), custom_call_target="tpu_custom_call" | custom-call | flops 377487360 | bytes 1507328 | tf_op jit(solution)/shard_map/score/pallas_call | solution.py:261
  45.6 5.9 %score.5 = (bf16[45,180,128]{2,1,0:T(8,128)(2,1)S(1)}, f32[768,128]{1,0:T(8,128)S(1)}) custom-call(bf16[45,180,128]{2,1,0:T(8,128)(2,1)S(1)} %bitcast.28, bf16[45,16,128]{2,1,0:T(8,128)(2,1)S(1)} %maximum_maximum_fusion.refs_1_, bf16[45,16,128]{2,1,0:T(8,128)(2,1)S(1)} %concatenate.91.refs_2_, ...), custom_call_target="tpu_custom_call", output_to_operand_aliasing={{0}: (8, {})} | custom-call | flops 660602880 | bytes 2637824 | tf_op jit(solution)/shard_map/score/pallas_call | solution.py:261
  51.5 5.7 %score.6 = (bf16[45,180,128]{2,1,0:T(8,128)(2,1)S(1)}, f32[768,128]{1,0:T(8,128)S(1)}) custom-call(bf16[45,180,128]{2,1,0:T(8,128)(2,1)S(1)} %bitcast.29, bf16[45,16,128]{2,1,0:T(8,128)(2,1)S(1)} %maximum_maximum_fusion.refs_1_, bf16[45,16,128]{2,1,0:T(8,128)(2,1)S(1)} %concatenate.91.refs_2_, ...), custom_call_target="tpu_custom_call", output_to_operand_aliasing={{0}: (8, {})} | custom-call | flops 660602880 | bytes 2637824 | tf_op jit(solution)/shard_map/score/pallas_call | solution.py:261
  57.2 4.9 %score.7 = (bf16[45,180,128]{2,1,0:T(8,128)(2,1)S(1)}, f32[768,128]{1,0:T(8,128)}) custom-call(bf16[45,180,128]{2,1,0:T(8,128)(2,1)S(1)} %bitcast.30, bf16[45,16,128]{2,1,0:T(8,128)(2,1)S(1)} %maximum_maximum_fusion.refs_1_, bf16[45,16,128]{2,1,0:T(8,128)(2,1)S(1)} %concatenate.91.refs_2_, ...), custom_call_target="tpu_custom_call", output_to_operand_aliasing={{0}: (10, {})} | custom-call | flops 424673280 | bytes 1695744 | tf_op jit(solution)/shard_map/score/pallas_call | solution.py:261
  62.1 1.3 %copy-done.5 = bf16[45,180,128]{2,1,0:T(8,128)(2,1)} copy-done((bf16[45,180,128]{2,1,0:T(8,128)(2,1)}, bf16[45,180,128]{2,1,0:T(8,128)(2,1)S(1)}, u32[]{:S(2)}) %copy-start.5) | copy-done | bytes 2073624
  63.4 0.1 broadcast_select_fusion.10
  63.5 0.1 collective-permute-start.8
  63.6 3.1 %collective-permute-start.9 = (bf16[45,1,128]{2,1,0:T(2,128)(2,1)S(1)}, bf16[45,1,128]{2,1,0:T(2,128)(2,1)S(1)}, u32[]{:S(2)}, u32[]{:S(2)}) collective-permute-start(bf16[45,1,128]{2,1,0:T(2,128)(2,1)S(1)} %get-tuple-element.38), channel_id=1, source_target_pairs={{32,64},{64,32},{33,65},{65,33},{34,66},{66,34},{35,67},{67,35},{3... | collective-permute-start | bytes 34568 | tf_op jit(solution)/shard_map/ppermute | solution.py:36
  66.7 9.6 %all-to-all-start = ((f32[256,1,384]{2,1,0:T(1,128)}), f32[256,1,384]{2,1,0:T(1,128)S(1)}, u32[]{:S(2)}, u32[]{:S(2)}) async-start(f32[256,1,384]{2,1,0:T(1,128)} %bitcast.10), calls=%async_computation | async-start | bytes 786432 | tf_op jit(solution)/shard_map/all_to_all | solution.py:346
  76.3 0.8 fusion
  77.2 0.9 slice.72
  78.1 0.1 broadcast_select_fusion.8
  78.1 0.1 maximum_maximum_fusion.1.refs_1_
  78.3 14.5 %all-to-all-done = f32[256,1,384]{2,1,0:T(1,128)S(1)} async-done(((f32[256,1,384]{2,1,0:T(1,128)}), f32[256,1,384]{2,1,0:T(1,128)S(1)}, u32[]{:S(2)}, u32[]{:S(2)}) %all-to-all-start) | async-done | bytes 393248 | tf_op jit(solution)/shard_map/all_to_all | solution.py:346
  92.7 0.3 reduce_sum.19
  93.0 1.0 broadcast_in_dim.14
  94.0 7.8 %all-to-all-start.1 = ((f32[256,1,384]{2,1,0:T(1,128)}), f32[256,1,384]{2,1,0:T(1,128)S(1)}, u32[]{:S(2)}, u32[]{:S(2)}) async-start(f32[256,1,384]{2,1,0:T(1,128)} %broadcast_in_dim.14), calls=%async_computation.1 | async-start | bytes 786432 | tf_op jit(solution)/shard_map/all_to_all | solution.py:346
  101.8 0.1 broadcast_select_fusion.2
  101.9 6.9 %collective-permute-start.10 = (bf16[1,256,128]{2,1,0:T(8,128)(2,1)S(1)}, bf16[1,256,128]{2,1,0:T(8,128)(2,1)S(1)}, u32[]{:S(2)}, u32[]{:S(2)}) collective-permute-start(bf16[1,256,128]{2,1,0:T(8,128)(2,1)S(1)} %get-tuple-element.53), channel_id=1, source_target_pairs={{1,2},{3,4},{5,6},{7,8},{9,10},{11,12},{13,14},{15,16},{17,18},{19... | collective-permute-start | bytes 196616 | tf_op jit(solution)/shard_map/ppermute | solution.py:36
  108.9 8.1 %collective-permute-done.10 = bf16[1,256,128]{2,1,0:T(8,128)(2,1)S(1)} collective-permute-done((bf16[1,256,128]{2,1,0:T(8,128)(2,1)S(1)}, bf16[1,256,128]{2,1,0:T(8,128)(2,1)S(1)}, u32[]{:S(2)}, u32[]{:S(2)}) %collective-permute-start.10) | collective-permute-done | bytes 65568 | tf_op jit(solution)/shard_map/ppermute | solution.py:36
  117.1 8.0 %backward.1 = bf16[45,180,128]{2,1,0:T(8,128)(2,1)} custom-call(bf16[45,180,128]{2,1,0:T(8,128)(2,1)S(1)} %copy-done.6, bf16[45,16,128]{2,1,0:T(8,128)(2,1)S(1)} %maximum_maximum_fusion.1.refs_1_, bf16[45,16,128]{2,1,0:T(8,128)(2,1)S(1)} %concatenate.96.refs_2_, bf16[1,256,128]{2,1,0:T(8,128)(2,1)S(1)} %get-tuple-element.49.refs_3_, ...), custom_call_target="tpu_custom_call" | custom-call | flops 3397386240 | bytes 5898240 | tf_op jit(solution)/shard_map/backward/pallas_call | solution.py:325
  125.0 0.5 slice.89
  126.2 1.1 slice_multiply_fusion
  (36 shorter events, 0.3 us)
Async XLA Ops:
  1.6 6.7 %collective-permute-start = (bf16[45,1,128]{2,1,0:T(2,128)(2,1)S(1)}, bf16[45,1,128]{2,1,0:T(2,128)(2,1)S(1)}, u32[]{:S(2)}, u32[]{:S(2)}) collective-permute-start(bf16[45,1,128]{2,1,0:T(2,128)(2,1)S(1)} %get-tuple-element.43), channel_id=1, source_target_pairs={{0,32},{64,96},{32,0},{96,64},{1,33},{65,97},{33,1},{97,65},{2,34}... | collective-permute-start | bytes 34568 | tf_op jit(solution)/shard_map/ppermute | solution.py:35
  2.9 5.7 %collective-permute-start.1 = (bf16[45,1,128]{2,1,0:T(2,128)(2,1)S(1)}, bf16[45,1,128]{2,1,0:T(2,128)(2,1)S(1)}, u32[]{:S(2)}, u32[]{:S(2)}) collective-permute-start(bf16[45,1,128]{2,1,0:T(2,128)(2,1)S(1)} %get-tuple-element.42), channel_id=1, source_target_pairs={{32,64},{64,32},{33,65},{65,33},{34,66},{66,34},{35,67},{67,35},{3... | collective-permute-start | bytes 34568 | tf_op jit(solution)/shard_map/ppermute | solution.py:36
  8.9 1.6 %copy-start = (bf16[1,180,45,128]{3,1,2,0:T(8,128)(2,1)S(1)}, bf16[1,180,45,128]{3,1,2,0:T(8,128)(2,1)}, u32[]{:S(2)}) copy-start(bf16[1,180,45,128]{3,1,2,0:T(8,128)(2,1)} %param.4) | copy-start | bytes 6220804
  10.5 1.5 %copy-start.4 = (bf16[1,180,45,80]{1,3,2,0:T(8,128)(2,1)S(1)}, bf16[1,180,45,80]{1,3,2,0:T(8,128)(2,1)}, u32[]{:S(2)}) copy-start(bf16[1,180,45,80]{1,3,2,0:T(8,128)(2,1)} %param.5) | copy-start | bytes 3888004
  12.0 0.9 copy-start.7
  12.9 11.1 %copy-start.8 = (bf16[3,3,128,80]{2,3,1,0:T(8,128)(2,1)S(1)}, bf16[3,3,128,80]{2,3,1,0:T(8,128)(2,1)}, u32[]{:S(2)}) copy-start(bf16[3,3,128,80]{2,3,1,0:T(8,128)(2,1)} %param.7) | copy-start | bytes 552964
  16.2 23.8 %collective-permute-start.7 = (bf16[12,80,128]{2,1,0:T(8,128)(2,1)}, bf16[12,80,128]{2,1,0:T(8,128)(2,1)}, u32[]{:S(2)}, u32[]{:S(2)}) collective-permute-start(bf16[12,80,128]{2,1,0:T(8,128)(2,1)} %get-tuple-element.27.refs_3_), channel_id=1, source_target_pairs={{0,128},{128,0},{1,129},{129,1},{2,130},{130,2},{3,131},{131,3},{4... | collective-permute-start | bytes 737288 | tf_op jit(solution)/shard_map/ppermute | solution.py:380
  18.0 17.3 %collective-permute-start.2 = (bf16[1,256,128]{2,1,0:T(8,128)(2,1)S(1)}, bf16[1,256,128]{2,1,0:T(8,128)(2,1)S(1)}, u32[]{:S(2)}, u32[]{:S(2)}) collective-permute-start(bf16[1,256,128]{2,1,0:T(8,128)(2,1)S(1)} %get-tuple-element.55), channel_id=1, source_target_pairs={{1,2},{3,4},{5,6},{7,8},{9,10},{11,12},{13,14},{15,16},{17,18},{19... | collective-permute-start | bytes 196616 | tf_op jit(solution)/shard_map/ppermute | solution.py:36
  24.0 11.3 %collective-permute-start.3 = (bf16[1,256,128]{2,1,0:T(8,128)(2,1)S(1)}, bf16[1,256,128]{2,1,0:T(8,128)(2,1)S(1)}, u32[]{:S(2)}, u32[]{:S(2)}) collective-permute-start(bf16[1,256,128]{2,1,0:T(8,128)(2,1)S(1)} %get-tuple-element.54), channel_id=1, source_target_pairs={{0,1},{2,3},{4,5},{6,7},{8,9},{10,11},{12,13},{14,15},{16,17},{18,... | collective-permute-start | bytes 196616 | tf_op jit(solution)/shard_map/ppermute | solution.py:35
  29.0 16.6 %collective-permute-start.6 = (bf16[21,80,128]{2,1,0:T(8,128)(2,1)}, bf16[21,80,128]{2,1,0:T(8,128)(2,1)}, u32[]{:S(2)}, u32[]{:S(2)}) collective-permute-start(bf16[21,80,128]{2,1,0:T(8,128)(2,1)} %get-tuple-element.26.refs_3_), channel_id=1, source_target_pairs={{0,128},{128,0},{1,129},{129,1},{2,130},{130,2},{3,131},{131,3},{4... | collective-permute-start | bytes 1290248 | tf_op jit(solution)/shard_map/ppermute | solution.py:380
  33.4 18.1 %collective-permute-start.5 = (bf16[21,80,128]{2,1,0:T(8,128)(2,1)S(1)}, bf16[21,80,128]{2,1,0:T(8,128)(2,1)}, u32[]{:S(2)}, u32[]{:S(2)}) collective-permute-start(bf16[21,80,128]{2,1,0:T(8,128)(2,1)S(1)} %get-tuple-element.25.refs_3_), channel_id=1, source_target_pairs={{0,128},{128,0},{1,129},{129,1},{2,130},{130,2},{3,131},{131,3},{4... | collective-permute-start | bytes 1290248 | tf_op jit(solution)/shard_map/ppermute | solution.py:380
  35.4 4.7 %copy-start.1 = (bf16[1,180,45,128]{3,1,2,0:T(8,128)(2,1)S(1)}, bf16[1,180,45,128]{3,1,2,0:T(8,128)(2,1)}, u32[]{:S(2)}) copy-start(bf16[1,180,45,128]{3,1,2,0:T(8,128)(2,1)} %param.4) | copy-start | bytes 6220804
  38.4 18.8 %collective-permute-start.4 = (bf16[14,80,128]{2,1,0:T(8,128)(2,1)S(1)}, bf16[14,80,128]{2,1,0:T(8,128)(2,1)}, u32[]{:S(2)}, u32[]{:S(2)}) collective-permute-start(bf16[14,80,128]{2,1,0:T(8,128)(2,1)S(1)} %get-tuple-element.24.refs_3_), channel_id=1, source_target_pairs={{0,128},{128,0},{1,129},{129,1},{2,130},{130,2},{3,131},{131,3},{4... | collective-permute-start | bytes 860168 | tf_op jit(solution)/shard_map/ppermute | solution.py:380
  40.0 1.5 %copy-start.2 = (bf16[180,45,80]{0,2,1:T(8,128)(2,1)S(1)}, bf16[180,45,80]{0,2,1:T(8,128)(2,1)}, u32[]{:S(2)}) copy-start(bf16[180,45,80]{0,2,1:T(8,128)(2,1)} %param.6) | copy-start | bytes 3888004
  41.5 4.0 %copy-start.3 = (bf16[180,45,80]{0,2,1:T(8,128)(2,1)S(1)}, bf16[180,45,80]{0,2,1:T(8,128)(2,1)}, u32[]{:S(2)}) copy-start(bf16[180,45,80]{0,2,1:T(8,128)(2,1)} %param.6) | copy-start | bytes 3888004
  62.1 1.3 %copy-start.5 = (bf16[45,180,128]{2,1,0:T(8,128)(2,1)}, bf16[45,180,128]{2,1,0:T(8,128)(2,1)S(1)}, u32[]{:S(2)}) copy-start(bf16[45,180,128]{2,1,0:T(8,128)(2,1)S(1)} %get-tuple-element.35.refs_0_) | copy-start | bytes 6220804
  63.5 53.6 %copy-start.6 = (bf16[45,180,128]{2,1,0:T(8,128)(2,1)S(1)}, bf16[45,180,128]{2,1,0:T(8,128)(2,1)}, u32[]{:S(2)}) copy-start(bf16[45,180,128]{2,1,0:T(8,128)(2,1)} %copy-done.5) | copy-start | bytes 6220804
  63.5 14.6 %collective-permute-start.8 = (bf16[45,1,128]{2,1,0:T(2,128)(2,1)S(1)}, bf16[45,1,128]{2,1,0:T(2,128)(2,1)S(1)}, u32[]{:S(2)}, u32[]{:S(2)}) collective-permute-start(bf16[45,1,128]{2,1,0:T(2,128)(2,1)S(1)} %get-tuple-element.39), channel_id=1, source_target_pairs={{0,32},{64,96},{32,0},{96,64},{1,33},{65,97},{33,1},{97,65},{2,34}... | collective-permute-start | bytes 34568 | tf_op jit(solution)/shard_map/ppermute | solution.py:35
  63.6 14.5 %collective-permute-start.9 = (bf16[45,1,128]{2,1,0:T(2,128)(2,1)S(1)}, bf16[45,1,128]{2,1,0:T(2,128)(2,1)S(1)}, u32[]{:S(2)}, u32[]{:S(2)}) collective-permute-start(bf16[45,1,128]{2,1,0:T(2,128)(2,1)S(1)} %get-tuple-element.38), channel_id=1, source_target_pairs={{32,64},{64,32},{33,65},{65,33},{34,66},{66,34},{35,67},{67,35},{3... | collective-permute-start | bytes 34568 | tf_op jit(solution)/shard_map/ppermute | solution.py:36
  66.7 26.0 %all-to-all-start = ((f32[256,1,384]{2,1,0:T(1,128)}), f32[256,1,384]{2,1,0:T(1,128)S(1)}, u32[]{:S(2)}, u32[]{:S(2)}) async-start(f32[256,1,384]{2,1,0:T(1,128)} %bitcast.10), calls=%async_computation | async-start | bytes 786432 | tf_op jit(solution)/shard_map/all_to_all | solution.py:346
  94.0 31.0 %all-to-all-start.1 = ((f32[256,1,384]{2,1,0:T(1,128)}), f32[256,1,384]{2,1,0:T(1,128)S(1)}, u32[]{:S(2)}, u32[]{:S(2)}) async-start(f32[256,1,384]{2,1,0:T(1,128)} %broadcast_in_dim.14), calls=%async_computation.1 | async-start | bytes 786432 | tf_op jit(solution)/shard_map/all_to_all | solution.py:346
  101.9 15.1 %collective-permute-start.10 = (bf16[1,256,128]{2,1,0:T(8,128)(2,1)S(1)}, bf16[1,256,128]{2,1,0:T(8,128)(2,1)S(1)}, u32[]{:S(2)}, u32[]{:S(2)}) collective-permute-start(bf16[1,256,128]{2,1,0:T(8,128)(2,1)S(1)} %get-tuple-element.53), channel_id=1, source_target_pairs={{1,2},{3,4},{5,6},{7,8},{9,10},{11,12},{13,14},{15,16},{17,18},{19... | collective-permute-start | bytes 196616 | tf_op jit(solution)/shard_map/ppermute | solution.py:36
  108.8 8.2 %collective-permute-start.11 = (bf16[1,256,128]{2,1,0:T(8,128)(2,1)S(1)}, bf16[1,256,128]{2,1,0:T(8,128)(2,1)S(1)}, u32[]{:S(2)}, u32[]{:S(2)}) collective-permute-start(bf16[1,256,128]{2,1,0:T(8,128)(2,1)S(1)} %get-tuple-element.52), channel_id=1, source_target_pairs={{0,1},{2,3},{4,5},{6,7},{8,9},{10,11},{12,13},{14,15},{16,17},{18,... | collective-permute-start | bytes 196616 | tf_op jit(solution)/shard_map/ppermute | solution.py:35

commit v3 on v2

--- a/solution.py
+++ b/solution.py
@@ -11,10 +11,11 @@
 epsilon = 1e-06
 RING = 256
 LANES = 128
+GRANT = 56 << 20
 TILE = 16
 AXES = ("member", "lat", "lon")
 VMEM = pl.BlockSpec(memory_space=pltpu.VMEM)
-ANY = pl.BlockSpec(memory_space=pl.ANY)
+HBM = pl.BlockSpec(memory_space=pltpu.HBM)
 
 
 def latitude_weights(row_index, total_rows):
@@ -56,29 +57,52 @@
     return swapped(ring(slice(0, 1)), ring(slice(-1, None)), "lon", True)
 
 
-def fill(slab_v, place, field_ref, low_ref, high_ref, column):
-    body = field_ref.shape[1] - field_ref.shape[1] % TILE
-    slab_v[place, :body] = field_ref[column, :body]
-    slab_v[place, body : body + TILE] = low_ref[column]
-    gap = RING - body - 2 * TILE
-    slab_v[place, body + TILE : RING - TILE] = jnp.zeros((gap, slab_v.shape[2]), slab_v.dtype)
-    slab_v[place, RING - TILE :] = high_ref[column]
-
-
-def fill_chunk(slab_v, start, count, wraps, field, edges):
-    inside = count + 1 if wraps else count + 2
-
-    def one(i, carry):
-        fill(slab_v, i, *field, start - 1 + i)
-        return carry
-
-    lax.fori_loop(0, inside, one, 0)
+def slab_copies(slab_v, place, field, column, count):
+    body = field[0].shape[1] - field[0].shape[1] % TILE
+    rows = (pl.ds(0, body), pl.ds(body, TILE), pl.ds(RING - TILE, TILE))
+    span, to = pl.ds(column, count), pl.ds(place, count)
+    sources = (field[0].at[span, rows[0]], field[1].at[span], field[2].at[span])
+    return [(source, slab_v.at[to, where]) for source, where in zip(sources, rows)]
+
+
+def clear_gap(slab_v, places, rows):
+    low = rows - rows % TILE + TILE
+    shape = (places.stop - places.start, RING - TILE - low, slab_v.shape[2])
+    slab_v[places, low : RING - TILE] = jnp.zeros(shape, slab_v.dtype)
+
+
+def chunk_copies(slab_v, start, count, wraps, field, edges):
+    if not wraps:
+        return slab_copies(slab_v, 0, field, start - 1, count + 2)
+    west_ref, east_ref = edges
+    around = [(east_ref, slab_v.at[pl.ds(count + 1, 1)]), (west_ref, slab_v.at[pl.ds(count + 2, 1)])]
+    return (
+        slab_copies(slab_v, 0, field, start - 1, count + 1)
+        + around
+        + slab_copies(slab_v, count + 3, field, 0, 2)
+    )
+
+
+def clear_chunk(slab_v, count, wraps, rows):
     if wraps:
-        west_ref, east_ref = edges
-        slab_v[inside] = east_ref[0]
-        slab_v[inside + 1] = west_ref[0]
-        fill(slab_v, inside + 2, *field, 0)
-        fill(slab_v, inside + 3, *field, 1)
+        clear_gap(slab_v, slice(0, count + 1), rows)
+        clear_gap(slab_v, slice(count + 3, count + 5), rows)
+    else:
+        clear_gap(slab_v, slice(0, count + 2), rows)
+
+
+def column_copies(source, start, count, wraps, target_v):
+    copies = [(source.at[pl.ds(start, count)], target_v.at[pl.ds(0, count)])]
+    if wraps:
+        copies.append((source.at[pl.ds(0, 1)], target_v.at[pl.ds(count, 1)]))
+    return copies
+
+
+def start_all(pairs, sems):
+    copies = [pltpu.make_async_copy(*pair, sems.at[i]) for i, pair in enumerate(pairs)]
+    for copy in copies:
+        copy.start()
+    return copies
 
 
 def window(slab_v, place):
@@ -99,18 +123,30 @@
     if count % 2:
         carry = at(count - 1, 0, carry)
     if wraps:
-        carry = one(count, 0, count + 2, total + count // 2, count % 2, carry)
+        carry = one(count, None, count + 2, total + count // 2, count % 2, carry)
     return carry
 
 
-def write_columns(source_v, out, start, count, wraps, sems):
-    copies = [pltpu.make_async_copy(source_v.at[pl.ds(0, count)], out.at[pl.ds(start, count)], sems.at[0])]
+def write_pair(source_v, out, start, slot, odd, sem):
+    if odd:
+        pltpu.make_async_copy(
+            source_v.at[pl.ds(slot - 1, 2)], out.at[pl.ds(start + slot - 1, 2)], sem
+        ).start()
+
+
+def write_rest(source_v, out, start, count, wraps, sems):
+    pairs = []
+    if count % 2:
+        pairs.append((source_v.at[pl.ds(count - 1, 1)], out.at[pl.ds(start + count - 1, 1)]))
     if wraps:
-        copies.append(
-            pltpu.make_async_copy(source_v.at[pl.ds(count, 1)], out.at[pl.ds(0, 1)], sems.at[1])
-        )
+        pairs.append((source_v.at[pl.ds(count, 1)], out.at[pl.ds(0, 1)]))
+    copies = [pltpu.make_async_copy(*pair, sems.at[1 + i]) for i, pair in enumerate(pairs)]
     for copy in copies:
         copy.start()
+    even = count - count % 2
+    copies.append(
+        pltpu.make_async_copy(source_v.at[pl.ds(0, even)], out.at[pl.ds(start, even)], sems.at[0])
+    )
     for copy in copies:
         copy.wait()
 
@@ -118,13 +154,22 @@
 def forward_kernel(start, count, wraps, n_given, *refs):
     field, present_ref, taps_ref = refs[:3], refs[3], refs[4]
     edges = refs[5:7] if wraps else ()
-    pred_out, packed_out, slab_v, weights_v, pred_v, sems = refs[n_given:]
+    pred_out, packed_out, slab_v, weights_v, taps_v, present_v, pred_v, in_sems, sems = refs[n_given:]
     outputs, rows = present_ref.shape[1:]
+    copies = start_all(
+        [(taps_ref, taps_v)]
+        + chunk_copies(slab_v, start, count, wraps, field, edges)
+        + column_copies(present_ref, start, count, wraps, present_v),
+        in_sems,
+    )
+    clear_chunk(slab_v, count, wraps, rows)
+    copies[0].wait()
     for a in range(3):
         weights_v[a * outputs : (a + 1) * outputs] = jnp.concatenate(
-            [taps_ref[a, b] for b in range(3)], axis=1
-        )
-    fill_chunk(slab_v, start, count, wraps, field, edges)
+            [taps_v[a, b] for b in range(3)], axis=1
+        )
+    for copy in copies[1:]:
+        copy.wait()
     half = LANES // 2
 
     def one(slot, column, place, block, odd, carry):
@@ -139,18 +184,20 @@
             + y[outputs : 2 * outputs]
             + pltpu.roll(y[2 * outputs :], RING - 1, 1)
         )
-        head = increment[:, :LANES] + present_ref[column, :, :LANES].astype(jnp.float32)
-        tail = increment[:, LANES:rows] + present_ref[column, :, LANES:].astype(jnp.float32)
+        head = increment[:, :LANES] + present_v[slot, :, :LANES].astype(jnp.float32)
+        tail = increment[:, LANES:rows] + present_v[slot, :, LANES:].astype(jnp.float32)
         head = head.astype(jnp.bfloat16)
         tail = tail.astype(jnp.bfloat16)
         pred_v[slot, :, :LANES] = head
         pred_v[slot, :, LANES:] = tail
         packed_out[slot] = head
         packed_out[block, :, odd * half : odd * half + rows - LANES] = tail
+        if column is not None:
+            write_pair(pred_v, pred_out, start, slot, odd, sems.at[0])
         return carry
 
     each_column(start, count, wraps, one, 0)
-    write_columns(pred_v, pred_out, start, count, wraps, sems)
+    write_rest(pred_v, pred_out, start, count, wraps, sems)
 
 
 def forward(start, count, wraps, field, present, taps, edges, pred):
@@ -158,12 +205,11 @@
     inputs = taps.shape[3]
     total = count + wraps
     given = [*field, present, taps] + (list(edges) if wraps else [])
-    in_specs = [VMEM] * len(given)
     aliases = {}
     if pred is not None:
         aliases = {len(given): 0}
         given.append(pred)
-        in_specs.append(ANY)
+    in_specs = [HBM] * len(given)
     return pl.pallas_call(
         functools.partial(forward_kernel, start, count, wraps, len(given)),
         out_shape=(
@@ -171,15 +217,18 @@
             jax.ShapeDtypeStruct((total + (total + 1) // 2, outputs, LANES), jnp.bfloat16),
         ),
         in_specs=in_specs,
-        out_specs=(ANY, VMEM),
+        out_specs=(HBM, VMEM),
         scratch_shapes=[
             pltpu.VMEM((count + 2 + 3 * wraps, RING, inputs), jnp.bfloat16),
             pltpu.VMEM((3 * outputs, 3 * inputs), jnp.bfloat16),
+            pltpu.VMEM(taps.shape, jnp.bfloat16),
             pltpu.VMEM((total, outputs, rows), jnp.bfloat16),
-            pltpu.SemaphoreType.DMA((2,)),
+            pltpu.VMEM((total, outputs, rows), jnp.bfloat16),
+            pltpu.SemaphoreType.DMA((11,)),
+            pltpu.SemaphoreType.DMA((3,)),
         ],
         input_output_aliases=aliases,
-        compiler_params=pltpu.CompilerParams(vmem_limit_bytes=24 << 20),
+        compiler_params=pltpu.CompilerParams(vmem_limit_bytes=GRANT),
         cost_estimate=pl.CostEstimate(
             flops=2 * total * 9 * inputs * outputs * RING,
             bytes_accessed=total * RING * (inputs + 3 * outputs) * 2,
@@ -193,14 +242,23 @@
     field, own_ref, other_ref, target_ref, weight_ref = refs[:3], *refs[3:7]
     edges = refs[7 : 7 + n_edges]
     sums_ref = refs[7 + n_edges] if adds else None
-    turned_out, sums_out, slab_v, cot_v, acc_v, turned_v, sems = refs[n_given:]
+    turned_out, sums_out, slab_v, own_v, other_v, target_v, cot_v, acc_v, turned_v = refs[n_given:-2]
+    in_sems, sems = refs[-2:]
+    copies = start_all(
+        [(own_ref, own_v), (other_ref, other_v)]
+        + chunk_copies(slab_v, start, count, wraps, field, edges)
+        + column_copies(target_ref, start, count, wraps, target_v),
+        in_sems,
+    )
     outputs, rows = target_ref.shape[1:]
     inputs = slab_v.shape[2]
     half = LANES // 2
     weight = weight_ref[...]
     cot_v[...] = jnp.zeros_like(cot_v)
     acc_v[...] = jnp.zeros_like(acc_v)
-    fill_chunk(slab_v, start, count, wraps, field, edges)
+    clear_chunk(slab_v, count, wraps, rows)
+    for copy in copies:
+        copy.wait()
 
     def one(slot, column, place, block, odd, score):
         lanes_of_tail = slice(odd * half, odd * half + rows - LANES)
@@ -208,12 +266,12 @@
         for side in range(2):
             lanes = slice(0, LANES) if side == 0 else slice(LANES, rows)
             if side == 0:
-                value, partner = (ref[slot].astype(jnp.float32) for ref in (own_ref, other_ref))
+                value, partner = (ref[slot].astype(jnp.float32) for ref in (own_v, other_v))
             else:
                 value, partner = (
-                    ref[block, :, lanes_of_tail].astype(jnp.float32) for ref in (own_ref, other_ref)
+                    ref[block, :, lanes_of_tail].astype(jnp.float32) for ref in (own_v, other_v)
                 )
-            misfit = value - target_ref[column, :, lanes].astype(jnp.float32)
+            misfit = value - target_v[slot, :, lanes].astype(jnp.float32)
             spread = value - partner
             error2 = jnp.sum(misfit * misfit, axis=0, keepdims=True) + epsilon
             pair2 = jnp.sum(spread * spread, axis=0, keepdims=True) + epsilon
@@ -224,6 +282,8 @@
             halves.append(scale * (error2 * error_inv - 0.5 * (pair2 * pair_inv)))
         cot = cot_v[odd]
         turned_v[slot] = cot.T[:rows].astype(jnp.bfloat16)
+        if column is not None:
+            write_pair(turned_v, turned_out, start, slot, odd, sems.at[0])
         cot = cot[:outputs]
         shifted = jnp.concatenate([pltpu.roll(cot, RING - 1, 1), cot, pltpu.roll(cot, 1, 1)], axis=0)
         acc_v[...] += jnp.dot(
@@ -242,7 +302,7 @@
     total = sum(jnp.sum(part, axis=1, keepdims=True) for part in score)
     filler = jnp.broadcast_to(total, (sums_out.shape[0] - 9 * outputs, inputs))
     sums_out[spare] = filler + sums_ref[spare] if adds else filler
-    write_columns(turned_v, turned_out, start, count, wraps, sems)
+    write_rest(turned_v, turned_out, start, count, wraps, sems)
 
 
 def scored(start, count, wraps, field, own, other, target, weight, edges, carried, sum_rows):
@@ -251,13 +311,13 @@
     total = count + wraps
     edges = list(edges) if wraps else []
     given = [*field, own, other, target, weight, *edges]
-    in_specs = [VMEM] * len(given)
+    in_specs = [HBM] * 6 + [VMEM] + [HBM] * len(edges)
     aliases = {}
     if carried is not None:
         turned, sums = carried
         aliases = {len(given) + 1: 0}
         given += [sums, turned]
-        in_specs += [VMEM, ANY]
+        in_specs += [VMEM, HBM]
     return pl.pallas_call(
         functools.partial(
             score_kernel, start, count, wraps, len(edges), carried is not None, len(given)
@@ -267,16 +327,20 @@
             jax.ShapeDtypeStruct((sum_rows, inputs), jnp.float32),
         ),
         in_specs=in_specs,
-        out_specs=(ANY, VMEM),
+        out_specs=(HBM, VMEM),
         scratch_shapes=[
             pltpu.VMEM((count + 2 + 3 * wraps, RING, inputs), jnp.bfloat16),
+            pltpu.VMEM(own.shape, jnp.bfloat16),
+            pltpu.VMEM(own.shape, jnp.bfloat16),
+            pltpu.VMEM((total, outputs, rows), jnp.bfloat16),
             pltpu.VMEM((2, LANES, RING), jnp.float32),
             pltpu.VMEM((3 * outputs, 3 * inputs), jnp.float32),
             pltpu.VMEM((total, rows, LANES), jnp.bfloat16),
-            pltpu.SemaphoreType.DMA((2,)),
+            pltpu.SemaphoreType.DMA((12,)),
+            pltpu.SemaphoreType.DMA((3,)),
         ],
         input_output_aliases=aliases,
-        compiler_params=pltpu.CompilerParams(vmem_limit_bytes=24 << 20),
+        compiler_params=pltpu.CompilerParams(vmem_limit_bytes=GRANT),
         cost_estimate=pl.CostEstimate(
             flops=2 * total * 9 * inputs * outputs * RING,
             bytes_accessed=total * RING * (inputs + 3 * outputs) * 2,
@@ -287,7 +351,7 @@
 
 
 def backward_kernel(block, *refs):
-    field, west_ref, east_ref, taps_ref, slope_out, slab_v, weights_v = refs[:3], *refs[3:]
+    field, west_ref, east_ref, taps_ref, slope_out, slab_v, weights_v, sems = refs[:3], *refs[3:]
     rows, inputs = slope_out.shape[1:]
     columns = field[0].shape[0]
     outputs = taps_ref.shape[2]
@@ -295,18 +359,19 @@
 
     @pl.when(pl.program_id(0) == 0)
     def _():
+        copies = start_all(
+            slab_copies(slab_v, 1, field, 0, columns)
+            + [(west_ref, slab_v.at[pl.ds(0, 1)]), (east_ref, slab_v.at[pl.ds(columns + 1, 1)])],
+            sems,
+        )
+        clear_gap(slab_v, slice(1, columns + 1), rows)
         spare = jnp.zeros((LANES - outputs, inputs), weights_v.dtype)
         for b in range(3):
             row = [jnp.concatenate([taps_ref[2 - a, 2 - b], spare], axis=0) for a in range(3)]
             weights_v[b * LANES : (b + 1) * LANES] = jnp.concatenate(row, axis=1)
 
-        def one(i, carry):
-            fill(slab_v, i + 1, *field, i)
-            return carry
-
-        lax.fori_loop(0, columns, one, 0)
-        slab_v[0] = west_ref[0]
-        slab_v[columns + 1] = east_ref[0]
+        for copy in copies:
+            copy.wait()
 
     for j in range(block):
         z = jnp.dot(window(slab_v, base + j), weights_v[...], preferred_element_type=jnp.float32)
@@ -326,13 +391,14 @@
         functools.partial(backward_kernel, block),
         grid=(columns // block,),
         out_shape=jax.ShapeDtypeStruct((columns, rows, inputs), jnp.bfloat16),
-        in_specs=[VMEM] * 6,
+        in_specs=[HBM] * 5 + [VMEM],
         out_specs=pl.BlockSpec((block, rows, inputs), lambda i: (i, 0, 0)),
         scratch_shapes=[
             pltpu.VMEM((columns + 2, RING, LANES), jnp.bfloat16),
             pltpu.VMEM((3 * LANES, 3 * inputs), jnp.bfloat16),
+            pltpu.SemaphoreType.DMA((5,)),
         ],
-        compiler_params=pltpu.CompilerParams(vmem_limit_bytes=24 << 20),
+        compiler_params=pltpu.CompilerParams(vmem_limit_bytes=GRANT),
         cost_estimate=pl.CostEstimate(
             flops=2 * columns * 9 * inputs * LANES * RING,
             bytes_accessed=columns * RING * (inputs + LANES) * 2,
@@ -388,11 +454,12 @@
             start, count, wraps, field, own, other, truth, weight, edges, carried, sum_rows
         )
     turned, sums = carried
-    share = jnp.sum(exchange(sums.reshape(devices, width)), axis=0, keepdims=True)
+    parts = exchange(sums.reshape(devices, width))
+    field = (turned, *lat_edges(turned))
+    share = jnp.sum(parts, axis=0, keepdims=True)
+    share, edges = lax.optimization_barrier((share, lon_edges(*field)))
     whole = exchange(jnp.broadcast_to(share, (devices, width))).reshape(sum_rows, inputs)
-
-    field = (turned, *lat_edges(turned))
-    slope = backward(field, lon_edges(*field), taps)
+    slope = backward(field, edges, taps)
     objective_mean = whole[9 * outputs, 0] / (total_rows * total_cols)
     summed = whole[: 9 * outputs] / math.sqrt(2.0 * total_rows * total_cols)
     filter_weights_slope = jnp.transpose(summed.reshape(3, 3, outputs, inputs), (0, 1, 3, 2))

time: 129 us -> 140 us (1.085)
  the two profiles are of different devices: /device:TPU:4 before, /device:TPU:1 now
where the time goes in v3:
time: 140 us
  Pallas kernels  60.8 us (43%)
  starting transfers between devices  42.7 us (30%)
  waiting for transfers between devices  16 us (11%)
  local copies, waits for them, and re-layouts  10.1 us (7%)
  other arithmetic  6.55 us (5%)
  between operations  3.37 us (2%)
    pallas_call x4, Pallas kernels, scored(): pl.pallas_call(functools.partial(score_kernel, start, count, wraps, len(e...  29 us
    pallas_call x4, Pallas kernels, forward(): pl.pallas_call(functools.partial(forward_kernel, start, count, wraps, len...  21.7 us
    all_to_all x2, starting transfers between devices, exchange(): return lax.all_to_all(blocks, AXES, 0, 0, tiled=True)  16.9 us
    all_to_all x2, waiting for transfers between devices, exchange(): return lax.all_to_all(blocks, AXES, 0, 0, tiled=True)  15.1 us
    ppermute x4, starting transfers between devices, swapped(): near = lax.ppermute(jnp.where(even, last, first), axis, both[0])  14.3 us
    pallas_call x1, Pallas kernels, backward(): pl.pallas_call(functools.partial(backward_kernel, block), grid=(columns /...  10.1 us
    ppermute x4, starting transfers between devices, swapped(): far = lax.ppermute(jnp.where(even, first, last), axis, both[1])  8.36 us
    unnamed x12, local copies, waits for them, and re-layouts  3.57 us
  transfers between devices with their start and end apart: 14, of which 3 were waited for; matrix products, arithmetic and copies ran while one was open for 5% of the time, Pallas kernels for 36%

profile of v3, /device:TPU:1, one launch (start us, length us, event | category | flops | bytes accessed | tf_op | source)
XLA Modules:
  0.0 139.6 jit_solution(12747774628421129511)
XLA Ops:
  0.6 1.0 broadcast_select_fusion.14
  1.6 2.1 %collective-permute-start = (bf16[45,1,128]{2,1,0:T(2,128)(2,1)S(1)}, bf16[45,1,128]{2,1,0:T(2,128)(2,1)S(1)}, u32[]{:S(2)}, u32[]{:S(2)}) collective-permute-start(bf16[45,1,128]{2,1,0:T(2,128)(2,1)S(1)} %get-tuple-element.49), channel_id=1, source_target_pairs={{0,32},{64,96},{32,0},{96,64},{1,33},{65,97},{33,1},{97,65},{2,34}... | collective-permute-start | bytes 34568 | tf_op jit(solution)/shard_map/ppermute | solution.py:36
  3.8 0.7 collective-permute-start.1
  4.4 0.8 fusion.1
  5.2 0.9 slice.82
  6.4 0.7 concatenate.91.refs_2_
  7.3 0.7 copy-done
  7.9 4.5 %forward.4 = (bf16[45,80,180]{2,1,0:T(8,128)(2,1)}, bf16[12,80,128]{2,1,0:T(8,128)(2,1)}) custom-call(bf16[45,180,128]{2,1,0:T(8,128)(2,1)} %bitcast.23, bf16[45,16,128]{2,1,0:T(8,128)(2,1)} %copy-done, bf16[45,16,128]{2,1,0:T(8,128)(2,1)} %concatenate.91.refs_2_, bf16[45,80,180]{2,1,0:T(8,128)(2,1)} %bitcast.35, bf16[3,3,80,128]{3,2,1,0:T(8,128)(2,1)} %bitcast.40), custom_call_target="tpu_custom_call" | custom-call | flops 377487360 | bytes 1507328 | tf_op jit(solution)/shard_map/forward/pallas_call | solution.py:213
  12.4 1.4 collective-permute-start.7
  13.9 3.8 %collective-permute-start.2 = (bf16[1,256,128]{2,1,0:T(8,128)(2,1)S(1)}, bf16[1,256,128]{2,1,0:T(8,128)(2,1)S(1)}, u32[]{:S(2)}, u32[]{:S(2)}) collective-permute-start(bf16[1,256,128]{2,1,0:T(8,128)(2,1)S(1)} %get-tuple-element.61), channel_id=1, source_target_pairs={{1,2},{3,4},{5,6},{7,8},{9,10},{11,12},{13,14},{15,16},{17,18},{19... | collective-permute-start | bytes 196616 | tf_op jit(solution)/shard_map/ppermute | solution.py:37
  17.8 4.6 %collective-permute-start.3 = (bf16[1,256,128]{2,1,0:T(8,128)(2,1)S(1)}, bf16[1,256,128]{2,1,0:T(8,128)(2,1)S(1)}, u32[]{:S(2)}, u32[]{:S(2)}) collective-permute-start(bf16[1,256,128]{2,1,0:T(8,128)(2,1)S(1)} %get-tuple-element.60), channel_id=1, source_target_pairs={{0,1},{2,3},{4,5},{6,7},{8,9},{10,11},{12,13},{14,15},{16,17},{18,... | collective-permute-start | bytes 196616 | tf_op jit(solution)/shard_map/ppermute | solution.py:36
  22.3 6.1 %forward.5 = (bf16[45,80,180]{2,1,0:T(8,128)(2,1)}, bf16[21,80,128]{2,1,0:T(8,128)(2,1)}) custom-call(bf16[45,180,128]{2,1,0:T(8,128)(2,1)} %bitcast.24, bf16[45,16,128]{2,1,0:T(8,128)(2,1)} %copy-done, bf16[45,16,128]{2,1,0:T(8,128)(2,1)} %concatenate.91.refs_2_, bf16[45,80,180]{2,1,0:T(8,128)(2,1)} %bitcast.36, ...), custom_call_target="tpu_custom_call", output_to_operand_aliasing={{0}: (5, {})} | custom-call | flops 660602880 | bytes 2637824 | tf_op jit(solution)/shard_map/forward/pallas_call | solution.py:213
  28.6 6.2 %forward.6 = (bf16[45,80,180]{2,1,0:T(8,128)(2,1)}, bf16[21,80,128]{2,1,0:T(8,128)(2,1)}) custom-call(bf16[45,180,128]{2,1,0:T(8,128)(2,1)} %bitcast.25, bf16[45,16,128]{2,1,0:T(8,128)(2,1)} %copy-done, bf16[45,16,128]{2,1,0:T(8,128)(2,1)} %concatenate.91.refs_2_, bf16[45,80,180]{2,1,0:T(8,128)(2,1)} %bitcast.37, ...), custom_call_target="tpu_custom_call", output_to_operand_aliasing={{0}: (5, {})} | custom-call | flops 660602880 | bytes 2637824 | tf_op jit(solution)/shard_map/forward/pallas_call | solution.py:213
  34.7 1.5 %collective-permute-start.5 = (bf16[21,80,128]{2,1,0:T(8,128)(2,1)}, bf16[21,80,128]{2,1,0:T(8,128)(2,1)S(1)}, u32[]{:S(2)}, u32[]{:S(2)}) collective-permute-start(bf16[21,80,128]{2,1,0:T(8,128)(2,1)} %get-tuple-element.28.refs_3_), channel_id=1, source_target_pairs={{0,128},{128,0},{1,129},{129,1},{2,130},{130,2},{3,131},{131,3},{4... | collective-permute-start | bytes 1290248 | tf_op jit(solution)/shard_map/ppermute | solution.py:446
  36.3 0.7 broadcast_select_fusion.4
  36.9 4.9 %forward.7 = (bf16[45,80,180]{2,1,0:T(8,128)(2,1)}, bf16[14,80,128]{2,1,0:T(8,128)(2,1)}) custom-call(bf16[45,180,128]{2,1,0:T(8,128)(2,1)} %bitcast.26, bf16[45,16,128]{2,1,0:T(8,128)(2,1)} %copy-done, bf16[45,16,128]{2,1,0:T(8,128)(2,1)} %concatenate.91.refs_2_, bf16[45,80,180]{2,1,0:T(8,128)(2,1)} %bitcast.38, ...), custom_call_target="tpu_custom_call", output_to_operand_aliasing={{0}: (7, {})} | custom-call | flops 424673280 | bytes 1695744 | tf_op jit(solution)/shard_map/forward/pallas_call | solution.py:213
  41.9 0.1 collective-permute-start.4
  42.0 0.6 cosine_reduce_fusion
  43.3 0.6 cosine_divide_fusion.refs_6_
  43.9 0.7 copy-done.4
  44.6 5.9 %score.4 = (bf16[45,180,128]{2,1,0:T(8,128)(2,1)}, f32[768,128]{1,0:T(8,128)}) custom-call(bf16[45,180,128]{2,1,0:T(8,128)(2,1)} %bitcast.27, bf16[45,16,128]{2,1,0:T(8,128)(2,1)} %copy-done, bf16[45,16,128]{2,1,0:T(8,128)(2,1)} %concatenate.91.refs_2_, bf16[12,80,128]{2,1,0:T(8,128)(2,1)} %get-tuple-element.30.refs_3_, bf16[12,80,128]{2,1,0:T(8,128)(2,1)} %copy-done.4, ...), custom_call_target="tpu_custom_call" | custom-call | flops 377487360 | bytes 1507328 | tf_op jit(solution)/shard_map/score/pallas_call | solution.py:321
  50.5 0.8 copy-done.2
  51.3 8.3 %score.5 = (bf16[45,180,128]{2,1,0:T(8,128)(2,1)}, f32[768,128]{1,0:T(8,128)}) custom-call(bf16[45,180,128]{2,1,0:T(8,128)(2,1)} %bitcast.28, bf16[45,16,128]{2,1,0:T(8,128)(2,1)} %copy-done, bf16[45,16,128]{2,1,0:T(8,128)(2,1)} %concatenate.91.refs_2_, bf16[21,80,128]{2,1,0:T(8,128)(2,1)} %get-tuple-element.29.refs_3_, ...), custom_call_target="tpu_custom_call", output_to_operand_aliasing={{0}: (8, {})} | custom-call | flops 660602880 | bytes 2637824 | tf_op jit(solution)/shard_map/score/pallas_call | solution.py:321
  59.6 0.7 copy-done.1
  60.3 8.3 %score.6 = (bf16[45,180,128]{2,1,0:T(8,128)(2,1)}, f32[768,128]{1,0:T(8,128)}) custom-call(bf16[45,180,128]{2,1,0:T(8,128)(2,1)} %bitcast.29, bf16[45,16,128]{2,1,0:T(8,128)(2,1)} %copy-done, bf16[45,16,128]{2,1,0:T(8,128)(2,1)} %concatenate.91.refs_2_, bf16[21,80,128]{2,1,0:T(8,128)(2,1)} %get-tuple-element.28.refs_3_, ...), custom_call_target="tpu_custom_call", output_to_operand_aliasing={{0}: (8, {})} | custom-call | flops 660602880 | bytes 2637824 | tf_op jit(solution)/shard_map/score/pallas_call | solution.py:321
  68.7 0.7 copy-done.3
  69.4 6.5 %score.7 = (bf16[45,180,128]{2,1,0:T(8,128)(2,1)}, f32[768,128]{1,0:T(8,128)}) custom-call(bf16[45,180,128]{2,1,0:T(8,128)(2,1)} %bitcast.30, bf16[45,16,128]{2,1,0:T(8,128)(2,1)} %copy-done, bf16[45,16,128]{2,1,0:T(8,128)(2,1)} %concatenate.91.refs_2_, bf16[14,80,128]{2,1,0:T(8,128)(2,1)} %get-tuple-element.27.refs_3_, ...), custom_call_target="tpu_custom_call", output_to_operand_aliasing={{0}: (10, {})} | custom-call | flops 424673280 | bytes 1695744 | tf_op jit(solution)/shard_map/score/pallas_call | solution.py:321
  75.9 1.0 broadcast_select_fusion.11
  76.9 3.5 %collective-permute-start.8 = (bf16[45,1,128]{2,1,0:T(2,128)(2,1)S(1)}, bf16[45,1,128]{2,1,0:T(2,128)(2,1)S(1)}, u32[]{:S(2)}, u32[]{:S(2)}) collective-permute-start(bf16[45,1,128]{2,1,0:T(2,128)(2,1)S(1)} %get-tuple-element.44), channel_id=1, source_target_pairs={{0,32},{64,96},{32,0},{96,64},{1,33},{65,97},{33,1},{97,65},{2,34}... | collective-permute-start | bytes 34568 | tf_op jit(solution)/shard_map/ppermute | solution.py:36
  80.4 0.7 collective-permute-start.9
  81.0 0.8 fusion
  81.8 0.9 slice.72
  82.8 10.5 %all-to-all-start = ((f32[256,1,384]{2,1,0:T(1,128)}), f32[256,1,384]{2,1,0:T(1,128)S(1)}, u32[]{:S(2)}, u32[]{:S(2)}) async-start(f32[256,1,384]{2,1,0:T(1,128)} %bitcast.46), calls=%async_computation | async-start | bytes 786432 | tf_op jit(solution)/shard_map/all_to_all | solution.py:412
  93.3 0.1 maximum_maximum_fusion.1.refs_1_
  93.4 0.1 broadcast_select_fusion.2
  93.6 3.2 %collective-permute-start.10 = (bf16[1,256,128]{2,1,0:T(8,128)(2,1)S(1)}, bf16[1,256,128]{2,1,0:T(8,128)(2,1)S(1)}, u32[]{:S(2)}, u32[]{:S(2)}) collective-permute-start(bf16[1,256,128]{2,1,0:T(8,128)(2,1)S(1)} %get-tuple-element.59), channel_id=1, source_target_pairs={{1,2},{3,4},{5,6},{7,8},{9,10},{11,12},{13,14},{15,16},{17,18},{19... | collective-permute-start | bytes 196616 | tf_op jit(solution)/shard_map/ppermute | solution.py:37
  96.8 4.1 %collective-permute-start.11 = (bf16[1,256,128]{2,1,0:T(8,128)(2,1)S(1)}, bf16[1,256,128]{2,1,0:T(8,128)(2,1)S(1)}, u32[]{:S(2)}, u32[]{:S(2)}) collective-permute-start(bf16[1,256,128]{2,1,0:T(8,128)(2,1)S(1)} %get-tuple-element.58), channel_id=1, source_target_pairs={{0,1},{2,3},{4,5},{6,7},{8,9},{10,11},{12,13},{14,15},{16,17},{18,... | collective-permute-start | bytes 196616 | tf_op jit(solution)/shard_map/ppermute | solution.py:36
  100.9 0.9 collective-permute-done.11
  101.8 0.7 broadcast_select_fusion
  102.5 8.5 %all-to-all-done = f32[256,1,384]{2,1,0:T(1,128)S(1)} async-done(((f32[256,1,384]{2,1,0:T(1,128)}), f32[256,1,384]{2,1,0:T(1,128)S(1)}, u32[]{:S(2)}, u32[]{:S(2)}) %all-to-all-start) | async-done | bytes 393248 | tf_op jit(solution)/shard_map/all_to_all | solution.py:412
  111.0 0.3 reduce_sum.19
  111.3 1.0 broadcast_in_dim.17
  112.3 6.4 %all-to-all-start.1 = ((f32[256,1,384]{2,1,0:T(1,128)}), f32[256,1,384]{2,1,0:T(1,128)S(1)}, u32[]{:S(2)}, u32[]{:S(2)}) async-start(f32[256,1,384]{2,1,0:T(1,128)} %broadcast_in_dim.17), calls=%async_computation.1 | async-start | bytes 786432 | tf_op jit(solution)/shard_map/all_to_all | solution.py:412
  118.7 0.7 concatenate.96.refs_2_
  119.5 10.1 %backward.1 = bf16[45,180,128]{2,1,0:T(8,128)(2,1)} custom-call(bf16[45,180,128]{2,1,0:T(8,128)(2,1)} %get-tuple-element.38.refs_0_, bf16[45,16,128]{2,1,0:T(8,128)(2,1)} %copy-done.5, bf16[45,16,128]{2,1,0:T(8,128)(2,1)} %concatenate.96.refs_2_, bf16[1,256,128]{2,1,0:T(8,128)(2,1)} %get-tuple-element.40.refs_3_, ...), custom_call_target="tpu_custom_call" | custom-call | flops 3397386240 | bytes 5898240 | tf_op jit(solution)/shard_map/backward/pallas_call | solution.py:390
  129.6 6.6 %all-to-all-done.1 = f32[256,1,384]{2,1,0:T(1,128)S(1)} async-done(((f32[256,1,384]{2,1,0:T(1,128)}), f32[256,1,384]{2,1,0:T(1,128)S(1)}, u32[]{:S(2)}, u32[]{:S(2)}) %all-to-all-start.1) | async-done | bytes 393248 | tf_op jit(solution)/shard_map/all_to_all | solution.py:412
  136.2 0.5 slice.91
  137.3 1.1 slice_multiply_fusion
  (32 shorter events, 0.7 us)
Async XLA Ops:
  1.6 4.7 %collective-permute-start = (bf16[45,1,128]{2,1,0:T(2,128)(2,1)S(1)}, bf16[45,1,128]{2,1,0:T(2,128)(2,1)S(1)}, u32[]{:S(2)}, u32[]{:S(2)}) collective-permute-start(bf16[45,1,128]{2,1,0:T(2,128)(2,1)S(1)} %get-tuple-element.49), channel_id=1, source_target_pairs={{0,32},{64,96},{32,0},{96,64},{1,33},{65,97},{33,1},{97,65},{2,34}... | collective-permute-start | bytes 34568 | tf_op jit(solution)/shard_map/ppermute | solution.py:36
  3.8 2.6 %collective-permute-start.1 = (bf16[45,1,128]{2,1,0:T(2,128)(2,1)S(1)}, bf16[45,1,128]{2,1,0:T(2,128)(2,1)S(1)}, u32[]{:S(2)}, u32[]{:S(2)}) collective-permute-start(bf16[45,1,128]{2,1,0:T(2,128)(2,1)S(1)} %get-tuple-element.48), channel_id=1, source_target_pairs={{32,64},{64,32},{33,65},{65,33},{34,66},{66,34},{35,67},{67,35},{3... | collective-permute-start | bytes 34568 | tf_op jit(solution)/shard_map/ppermute | solution.py:37
  7.2 0.7 copy-start
  12.4 31.5 %collective-permute-start.7 = (bf16[12,80,128]{2,1,0:T(8,128)(2,1)}, bf16[12,80,128]{2,1,0:T(8,128)(2,1)S(1)}, u32[]{:S(2)}, u32[]{:S(2)}) collective-permute-start(bf16[12,80,128]{2,1,0:T(8,128)(2,1)} %get-tuple-element.30.refs_3_), channel_id=1, source_target_pairs={{0,128},{128,0},{1,129},{129,1},{2,130},{130,2},{3,131},{131,3},{4... | collective-permute-start | bytes 737288 | tf_op jit(solution)/shard_map/ppermute | solution.py:446
  13.9 22.4 %collective-permute-start.2 = (bf16[1,256,128]{2,1,0:T(8,128)(2,1)S(1)}, bf16[1,256,128]{2,1,0:T(8,128)(2,1)S(1)}, u32[]{:S(2)}, u32[]{:S(2)}) collective-permute-start(bf16[1,256,128]{2,1,0:T(8,128)(2,1)S(1)} %get-tuple-element.61), channel_id=1, source_target_pairs={{1,2},{3,4},{5,6},{7,8},{9,10},{11,12},{13,14},{15,16},{17,18},{19... | collective-permute-start | bytes 196616 | tf_op jit(solution)/shard_map/ppermute | solution.py:37
  17.8 18.5 %collective-permute-start.3 = (bf16[1,256,128]{2,1,0:T(8,128)(2,1)S(1)}, bf16[1,256,128]{2,1,0:T(8,128)(2,1)S(1)}, u32[]{:S(2)}, u32[]{:S(2)}) collective-permute-start(bf16[1,256,128]{2,1,0:T(8,128)(2,1)S(1)} %get-tuple-element.60), channel_id=1, source_target_pairs={{0,1},{2,3},{4,5},{6,7},{8,9},{10,11},{12,13},{14,15},{16,17},{18,... | collective-permute-start | bytes 196616 | tf_op jit(solution)/shard_map/ppermute | solution.py:36
  28.5 22.1 %collective-permute-start.6 = (bf16[21,80,128]{2,1,0:T(8,128)(2,1)}, bf16[21,80,128]{2,1,0:T(8,128)(2,1)S(1)}, u32[]{:S(2)}, u32[]{:S(2)}) collective-permute-start(bf16[21,80,128]{2,1,0:T(8,128)(2,1)} %get-tuple-element.29.refs_3_), channel_id=1, source_target_pairs={{0,128},{128,0},{1,129},{129,1},{2,130},{130,2},{3,131},{131,3},{4... | collective-permute-start | bytes 1290248 | tf_op jit(solution)/shard_map/ppermute | solution.py:446
  34.7 24.9 %collective-permute-start.5 = (bf16[21,80,128]{2,1,0:T(8,128)(2,1)}, bf16[21,80,128]{2,1,0:T(8,128)(2,1)S(1)}, u32[]{:S(2)}, u32[]{:S(2)}) collective-permute-start(bf16[21,80,128]{2,1,0:T(8,128)(2,1)} %get-tuple-element.28.refs_3_), channel_id=1, source_target_pairs={{0,128},{128,0},{1,129},{129,1},{2,130},{130,2},{3,131},{131,3},{4... | collective-permute-start | bytes 1290248 | tf_op jit(solution)/shard_map/ppermute | solution.py:446
  41.9 26.8 %collective-permute-start.4 = (bf16[14,80,128]{2,1,0:T(8,128)(2,1)}, bf16[14,80,128]{2,1,0:T(8,128)(2,1)S(1)}, u32[]{:S(2)}, u32[]{:S(2)}) collective-permute-start(bf16[14,80,128]{2,1,0:T(8,128)(2,1)} %get-tuple-element.27.refs_3_), channel_id=1, source_target_pairs={{0,128},{128,0},{1,129},{129,1},{2,130},{130,2},{3,131},{131,3},{4... | collective-permute-start | bytes 860168 | tf_op jit(solution)/shard_map/ppermute | solution.py:446
  43.9 0.7 copy-start.4
  50.5 0.8 copy-start.2
  59.6 0.8 copy-start.1
  68.6 0.7 copy-start.3
  76.9 16.3 %collective-permute-start.8 = (bf16[45,1,128]{2,1,0:T(2,128)(2,1)S(1)}, bf16[45,1,128]{2,1,0:T(2,128)(2,1)S(1)}, u32[]{:S(2)}, u32[]{:S(2)}) collective-permute-start(bf16[45,1,128]{2,1,0:T(2,128)(2,1)S(1)} %get-tuple-element.44), channel_id=1, source_target_pairs={{0,32},{64,96},{32,0},{96,64},{1,33},{65,97},{33,1},{97,65},{2,34}... | collective-permute-start | bytes 34568 | tf_op jit(solution)/shard_map/ppermute | solution.py:36
  80.4 12.9 %collective-permute-start.9 = (bf16[45,1,128]{2,1,0:T(2,128)(2,1)S(1)}, bf16[45,1,128]{2,1,0:T(2,128)(2,1)S(1)}, u32[]{:S(2)}, u32[]{:S(2)}) collective-permute-start(bf16[45,1,128]{2,1,0:T(2,128)(2,1)S(1)} %get-tuple-element.45), channel_id=1, source_target_pairs={{32,64},{64,32},{33,65},{65,33},{34,66},{66,34},{35,67},{67,35},{3... | collective-permute-start | bytes 34568 | tf_op jit(solution)/shard_map/ppermute | solution.py:37
  82.8 28.2 %all-to-all-start = ((f32[256,1,384]{2,1,0:T(1,128)}), f32[256,1,384]{2,1,0:T(1,128)S(1)}, u32[]{:S(2)}, u32[]{:S(2)}) async-start(f32[256,1,384]{2,1,0:T(1,128)} %bitcast.46), calls=%async_computation | async-start | bytes 786432 | tf_op jit(solution)/shard_map/all_to_all | solution.py:412
  93.4 26.0 %copy-start.5 = (bf16[45,16,128]{2,1,0:T(8,128)(2,1)}, bf16[45,16,128]{2,1,0:T(8,128)(2,1)S(1)}, u32[]{:S(2)}) copy-start(bf16[45,16,128]{2,1,0:T(8,128)(2,1)S(1)} %maximum_maximum_fusion.1.refs_1_) | copy-start | bytes 552964
  93.6 7.4 %collective-permute-start.10 = (bf16[1,256,128]{2,1,0:T(8,128)(2,1)S(1)}, bf16[1,256,128]{2,1,0:T(8,128)(2,1)S(1)}, u32[]{:S(2)}, u32[]{:S(2)}) collective-permute-start(bf16[1,256,128]{2,1,0:T(8,128)(2,1)S(1)} %get-tuple-element.59), channel_id=1, source_target_pairs={{1,2},{3,4},{5,6},{7,8},{9,10},{11,12},{13,14},{15,16},{17,18},{19... | collective-permute-start | bytes 196616 | tf_op jit(solution)/shard_map/ppermute | solution.py:37
  96.8 5.0 %collective-permute-start.11 = (bf16[1,256,128]{2,1,0:T(8,128)(2,1)S(1)}, bf16[1,256,128]{2,1,0:T(8,128)(2,1)S(1)}, u32[]{:S(2)}, u32[]{:S(2)}) collective-permute-start(bf16[1,256,128]{2,1,0:T(8,128)(2,1)S(1)} %get-tuple-element.58), channel_id=1, source_target_pairs={{0,1},{2,3},{4,5},{6,7},{8,9},{10,11},{12,13},{14,15},{16,17},{18,... | collective-permute-start | bytes 196616 | tf_op jit(solution)/shard_map/ppermute | solution.py:36
  112.3 23.9 %all-to-all-start.1 = ((f32[256,1,384]{2,1,0:T(1,128)}), f32[256,1,384]{2,1,0:T(1,128)S(1)}, u32[]{:S(2)}, u32[]{:S(2)}) async-start(f32[256,1,384]{2,1,0:T(1,128)} %broadcast_in_dim.17), calls=%async_computation.1 | async-start | bytes 786432 | tf_op jit(solution)/shard_map/all_to_all | solution.py:412

commit v4 on v2

--- a/solution.py
+++ b/solution.py
@@ -56,61 +56,43 @@
     return swapped(ring(slice(0, 1)), ring(slice(-1, None)), "lon", True)
 
 
-def fill(slab_v, place, field_ref, low_ref, high_ref, column):
+def ring_column(field, edges, column):
+    field_ref, low_ref, high_ref = field
+    if isinstance(column, int) and not 0 <= column < field_ref.shape[0]:
+        return edges[0 if column < 0 else 1][0]
     body = field_ref.shape[1] - field_ref.shape[1] % TILE
-    slab_v[place, :body] = field_ref[column, :body]
-    slab_v[place, body : body + TILE] = low_ref[column]
-    gap = RING - body - 2 * TILE
-    slab_v[place, body + TILE : RING - TILE] = jnp.zeros((gap, slab_v.shape[2]), slab_v.dtype)
-    slab_v[place, RING - TILE :] = high_ref[column]
-
-
-def fill_chunk(slab_v, start, count, wraps, field, edges):
-    inside = count + 1 if wraps else count + 2
-
-    def one(i, carry):
-        fill(slab_v, i, *field, start - 1 + i)
+    gap = jnp.zeros((RING - body - 2 * TILE, field_ref.shape[2]), field_ref.dtype)
+    return jnp.concatenate([field_ref[column, :body], low_ref[column], gap, high_ref[column]], axis=0)
+
+
+def window(field, edges, column):
+    return jnp.concatenate([ring_column(field, edges, column + b - 1) for b in range(3)], axis=1)
+
+
+def each_column(start, count, wraps, one, source_v, out, sems):
+    total = count + wraps
+    pairs = (count - wraps) // 2
+
+    def pair(t, carry):
+        one(2 * t, start + 2 * t, total + t, 0)
+        one(2 * t + 1, start + 2 * t + 1, total + t, 1)
+        to = out.at[pl.ds(start + 2 * t, 2)]
+        pltpu.make_async_copy(source_v.at[pl.ds(2 * t, 2)], to, sems.at[0]).start()
         return carry
 
-    lax.fori_loop(0, inside, one, 0)
-    if wraps:
-        west_ref, east_ref = edges
-        slab_v[inside] = east_ref[0]
-        slab_v[inside + 1] = west_ref[0]
-        fill(slab_v, inside + 2, *field, 0)
-        fill(slab_v, inside + 3, *field, 1)
-
-
-def window(slab_v, place):
-    return jnp.concatenate([slab_v[place + b] for b in range(3)], axis=1)
-
-
-def each_column(start, count, wraps, one, carry):
-    total = count + wraps
-
-    def at(slot, odd, carry):
-        return one(slot, start + slot, slot, total + slot // 2, odd, carry)
-
-    def pair(t, carry):
-        carry = one(2 * t, start + 2 * t, 2 * t, total + t, 0, carry)
-        return one(2 * t + 1, start + 2 * t + 1, 2 * t + 1, total + t, 1, carry)
-
-    carry = lax.fori_loop(0, count // 2, pair, carry)
-    if count % 2:
-        carry = at(count - 1, 0, carry)
-    if wraps:
-        carry = one(count, 0, count + 2, total + count // 2, count % 2, carry)
-    return carry
-
-
-def write_columns(source_v, out, start, count, wraps, sems):
-    copies = [pltpu.make_async_copy(source_v.at[pl.ds(0, count)], out.at[pl.ds(start, count)], sems.at[0])]
-    if wraps:
-        copies.append(
-            pltpu.make_async_copy(source_v.at[pl.ds(count, 1)], out.at[pl.ds(0, 1)], sems.at[1])
-        )
-    for copy in copies:
+    lax.fori_loop(0, pairs, pair, 0)
+    copies = []
+    if pairs:
+        span = pl.ds(0, 2 * pairs), pl.ds(start, 2 * pairs)
+        copies.append(pltpu.make_async_copy(source_v.at[span[0]], out.at[span[1]], sems.at[0]))
+    for slot in range(2 * pairs, total):
+        column = start + slot if slot < count else 0
+        one(slot, column, total + slot // 2, slot % 2)
+        copy = pltpu.make_async_copy(
+            source_v.at[pl.ds(slot, 1)], out.at[pl.ds(column, 1)], sems.at[1 + slot - 2 * pairs]
+        )
         copy.start()
+        copies.append(copy)
     for copy in copies:
         copy.wait()
 
@@ -118,19 +100,18 @@
 def forward_kernel(start, count, wraps, n_given, *refs):
     field, present_ref, taps_ref = refs[:3], refs[3], refs[4]
     edges = refs[5:7] if wraps else ()
-    pred_out, packed_out, slab_v, weights_v, pred_v, sems = refs[n_given:]
+    pred_out, packed_out, weights_v, pred_v, sems = refs[n_given:]
     outputs, rows = present_ref.shape[1:]
     for a in range(3):
         weights_v[a * outputs : (a + 1) * outputs] = jnp.concatenate(
             [taps_ref[a, b] for b in range(3)], axis=1
         )
-    fill_chunk(slab_v, start, count, wraps, field, edges)
     half = LANES // 2
 
-    def one(slot, column, place, block, odd, carry):
+    def one(slot, column, block, odd):
         y = lax.dot_general(
             weights_v[...],
-            window(slab_v, place),
+            window(field, edges, column),
             (((1,), (1,)), ((), ())),
             preferred_element_type=jnp.float32,
         )
@@ -147,10 +128,8 @@
         pred_v[slot, :, LANES:] = tail
         packed_out[slot] = head
         packed_out[block, :, odd * half : odd * half + rows - LANES] = tail
-        return carry
-
-    each_column(start, count, wraps, one, 0)
-    write_columns(pred_v, pred_out, start, count, wraps, sems)
+
+    each_column(start, count, wraps, one, pred_v, pred_out, sems)
 
 
 def forward(start, count, wraps, field, present, taps, edges, pred):
@@ -173,10 +152,9 @@
         in_specs=in_specs,
         out_specs=(ANY, VMEM),
         scratch_shapes=[
-            pltpu.VMEM((count + 2 + 3 * wraps, RING, inputs), jnp.bfloat16),
             pltpu.VMEM((3 * outputs, 3 * inputs), jnp.bfloat16),
             pltpu.VMEM((total, outputs, rows), jnp.bfloat16),
-            pltpu.SemaphoreType.DMA((2,)),
+            pltpu.SemaphoreType.DMA((4,)),
         ],
         input_output_aliases=aliases,
         compiler_params=pltpu.CompilerParams(vmem_limit_bytes=24 << 20),
@@ -193,18 +171,17 @@
     field, own_ref, other_ref, target_ref, weight_ref = refs[:3], *refs[3:7]
     edges = refs[7 : 7 + n_edges]
     sums_ref = refs[7 + n_edges] if adds else None
-    turned_out, sums_out, slab_v, cot_v, acc_v, turned_v, sems = refs[n_given:]
+    turned_out, sums_out, cot_v, acc_v, score_v, turned_v, sems = refs[n_given:]
     outputs, rows = target_ref.shape[1:]
-    inputs = slab_v.shape[2]
+    inputs = field[0].shape[2]
     half = LANES // 2
     weight = weight_ref[...]
     cot_v[...] = jnp.zeros_like(cot_v)
     acc_v[...] = jnp.zeros_like(acc_v)
-    fill_chunk(slab_v, start, count, wraps, field, edges)
-
-    def one(slot, column, place, block, odd, score):
+    score_v[...] = jnp.zeros_like(score_v)
+
+    def one(slot, column, block, odd):
         lanes_of_tail = slice(odd * half, odd * half + rows - LANES)
-        halves = []
         for side in range(2):
             lanes = slice(0, LANES) if side == 0 else slice(LANES, rows)
             if side == 0:
@@ -221,28 +198,25 @@
             pair_inv = lax.rsqrt(pair2)
             scale = 0.5 * weight[:, lanes]
             cot_v[odd, :outputs, lanes] = misfit * (scale * error_inv) - spread * (scale * pair_inv)
-            halves.append(scale * (error2 * error_inv - 0.5 * (pair2 * pair_inv)))
+            score_v[:, lanes] += scale * (error2 * error_inv - 0.5 * (pair2 * pair_inv))
         cot = cot_v[odd]
         turned_v[slot] = cot.T[:rows].astype(jnp.bfloat16)
         cot = cot[:outputs]
         shifted = jnp.concatenate([pltpu.roll(cot, RING - 1, 1), cot, pltpu.roll(cot, 1, 1)], axis=0)
         acc_v[...] += jnp.dot(
-            shifted.astype(jnp.bfloat16), window(slab_v, place), preferred_element_type=jnp.float32
-        )
-        return tuple(s + h for s, h in zip(score, halves))
-
-    score = (jnp.zeros((1, LANES), jnp.float32), jnp.zeros((1, rows - LANES), jnp.float32))
-    score = each_column(start, count, wraps, one, score)
+            shifted.astype(jnp.bfloat16), window(field, edges, column), preferred_element_type=jnp.float32
+        )
+
+    each_column(start, count, wraps, one, turned_v, turned_out, sems)
     for a in range(3):
         for b in range(3):
             block = acc_v[a * outputs : (a + 1) * outputs, b * inputs : (b + 1) * inputs]
             place = slice((3 * a + b) * outputs, (3 * a + b + 1) * outputs)
             sums_out[place] = block + sums_ref[place] if adds else block
     spare = slice(9 * outputs, sums_out.shape[0])
-    total = sum(jnp.sum(part, axis=1, keepdims=True) for part in score)
+    total = jnp.sum(score_v[...], axis=1, keepdims=True)
     filler = jnp.broadcast_to(total, (sums_out.shape[0] - 9 * outputs, inputs))
     sums_out[spare] = filler + sums_ref[spare] if adds else filler
-    write_columns(turned_v, turned_out, start, count, wraps, sems)
 
 
 def scored(start, count, wraps, field, own, other, target, weight, edges, carried, sum_rows):
@@ -269,11 +243,11 @@
         in_specs=in_specs,
         out_specs=(ANY, VMEM),
         scratch_shapes=[
-            pltpu.VMEM((count + 2 + 3 * wraps, RING, inputs), jnp.bfloat16),
             pltpu.VMEM((2, LANES, RING), jnp.float32),
             pltpu.VMEM((3 * outputs, 3 * inputs), jnp.float32),
+            pltpu.VMEM((1, RING), jnp.float32),
             pltpu.VMEM((total, rows, LANES), jnp.bfloat16),
-            pltpu.SemaphoreType.DMA((2,)),
+            pltpu.SemaphoreType.DMA((4,)),
         ],
         input_output_aliases=aliases,
         compiler_params=pltpu.CompilerParams(vmem_limit_bytes=24 << 20),
@@ -287,7 +261,7 @@
 
 
 def backward_kernel(block, *refs):
-    field, west_ref, east_ref, taps_ref, slope_out, slab_v, weights_v = refs[:3], *refs[3:]
+    field, west_ref, east_ref, taps_ref, slope_out, weights_v = refs[:3], *refs[3:]
     rows, inputs = slope_out.shape[1:]
     columns = field[0].shape[0]
     outputs = taps_ref.shape[2]
@@ -300,16 +274,20 @@
             row = [jnp.concatenate([taps_ref[2 - a, 2 - b], spare], axis=0) for a in range(3)]
             weights_v[b * LANES : (b + 1) * LANES] = jnp.concatenate(row, axis=1)
 
-        def one(i, carry):
-            fill(slab_v, i + 1, *field, i)
-            return carry
-
-        lax.fori_loop(0, columns, one, 0)
-        slab_v[0] = west_ref[0]
-        slab_v[columns + 1] = east_ref[0]
-
+    def halo_column(j):
+        at = base + j
+        inner = ring_column(field, (), jnp.clip(at, 0, columns - 1))
+        if j == -1:
+            return jnp.where(at < 0, west_ref[0], inner)
+        return jnp.where(at == columns, east_ref[0], inner) if j == block else inner
+
+    ring = [halo_column(j) for j in range(-1, block + 1)]
     for j in range(block):
-        z = jnp.dot(window(slab_v, base + j), weights_v[...], preferred_element_type=jnp.float32)
+        z = jnp.dot(
+            jnp.concatenate(ring[j : j + 3], axis=1),
+            weights_v[...],
+            preferred_element_type=jnp.float32,
+        )
         slope = (
             pltpu.roll(z[:, :inputs], 1, 0)
             + z[:, inputs : 2 * inputs]
@@ -329,7 +307,6 @@
         in_specs=[VMEM] * 6,
         out_specs=pl.BlockSpec((block, rows, inputs), lambda i: (i, 0, 0)),
         scratch_shapes=[
-            pltpu.VMEM((columns + 2, RING, LANES), jnp.bfloat16),
             pltpu.VMEM((3 * LANES, 3 * inputs), jnp.bfloat16),
         ],
         compiler_params=pltpu.CompilerParams(vmem_limit_bytes=24 << 20),
@@ -389,10 +366,10 @@
         )
     turned, sums = carried
     share = jnp.sum(exchange(sums.reshape(devices, width)), axis=0, keepdims=True)
+    field = (turned, *lat_edges(turned))
+    share, edges = lax.optimization_barrier((share, lon_edges(*field)))
     whole = exchange(jnp.broadcast_to(share, (devices, width))).reshape(sum_rows, inputs)
-
-    field = (turned, *lat_edges(turned))
-    slope = backward(field, lon_edges(*field), taps)
+    slope = backward(field, edges, taps)
     objective_mean = whole[9 * outputs, 0] / (total_rows * total_cols)
     summed = whole[: 9 * outputs] / math.sqrt(2.0 * total_rows * total_cols)
     filter_weights_slope = jnp.transpose(summed.reshape(3, 3, outputs, inputs), (0, 1, 3, 2))

time: 129 us -> 125 us (0.969)
  the two profiles are of different devices: /device:TPU:4 before, /device:TPU:1 now
where the time goes in v4:
time: 125 us; the launch traced here: 124 us
  Pallas kernels  44.4 us (36%)
  starting transfers between devices  42.7 us (34%)
  waiting for transfers between devices  19.6 us (16%)
  local copies, waits for them, and re-layouts  10.3 us (8%)
  other arithmetic  3.74 us (3%)
  between operations  3.45 us (3%)
    pallas_call x4, Pallas kernels, scored(): pl.pallas_call(functools.partial(score_kernel, start, count, wraps, len(e...  22.3 us
    all_to_all x2, waiting for transfers between devices, exchange(): return lax.all_to_all(blocks, AXES, 0, 0, tiled=True)  18.7 us
    all_to_all x2, starting transfers between devices, exchange(): return lax.all_to_all(blocks, AXES, 0, 0, tiled=True)  16.9 us
    pallas_call x4, Pallas kernels, forward(): pl.pallas_call(functools.partial(forward_kernel, start, count, wraps, len...  14.3 us
    ppermute x4, starting transfers between devices, swapped(): near = lax.ppermute(jnp.where(even, last, first), axis, both[0])  14.3 us
    ppermute x4, starting transfers between devices, swapped(): far = lax.ppermute(jnp.where(even, first, last), axis, both[1])  8.36 us
    pallas_call x1, Pallas kernels, backward(): pl.pallas_call(functools.partial(backward_kernel, block), grid=(columns /...  7.75 us
    unnamed x18, local copies, waits for them, and re-layouts  6.85 us
  transfers between devices with their start and end apart: 14, of which 3 were waited for; matrix products, arithmetic and copies ran while one was open for 2% of the time, Pallas kernels for 29%

profile of v4, /device:TPU:1, one launch (start us, length us, event | category | flops | bytes accessed | tf_op | source)
XLA Modules:
  0.0 124.2 jit_solution(2648732134695949204)
XLA Ops:
  0.6 1.0 broadcast_select_fusion.14
  1.6 2.1 %collective-permute-start = (bf16[45,1,128]{2,1,0:T(2,128)(2,1)S(1)}, bf16[45,1,128]{2,1,0:T(2,128)(2,1)S(1)}, u32[]{:S(2)}, u32[]{:S(2)}) collective-permute-start(bf16[45,1,128]{2,1,0:T(2,128)(2,1)S(1)} %get-tuple-element.49), channel_id=1, source_target_pairs={{0,32},{64,96},{32,0},{96,64},{1,33},{65,97},{33,1},{97,65},{2,34}... | collective-permute-start | bytes 34568 | tf_op jit(solution)/shard_map/ppermute | solution.py:35
  3.8 0.7 collective-permute-start.1
  4.4 0.8 fusion.1
  5.2 0.9 slice.82
  6.2 0.1 pad.23.clone
  6.3 0.1 pad.19.clone
  6.5 0.1 maximum_maximum_fusion.refs_1_
  6.6 1.6 %copy-done = bf16[1,180,45,128]{3,1,2,0:T(8,128)(2,1)S(1)} copy-done((bf16[1,180,45,128]{3,1,2,0:T(8,128)(2,1)S(1)}, bf16[1,180,45,128]{3,1,2,0:T(8,128)(2,1)}, u32[]{:S(2)}) %copy-start) | copy-done | bytes 2073624
  8.2 1.5 %copy-done.4 = bf16[1,180,45,80]{1,3,2,0:T(8,128)(2,1)S(1)} copy-done((bf16[1,180,45,80]{1,3,2,0:T(8,128)(2,1)S(1)}, bf16[1,180,45,80]{1,3,2,0:T(8,128)(2,1)}, u32[]{:S(2)}) %copy-start.4) | copy-done | bytes 1296024
  9.7 0.9 copy-done.7
  10.6 3.2 %forward.4 = (bf16[45,80,180]{2,1,0:T(8,128)(2,1)}, bf16[12,80,128]{2,1,0:T(8,128)(2,1)}) custom-call(bf16[45,180,128]{2,1,0:T(8,128)(2,1)S(1)} %bitcast.23, bf16[45,16,128]{2,1,0:T(8,128)(2,1)S(1)} %maximum_maximum_fusion.refs_1_, bf16[45,16,128]{2,1,0:T(8,128)(2,1)S(1)} %concatenate.91.refs_2_, bf16[45,80,180]{2,1,0:T(8,128)(2,1)S(1)} %bitcast.35, ...), custom_call_target="tpu_custom_call" | custom-call | flops 377487360 | bytes 1507328 | tf_op jit(solution)/shard_map/forward/pallas_call | solution.py:146
  13.8 1.4 %collective-permute-start.7 = (bf16[12,80,128]{2,1,0:T(8,128)(2,1)}, bf16[12,80,128]{2,1,0:T(8,128)(2,1)}, u32[]{:S(2)}, u32[]{:S(2)}) collective-permute-start(bf16[12,80,128]{2,1,0:T(8,128)(2,1)} %get-tuple-element.30.refs_3_), channel_id=1, source_target_pairs={{0,128},{128,0},{1,129},{129,1},{2,130},{130,2},{3,131},{131,3},{4... | collective-permute-start | bytes 737288 | tf_op jit(solution)/shard_map/ppermute | solution.py:357
  15.2 0.1 broadcast_select_fusion.6
  15.3 3.8 %collective-permute-start.2 = (bf16[1,256,128]{2,1,0:T(8,128)(2,1)S(1)}, bf16[1,256,128]{2,1,0:T(8,128)(2,1)S(1)}, u32[]{:S(2)}, u32[]{:S(2)}) collective-permute-start(bf16[1,256,128]{2,1,0:T(8,128)(2,1)S(1)} %get-tuple-element.61), channel_id=1, source_target_pairs={{1,2},{3,4},{5,6},{7,8},{9,10},{11,12},{13,14},{15,16},{17,18},{19... | collective-permute-start | bytes 196616 | tf_op jit(solution)/shard_map/ppermute | solution.py:36
  19.1 4.6 %collective-permute-start.3 = (bf16[1,256,128]{2,1,0:T(8,128)(2,1)S(1)}, bf16[1,256,128]{2,1,0:T(8,128)(2,1)S(1)}, u32[]{:S(2)}, u32[]{:S(2)}) collective-permute-start(bf16[1,256,128]{2,1,0:T(8,128)(2,1)S(1)} %get-tuple-element.60), channel_id=1, source_target_pairs={{0,1},{2,3},{4,5},{6,7},{8,9},{10,11},{12,13},{14,15},{16,17},{18,... | collective-permute-start | bytes 196616 | tf_op jit(solution)/shard_map/ppermute | solution.py:35
  23.7 3.9 %forward.5 = (bf16[45,80,180]{2,1,0:T(8,128)(2,1)}, bf16[21,80,128]{2,1,0:T(8,128)(2,1)S(1)}) custom-call(bf16[45,180,128]{2,1,0:T(8,128)(2,1)S(1)} %bitcast.24, bf16[45,16,128]{2,1,0:T(8,128)(2,1)S(1)} %maximum_maximum_fusion.refs_1_, bf16[45,16,128]{2,1,0:T(8,128)(2,1)S(1)} %concatenate.91.refs_2_, ...), custom_call_target="tpu_custom_call", output_to_operand_aliasing={{0}: (5, {})} | custom-call | flops 660602880 | bytes 2637824 | tf_op jit(solution)/shard_map/forward/pallas_call | solution.py:146
  27.6 0.1 collective-permute-start.6
  27.7 3.9 %forward.6 = (bf16[45,80,180]{2,1,0:T(8,128)(2,1)}, bf16[21,80,128]{2,1,0:T(8,128)(2,1)S(1)}) custom-call(bf16[45,180,128]{2,1,0:T(8,128)(2,1)S(1)} %bitcast.25, bf16[45,16,128]{2,1,0:T(8,128)(2,1)S(1)} %maximum_maximum_fusion.refs_1_, bf16[45,16,128]{2,1,0:T(8,128)(2,1)S(1)} %concatenate.91.refs_2_, ...), custom_call_target="tpu_custom_call", output_to_operand_aliasing={{0}: (5, {})} | custom-call | flops 660602880 | bytes 2637824 | tf_op jit(solution)/shard_map/forward/pallas_call | solution.py:146
  31.7 1.5 %collective-permute-start.5 = (bf16[21,80,128]{2,1,0:T(8,128)(2,1)S(1)}, bf16[21,80,128]{2,1,0:T(8,128)(2,1)}, u32[]{:S(2)}, u32[]{:S(2)}) collective-permute-start(bf16[21,80,128]{2,1,0:T(8,128)(2,1)S(1)} %get-tuple-element.28.refs_3_), channel_id=1, source_target_pairs={{0,128},{128,0},{1,129},{129,1},{2,130},{130,2},{3,131},{131,3},{4... | collective-permute-start | bytes 1290248 | tf_op jit(solution)/shard_map/ppermute | solution.py:357
  33.2 3.3 %forward.7 = (bf16[45,80,180]{2,1,0:T(8,128)(2,1)}, bf16[14,80,128]{2,1,0:T(8,128)(2,1)}) custom-call(bf16[45,180,128]{2,1,0:T(8,128)(2,1)S(1)} %bitcast.26, bf16[45,16,128]{2,1,0:T(8,128)(2,1)S(1)} %maximum_maximum_fusion.refs_1_, bf16[45,16,128]{2,1,0:T(8,128)(2,1)S(1)} %concatenate.91.refs_2_, ...), custom_call_target="tpu_custom_call", output_to_operand_aliasing={{0}: (7, {})} | custom-call | flops 424673280 | bytes 1695744 | tf_op jit(solution)/shard_map/forward/pallas_call | solution.py:146
  36.5 0.1 collective-permute-start.4
  36.6 0.6 cosine_reduce_fusion
  37.9 0.1 cosine_divide_fusion.refs_6_
  38.0 1.5 %copy-done.2 = bf16[180,45,80]{0,2,1:T(8,128)(2,1)S(1)} copy-done((bf16[180,45,80]{0,2,1:T(8,128)(2,1)S(1)}, bf16[180,45,80]{0,2,1:T(8,128)(2,1)}, u32[]{:S(2)}) %copy-start.2) | copy-done | bytes 1296024
  39.5 4.3 %score.4 = (bf16[45,180,128]{2,1,0:T(8,128)(2,1)S(1)}, f32[768,128]{1,0:T(8,128)S(1)}) custom-call(bf16[45,180,128]{2,1,0:T(8,128)(2,1)S(1)} %bitcast.27, bf16[45,16,128]{2,1,0:T(8,128)(2,1)S(1)} %maximum_maximum_fusion.refs_1_, bf16[45,16,128]{2,1,0:T(8,128)(2,1)S(1)} %concatenate.91.refs_2_, bf16[12,80,128]{2,1,0:T(8,128)(2,1)} %get-tuple-element.30.refs_3_, ...), custom_call_target="tpu_custom_call" | custom-call | flops 377487360 | bytes 1507328 | tf_op jit(solution)/shard_map/score/pallas_call | solution.py:235
  43.8 6.3 %score.5 = (bf16[45,180,128]{2,1,0:T(8,128)(2,1)S(1)}, f32[768,128]{1,0:T(8,128)S(1)}) custom-call(bf16[45,180,128]{2,1,0:T(8,128)(2,1)S(1)} %bitcast.28, bf16[45,16,128]{2,1,0:T(8,128)(2,1)S(1)} %maximum_maximum_fusion.refs_1_, bf16[45,16,128]{2,1,0:T(8,128)(2,1)S(1)} %concatenate.91.refs_2_, ...), custom_call_target="tpu_custom_call", output_to_operand_aliasing={{0}: (8, {})} | custom-call | flops 660602880 | bytes 2637824 | tf_op jit(solution)/shard_map/score/pallas_call | solution.py:235
  50.1 6.3 %score.6 = (bf16[45,180,128]{2,1,0:T(8,128)(2,1)S(1)}, f32[768,128]{1,0:T(8,128)S(1)}) custom-call(bf16[45,180,128]{2,1,0:T(8,128)(2,1)S(1)} %bitcast.29, bf16[45,16,128]{2,1,0:T(8,128)(2,1)S(1)} %maximum_maximum_fusion.refs_1_, bf16[45,16,128]{2,1,0:T(8,128)(2,1)S(1)} %concatenate.91.refs_2_, ...), custom_call_target="tpu_custom_call", output_to_operand_aliasing={{0}: (8, {})} | custom-call | flops 660602880 | bytes 2637824 | tf_op jit(solution)/shard_map/score/pallas_call | solution.py:235
  56.4 5.5 %score.7 = (bf16[45,180,128]{2,1,0:T(8,128)(2,1)S(1)}, f32[768,128]{1,0:T(8,128)}) custom-call(bf16[45,180,128]{2,1,0:T(8,128)(2,1)S(1)} %bitcast.30, bf16[45,16,128]{2,1,0:T(8,128)(2,1)S(1)} %maximum_maximum_fusion.refs_1_, bf16[45,16,128]{2,1,0:T(8,128)(2,1)S(1)} %concatenate.91.refs_2_, ...), custom_call_target="tpu_custom_call", output_to_operand_aliasing={{0}: (10, {})} | custom-call | flops 424673280 | bytes 1695744 | tf_op jit(solution)/shard_map/score/pallas_call | solution.py:235
  61.9 0.1 broadcast_select_fusion.11
  62.0 3.5 %collective-permute-start.8 = (bf16[45,1,128]{2,1,0:T(2,128)(2,1)S(1)}, bf16[45,1,128]{2,1,0:T(2,128)(2,1)S(1)}, u32[]{:S(2)}, u32[]{:S(2)}) collective-permute-start(bf16[45,1,128]{2,1,0:T(2,128)(2,1)S(1)} %get-tuple-element.44), channel_id=1, source_target_pairs={{0,32},{64,96},{32,0},{96,64},{1,33},{65,97},{33,1},{97,65},{2,34}... | collective-permute-start | bytes 34568 | tf_op jit(solution)/shard_map/ppermute | solution.py:35
  65.5 0.7 collective-permute-start.9
  66.2 1.3 %copy-done.5 = bf16[45,180,128]{2,1,0:T(8,128)(2,1)} copy-done((bf16[45,180,128]{2,1,0:T(8,128)(2,1)}, bf16[45,180,128]{2,1,0:T(8,128)(2,1)S(1)}, u32[]{:S(2)}) %copy-start.5) | copy-done | bytes 2073624
  67.5 10.5 %all-to-all-start = ((f32[256,1,384]{2,1,0:T(1,128)}), f32[256,1,384]{2,1,0:T(1,128)S(1)}, u32[]{:S(2)}, u32[]{:S(2)}) async-start(f32[256,1,384]{2,1,0:T(1,128)} %bitcast.10), calls=%async_computation | async-start | bytes 786432 | tf_op jit(solution)/shard_map/all_to_all | solution.py:323
  78.0 0.1 broadcast_select_fusion.9
  78.0 0.1 maximum_maximum_fusion.1.refs_1_
  78.2 0.1 broadcast_select_fusion.2
  78.3 3.2 %collective-permute-start.10 = (bf16[1,256,128]{2,1,0:T(8,128)(2,1)S(1)}, bf16[1,256,128]{2,1,0:T(8,128)(2,1)S(1)}, u32[]{:S(2)}, u32[]{:S(2)}) collective-permute-start(bf16[1,256,128]{2,1,0:T(8,128)(2,1)S(1)} %get-tuple-element.59), channel_id=1, source_target_pairs={{1,2},{3,4},{5,6},{7,8},{9,10},{11,12},{13,14},{15,16},{17,18},{19... | collective-permute-start | bytes 196616 | tf_op jit(solution)/shard_map/ppermute | solution.py:36
  81.5 4.1 %collective-permute-start.11 = (bf16[1,256,128]{2,1,0:T(8,128)(2,1)S(1)}, bf16[1,256,128]{2,1,0:T(8,128)(2,1)S(1)}, u32[]{:S(2)}, u32[]{:S(2)}) collective-permute-start(bf16[1,256,128]{2,1,0:T(8,128)(2,1)S(1)} %get-tuple-element.58), channel_id=1, source_target_pairs={{0,1},{2,3},{4,5},{6,7},{8,9},{10,11},{12,13},{14,15},{16,17},{18,... | collective-permute-start | bytes 196616 | tf_op jit(solution)/shard_map/ppermute | solution.py:35
  85.6 0.9 collective-permute-done.11
  86.5 9.2 %all-to-all-done = f32[256,1,384]{2,1,0:T(1,128)S(1)} async-done(((f32[256,1,384]{2,1,0:T(1,128)}), f32[256,1,384]{2,1,0:T(1,128)S(1)}, u32[]{:S(2)}, u32[]{:S(2)}) %all-to-all-start) | async-done | bytes 393248 | tf_op jit(solution)/shard_map/all_to_all | solution.py:323
  95.7 0.3 reduce_sum.19
  96.0 1.0 broadcast_in_dim.17
  97.0 6.4 %all-to-all-start.1 = ((f32[256,1,384]{2,1,0:T(1,128)}), f32[256,1,384]{2,1,0:T(1,128)S(1)}, u32[]{:S(2)}, u32[]{:S(2)}) async-start(f32[256,1,384]{2,1,0:T(1,128)} %broadcast_in_dim.17), calls=%async_computation.1 | async-start | bytes 786432 | tf_op jit(solution)/shard_map/all_to_all | solution.py:323
  103.5 7.7 %backward.1 = bf16[45,180,128]{2,1,0:T(8,128)(2,1)} custom-call(bf16[45,180,128]{2,1,0:T(8,128)(2,1)S(1)} %copy-done.6, bf16[45,16,128]{2,1,0:T(8,128)(2,1)S(1)} %maximum_maximum_fusion.1.refs_1_, bf16[45,16,128]{2,1,0:T(8,128)(2,1)S(1)} %concatenate.96.refs_2_, bf16[1,256,128]{2,1,0:T(8,128)(2,1)S(1)} %get-tuple-element.40.refs_3_, ...), custom_call_target="tpu_custom_call" | custom-call | flops 3397386240 | bytes 5898240 | tf_op jit(solution)/shard_map/backward/pallas_call | solution.py:303
  111.3 9.6 %all-to-all-done.1 = f32[256,1,384]{2,1,0:T(1,128)S(1)} async-done(((f32[256,1,384]{2,1,0:T(1,128)}), f32[256,1,384]{2,1,0:T(1,128)S(1)}, u32[]{:S(2)}, u32[]{:S(2)}) %all-to-all-start.1) | async-done | bytes 393248 | tf_op jit(solution)/shard_map/all_to_all | solution.py:323
  120.8 0.5 slice.91
  122.0 1.1 slice_multiply_fusion
  (38 shorter events, 0.3 us)
Async XLA Ops:
  1.6 4.7 %collective-permute-start = (bf16[45,1,128]{2,1,0:T(2,128)(2,1)S(1)}, bf16[45,1,128]{2,1,0:T(2,128)(2,1)S(1)}, u32[]{:S(2)}, u32[]{:S(2)}) collective-permute-start(bf16[45,1,128]{2,1,0:T(2,128)(2,1)S(1)} %get-tuple-element.49), channel_id=1, source_target_pairs={{0,32},{64,96},{32,0},{96,64},{1,33},{65,97},{33,1},{97,65},{2,34}... | collective-permute-start | bytes 34568 | tf_op jit(solution)/shard_map/ppermute | solution.py:35
  3.8 2.6 %collective-permute-start.1 = (bf16[45,1,128]{2,1,0:T(2,128)(2,1)S(1)}, bf16[45,1,128]{2,1,0:T(2,128)(2,1)S(1)}, u32[]{:S(2)}, u32[]{:S(2)}) collective-permute-start(bf16[45,1,128]{2,1,0:T(2,128)(2,1)S(1)} %get-tuple-element.48), channel_id=1, source_target_pairs={{32,64},{64,32},{33,65},{65,33},{34,66},{66,34},{35,67},{67,35},{3... | collective-permute-start | bytes 34568 | tf_op jit(solution)/shard_map/ppermute | solution.py:36
  6.6 1.6 %copy-start = (bf16[1,180,45,128]{3,1,2,0:T(8,128)(2,1)S(1)}, bf16[1,180,45,128]{3,1,2,0:T(8,128)(2,1)}, u32[]{:S(2)}) copy-start(bf16[1,180,45,128]{3,1,2,0:T(8,128)(2,1)} %param.4) | copy-start | bytes 6220804
  8.2 1.5 %copy-start.4 = (bf16[1,180,45,80]{1,3,2,0:T(8,128)(2,1)S(1)}, bf16[1,180,45,80]{1,3,2,0:T(8,128)(2,1)}, u32[]{:S(2)}) copy-start(bf16[1,180,45,80]{1,3,2,0:T(8,128)(2,1)} %param.5) | copy-start | bytes 3888004
  9.7 0.9 copy-start.7
  13.8 24.2 %collective-permute-start.7 = (bf16[12,80,128]{2,1,0:T(8,128)(2,1)}, bf16[12,80,128]{2,1,0:T(8,128)(2,1)}, u32[]{:S(2)}, u32[]{:S(2)}) collective-permute-start(bf16[12,80,128]{2,1,0:T(8,128)(2,1)} %get-tuple-element.30.refs_3_), channel_id=1, source_target_pairs={{0,128},{128,0},{1,129},{129,1},{2,130},{130,2},{3,131},{131,3},{4... | collective-permute-start | bytes 737288 | tf_op jit(solution)/shard_map/ppermute | solution.py:357
  15.3 17.9 %collective-permute-start.2 = (bf16[1,256,128]{2,1,0:T(8,128)(2,1)S(1)}, bf16[1,256,128]{2,1,0:T(8,128)(2,1)S(1)}, u32[]{:S(2)}, u32[]{:S(2)}) collective-permute-start(bf16[1,256,128]{2,1,0:T(8,128)(2,1)S(1)} %get-tuple-element.61), channel_id=1, source_target_pairs={{1,2},{3,4},{5,6},{7,8},{9,10},{11,12},{13,14},{15,16},{17,18},{19... | collective-permute-start | bytes 196616 | tf_op jit(solution)/shard_map/ppermute | solution.py:36
  19.1 14.1 %collective-permute-start.3 = (bf16[1,256,128]{2,1,0:T(8,128)(2,1)S(1)}, bf16[1,256,128]{2,1,0:T(8,128)(2,1)S(1)}, u32[]{:S(2)}, u32[]{:S(2)}) collective-permute-start(bf16[1,256,128]{2,1,0:T(8,128)(2,1)S(1)} %get-tuple-element.60), channel_id=1, source_target_pairs={{0,1},{2,3},{4,5},{6,7},{8,9},{10,11},{12,13},{14,15},{16,17},{18,... | collective-permute-start | bytes 196616 | tf_op jit(solution)/shard_map/ppermute | solution.py:35
  27.6 16.2 %collective-permute-start.6 = (bf16[21,80,128]{2,1,0:T(8,128)(2,1)S(1)}, bf16[21,80,128]{2,1,0:T(8,128)(2,1)}, u32[]{:S(2)}, u32[]{:S(2)}) collective-permute-start(bf16[21,80,128]{2,1,0:T(8,128)(2,1)S(1)} %get-tuple-element.29.refs_3_), channel_id=1, source_target_pairs={{0,128},{128,0},{1,129},{129,1},{2,130},{130,2},{3,131},{131,3},{4... | collective-permute-start | bytes 1290248 | tf_op jit(solution)/shard_map/ppermute | solution.py:357
  31.7 18.4 %collective-permute-start.5 = (bf16[21,80,128]{2,1,0:T(8,128)(2,1)S(1)}, bf16[21,80,128]{2,1,0:T(8,128)(2,1)}, u32[]{:S(2)}, u32[]{:S(2)}) collective-permute-start(bf16[21,80,128]{2,1,0:T(8,128)(2,1)S(1)} %get-tuple-element.28.refs_3_), channel_id=1, source_target_pairs={{0,128},{128,0},{1,129},{129,1},{2,130},{130,2},{3,131},{131,3},{4... | collective-permute-start | bytes 1290248 | tf_op jit(solution)/shard_map/ppermute | solution.py:357
  33.2 4.8 %copy-start.1 = (bf16[1,180,45,128]{3,1,2,0:T(8,128)(2,1)S(1)}, bf16[1,180,45,128]{3,1,2,0:T(8,128)(2,1)}, u32[]{:S(2)}) copy-start(bf16[1,180,45,128]{3,1,2,0:T(8,128)(2,1)} %param.4) | copy-start | bytes 6220804
  36.5 19.9 %collective-permute-start.4 = (bf16[14,80,128]{2,1,0:T(8,128)(2,1)}, bf16[14,80,128]{2,1,0:T(8,128)(2,1)}, u32[]{:S(2)}, u32[]{:S(2)}) collective-permute-start(bf16[14,80,128]{2,1,0:T(8,128)(2,1)} %get-tuple-element.27.refs_3_), channel_id=1, source_target_pairs={{0,128},{128,0},{1,129},{129,1},{2,130},{130,2},{3,131},{131,3},{4... | collective-permute-start | bytes 860168 | tf_op jit(solution)/shard_map/ppermute | solution.py:357
  38.0 1.5 %copy-start.2 = (bf16[180,45,80]{0,2,1:T(8,128)(2,1)S(1)}, bf16[180,45,80]{0,2,1:T(8,128)(2,1)}, u32[]{:S(2)}) copy-start(bf16[180,45,80]{0,2,1:T(8,128)(2,1)} %param.6) | copy-start | bytes 3888004
  39.5 4.3 %copy-start.3 = (bf16[180,45,80]{0,2,1:T(8,128)(2,1)S(1)}, bf16[180,45,80]{0,2,1:T(8,128)(2,1)}, u32[]{:S(2)}) copy-start(bf16[180,45,80]{0,2,1:T(8,128)(2,1)} %param.6) | copy-start | bytes 3888004
  61.9 41.6 %copy-start.8 = (bf16[3,3,128,80]{2,3,1,0:T(8,128)(2,1)S(1)}, bf16[3,3,128,80]{2,3,1,0:T(8,128)(2,1)}, u32[]{:S(2)}) copy-start(bf16[3,3,128,80]{2,3,1,0:T(8,128)(2,1)} %param.7) | copy-start | bytes 552964
  62.0 16.0 %collective-permute-start.8 = (bf16[45,1,128]{2,1,0:T(2,128)(2,1)S(1)}, bf16[45,1,128]{2,1,0:T(2,128)(2,1)S(1)}, u32[]{:S(2)}, u32[]{:S(2)}) collective-permute-start(bf16[45,1,128]{2,1,0:T(2,128)(2,1)S(1)} %get-tuple-element.44), channel_id=1, source_target_pairs={{0,32},{64,96},{32,0},{96,64},{1,33},{65,97},{33,1},{97,65},{2,34}... | collective-permute-start | bytes 34568 | tf_op jit(solution)/shard_map/ppermute | solution.py:35
  65.5 12.5 %collective-permute-start.9 = (bf16[45,1,128]{2,1,0:T(2,128)(2,1)S(1)}, bf16[45,1,128]{2,1,0:T(2,128)(2,1)S(1)}, u32[]{:S(2)}, u32[]{:S(2)}) collective-permute-start(bf16[45,1,128]{2,1,0:T(2,128)(2,1)S(1)} %get-tuple-element.45), channel_id=1, source_target_pairs={{32,64},{64,32},{33,65},{65,33},{34,66},{66,34},{35,67},{67,35},{3... | collective-permute-start | bytes 34568 | tf_op jit(solution)/shard_map/ppermute | solution.py:36
  66.1 1.3 %copy-start.5 = (bf16[45,180,128]{2,1,0:T(8,128)(2,1)}, bf16[45,180,128]{2,1,0:T(8,128)(2,1)S(1)}, u32[]{:S(2)}) copy-start(bf16[45,180,128]{2,1,0:T(8,128)(2,1)S(1)} %get-tuple-element.38.refs_0_) | copy-start | bytes 6220804
  67.5 36.0 %copy-start.6 = (bf16[45,180,128]{2,1,0:T(8,128)(2,1)S(1)}, bf16[45,180,128]{2,1,0:T(8,128)(2,1)}, u32[]{:S(2)}) copy-start(bf16[45,180,128]{2,1,0:T(8,128)(2,1)} %copy-done.5) | copy-start | bytes 6220804
  67.5 28.2 %all-to-all-start = ((f32[256,1,384]{2,1,0:T(1,128)}), f32[256,1,384]{2,1,0:T(1,128)S(1)}, u32[]{:S(2)}, u32[]{:S(2)}) async-start(f32[256,1,384]{2,1,0:T(1,128)} %bitcast.10), calls=%async_computation | async-start | bytes 786432 | tf_op jit(solution)/shard_map/all_to_all | solution.py:323
  78.3 7.4 %collective-permute-start.10 = (bf16[1,256,128]{2,1,0:T(8,128)(2,1)S(1)}, bf16[1,256,128]{2,1,0:T(8,128)(2,1)S(1)}, u32[]{:S(2)}, u32[]{:S(2)}) collective-permute-start(bf16[1,256,128]{2,1,0:T(8,128)(2,1)S(1)} %get-tuple-element.59), channel_id=1, source_target_pairs={{1,2},{3,4},{5,6},{7,8},{9,10},{11,12},{13,14},{15,16},{17,18},{19... | collective-permute-start | bytes 196616 | tf_op jit(solution)/shard_map/ppermute | solution.py:36
  81.5 5.0 %collective-permute-start.11 = (bf16[1,256,128]{2,1,0:T(8,128)(2,1)S(1)}, bf16[1,256,128]{2,1,0:T(8,128)(2,1)S(1)}, u32[]{:S(2)}, u32[]{:S(2)}) collective-permute-start(bf16[1,256,128]{2,1,0:T(8,128)(2,1)S(1)} %get-tuple-element.58), channel_id=1, source_target_pairs={{0,1},{2,3},{4,5},{6,7},{8,9},{10,11},{12,13},{14,15},{16,17},{18,... | collective-permute-start | bytes 196616 | tf_op jit(solution)/shard_map/ppermute | solution.py:35
  97.0 23.8 %all-to-all-start.1 = ((f32[256,1,384]{2,1,0:T(1,128)}), f32[256,1,384]{2,1,0:T(1,128)S(1)}, u32[]{:S(2)}, u32[]{:S(2)}) async-start(f32[256,1,384]{2,1,0:T(1,128)} %broadcast_in_dim.17), calls=%async_computation.1 | async-start | bytes 786432 | tf_op jit(solution)/shard_map/all_to_all | solution.py:323

commit v5 on v4

--- a/solution.py
+++ b/solution.py
@@ -20,10 +20,8 @@
 def latitude_weights(row_index, total_rows):
     scale = math.pi / total_rows
     angles = 0.5 * math.pi - (row_index.astype(jnp.float32) + 0.5) * scale
-    every_row = (
-        0.5 * math.pi - (jnp.arange(total_rows, dtype=jnp.int32).astype(jnp.float32) + 0.5) * scale
-    )
-    return jnp.cos(angles) / jnp.mean(jnp.cos(every_row))
+    mean = sum(math.cos(0.5 * math.pi - (r + 0.5) * scale) for r in range(total_rows)) / total_rows
+    return jnp.cos(angles) * (1.0 / mean)
 
 
 def swapped(first, last, axis, wraps):
@@ -69,13 +67,12 @@
     return jnp.concatenate([ring_column(field, edges, column + b - 1) for b in range(3)], axis=1)
 
 
-def each_column(start, count, wraps, one, source_v, out, sems):
+def each_pair(start, count, wraps, two, source_v, out, sems):
     total = count + wraps
     pairs = (count - wraps) // 2
 
     def pair(t, carry):
-        one(2 * t, start + 2 * t, total + t, 0)
-        one(2 * t + 1, start + 2 * t + 1, total + t, 1)
+        two(2 * t, (start + 2 * t, start + 2 * t + 1))
         to = out.at[pl.ds(start + 2 * t, 2)]
         pltpu.make_async_copy(source_v.at[pl.ds(2 * t, 2)], to, sems.at[0]).start()
         return carry
@@ -85,30 +82,37 @@
     if pairs:
         span = pl.ds(0, 2 * pairs), pl.ds(start, 2 * pairs)
         copies.append(pltpu.make_async_copy(source_v.at[span[0]], out.at[span[1]], sems.at[0]))
-    for slot in range(2 * pairs, total):
-        column = start + slot if slot < count else 0
-        one(slot, column, total + slot // 2, slot % 2)
-        copy = pltpu.make_async_copy(
-            source_v.at[pl.ds(slot, 1)], out.at[pl.ds(column, 1)], sems.at[1 + slot - 2 * pairs]
-        )
-        copy.start()
-        copies.append(copy)
+    columns = [start + slot if slot < count else 0 for slot in range(total)]
+    for slot in range(2 * pairs, total, 2):
+        two(slot, tuple(columns[slot : slot + 2]))
+        for i in range(slot, min(slot + 2, total)):
+            copy = pltpu.make_async_copy(
+                source_v.at[pl.ds(i, 1)], out.at[pl.ds(columns[i], 1)], sems.at[1 + i - 2 * pairs]
+            )
+            copy.start()
+            copies.append(copy)
     for copy in copies:
         copy.wait()
+
+
+def together(low, high):
+    lane = lax.broadcasted_iota(jnp.int32, low.shape, 1)
+    return jnp.where(lane < LANES // 2, low, pltpu.roll(high, LANES // 2, 1))
 
 
 def forward_kernel(start, count, wraps, n_given, *refs):
     field, present_ref, taps_ref = refs[:3], refs[3], refs[4]
     edges = refs[5:7] if wraps else ()
-    pred_out, packed_out, weights_v, pred_v, sems = refs[n_given:]
+    pred_out, packed_out, weights_v, tails_v, pred_v, sems = refs[n_given:]
     outputs, rows = present_ref.shape[1:]
     for a in range(3):
         weights_v[a * outputs : (a + 1) * outputs] = jnp.concatenate(
             [taps_ref[a, b] for b in range(3)], axis=1
         )
-    half = LANES // 2
-
-    def one(slot, column, block, odd):
+    total = count + wraps
+    tails_v[...] = jnp.zeros_like(tails_v)
+
+    def one(slot, column, odd):
         y = lax.dot_general(
             weights_v[...],
             window(field, edges, column),
@@ -127,9 +131,14 @@
         pred_v[slot, :, :LANES] = head
         pred_v[slot, :, LANES:] = tail
         packed_out[slot] = head
-        packed_out[block, :, odd * half : odd * half + rows - LANES] = tail
-
-    each_column(start, count, wraps, one, pred_v, pred_out, sems)
+        tails_v[odd, :, : rows - LANES] = tail.astype(jnp.float32)
+
+    def two(slot, columns):
+        for i, column in enumerate(columns):
+            one(slot + i, column, i)
+        packed_out[total + slot // 2] = together(tails_v[0], tails_v[1]).astype(jnp.bfloat16)
+
+    each_pair(start, count, wraps, two, pred_v, pred_out, sems)
 
 
 def forward(start, count, wraps, field, present, taps, edges, pred):
@@ -153,6 +162,7 @@
         out_specs=(ANY, VMEM),
         scratch_shapes=[
             pltpu.VMEM((3 * outputs, 3 * inputs), jnp.bfloat16),
+            pltpu.VMEM((2, outputs, LANES), jnp.float32),
             pltpu.VMEM((total, outputs, rows), jnp.bfloat16),
             pltpu.SemaphoreType.DMA((4,)),
         ],
@@ -171,51 +181,72 @@
     field, own_ref, other_ref, target_ref, weight_ref = refs[:3], *refs[3:7]
     edges = refs[7 : 7 + n_edges]
     sums_ref = refs[7 + n_edges] if adds else None
-    turned_out, sums_out, cot_v, acc_v, score_v, turned_v, sems = refs[n_given:]
+    turned_out, sums_out, cot_v, acc_v, score_v, tails_v, turned_v, sems = refs[n_given:]
     outputs, rows = target_ref.shape[1:]
     inputs = field[0].shape[2]
-    half = LANES // 2
-    weight = weight_ref[...]
+    total = count + wraps
+    tail = rows - LANES
+    half_weight = 0.5 * weight_ref[...]
     cot_v[...] = jnp.zeros_like(cot_v)
     acc_v[...] = jnp.zeros_like(acc_v)
     score_v[...] = jnp.zeros_like(score_v)
-
-    def one(slot, column, block, odd):
-        lanes_of_tail = slice(odd * half, odd * half + rows - LANES)
-        for side in range(2):
-            lanes = slice(0, LANES) if side == 0 else slice(LANES, rows)
-            if side == 0:
-                value, partner = (ref[slot].astype(jnp.float32) for ref in (own_ref, other_ref))
-            else:
-                value, partner = (
-                    ref[block, :, lanes_of_tail].astype(jnp.float32) for ref in (own_ref, other_ref)
-                )
-            misfit = value - target_ref[column, :, lanes].astype(jnp.float32)
-            spread = value - partner
-            error2 = jnp.sum(misfit * misfit, axis=0, keepdims=True) + epsilon
-            pair2 = jnp.sum(spread * spread, axis=0, keepdims=True) + epsilon
-            error_inv = lax.rsqrt(error2)
-            pair_inv = lax.rsqrt(pair2)
-            scale = 0.5 * weight[:, lanes]
-            cot_v[odd, :outputs, lanes] = misfit * (scale * error_inv) - spread * (scale * pair_inv)
-            score_v[:, lanes] += scale * (error2 * error_inv - 0.5 * (pair2 * pair_inv))
-        cot = cot_v[odd]
-        turned_v[slot] = cot.T[:rows].astype(jnp.bfloat16)
-        cot = cot[:outputs]
-        shifted = jnp.concatenate([pltpu.roll(cot, RING - 1, 1), cot, pltpu.roll(cot, 1, 1)], axis=0)
-        acc_v[...] += jnp.dot(
-            shifted.astype(jnp.bfloat16), window(field, edges, column), preferred_element_type=jnp.float32
-        )
-
-    each_column(start, count, wraps, one, turned_v, turned_out, sems)
+    tails_v[...] = jnp.zeros_like(tails_v)
+
+    def gradient(value, partner, truth, scale, lanes):
+        misfit = value - truth
+        spread = value - partner
+        error2 = jnp.sum(misfit * misfit, axis=0, keepdims=True) + epsilon
+        pair2 = jnp.sum(spread * spread, axis=0, keepdims=True) + epsilon
+        error_inv = lax.rsqrt(error2)
+        pair_inv = lax.rsqrt(pair2)
+        score_v[:, lanes] += scale * (error2 * error_inv - 0.5 * (pair2 * pair_inv))
+        return misfit * (scale * error_inv) - spread * (scale * pair_inv)
+
+    def two(slot, columns):
+        for i, column in enumerate(columns):
+            cot_v[i, :outputs, :LANES] = gradient(
+                own_ref[slot + i].astype(jnp.float32),
+                other_ref[slot + i].astype(jnp.float32),
+                target_ref[column, :, :LANES].astype(jnp.float32),
+                half_weight[:, :LANES],
+                slice(0, LANES),
+            )
+            tails_v[i, :, :tail] = target_ref[column, :, LANES:].astype(jnp.float32)
+        block = total + slot // 2
+        ends = gradient(
+            own_ref[block].astype(jnp.float32),
+            other_ref[block].astype(jnp.float32),
+            together(tails_v[0], tails_v[1]),
+            half_weight[:, LANES:] if len(columns) == 2 else single_weight,
+            slice(LANES, 2 * LANES),
+        )
+        cot_v[0, :outputs, LANES:rows] = ends[:, :tail]
+        if len(columns) == 2:
+            cot_v[1, :outputs, LANES:rows] = pltpu.roll(ends, LANES // 2, 1)[:, :tail]
+        for i, column in enumerate(columns):
+            cot = cot_v[i]
+            turned_v[slot + i] = cot.T[:rows].astype(jnp.bfloat16)
+            cot = cot[:outputs]
+            shifted = jnp.concatenate(
+                [pltpu.roll(cot, RING - 1, 1), cot, pltpu.roll(cot, 1, 1)], axis=0
+            )
+            acc_v[...] += jnp.dot(
+                shifted.astype(jnp.bfloat16),
+                window(field, edges, column),
+                preferred_element_type=jnp.float32,
+            )
+
+    lane = lax.broadcasted_iota(jnp.int32, (1, LANES), 1)
+    single_weight = jnp.where(lane < LANES // 2, half_weight[:, LANES:], 0.0)
+    each_pair(start, count, wraps, two, turned_v, turned_out, sems)
     for a in range(3):
         for b in range(3):
             block = acc_v[a * outputs : (a + 1) * outputs, b * inputs : (b + 1) * inputs]
             place = slice((3 * a + b) * outputs, (3 * a + b + 1) * outputs)
             sums_out[place] = block + sums_ref[place] if adds else block
     spare = slice(9 * outputs, sums_out.shape[0])
-    total = jnp.sum(score_v[...], axis=1, keepdims=True)
-    filler = jnp.broadcast_to(total, (sums_out.shape[0] - 9 * outputs, inputs))
+    whole = jnp.sum(score_v[...], axis=1, keepdims=True)
+    filler = jnp.broadcast_to(whole, (sums_out.shape[0] - 9 * outputs, inputs))
     sums_out[spare] = filler + sums_ref[spare] if adds else filler
 
 
@@ -245,7 +276,8 @@
         scratch_shapes=[
             pltpu.VMEM((2, LANES, RING), jnp.float32),
             pltpu.VMEM((3 * outputs, 3 * inputs), jnp.float32),
-            pltpu.VMEM((1, RING), jnp.float32),
+            pltpu.VMEM((1, 2 * LANES), jnp.float32),
+            pltpu.VMEM((2, outputs, LANES), jnp.float32),
             pltpu.VMEM((total, rows, LANES), jnp.bfloat16),
             pltpu.SemaphoreType.DMA((4,)),
         ],
@@ -324,7 +356,7 @@
 
 
 def split(columns):
-    shares = (8, 14, 14, 9)
+    shares = (12, 18, 15)
     edges = [1]
     for i in range(len(shares) - 1):
         edges.append(1 + 2 * round(columns * sum(shares[: i + 1]) / sum(shares) / 2))
@@ -341,7 +373,9 @@
 
     taps = jnp.transpose(filter_weights_tensor, (0, 1, 3, 2))
     row_index = lax.axis_index("lat") * lat_rows + jnp.arange(lat_rows, dtype=jnp.int32)
-    weight = latitude_weights(row_index, total_rows)[None]
+    weight = latitude_weights(row_index, total_rows)
+    ends = jnp.pad(weight[LANES:], (0, LANES + LANES // 2 - lat_rows))
+    weight = jnp.concatenate([weight[:LANES], ends, ends])[None]
     columns = jnp.transpose(features[0], (1, 0, 2))
     present = jnp.transpose(present_condition[0], (1, 2, 0))
     truth = jnp.transpose(target, (1, 2, 0))

time: 125 us -> 123 us (0.984)
  waiting for transfers between devices: 19.6 us -> 28.3 us
  Pallas kernels: 44.4 us -> 39.4 us
  starting transfers between devices: 42.7 us -> 38.2 us
    ppermute x4, waiting for transfers between devices: 0.01 us -> 4.8 us  [swapped(): far = lax.ppermute(jnp.where(even, first, last), axis, both[1])]
    ppermute x4 -> x3, waiting for transfers between devices: 0.01 us -> 4.69 us  [local(): packed.append((own, lax.ppermute(own, 'member', [(0, 1), (1, 0)])))]
    pallas_call x4 -> x3, Pallas kernels: 22.3 us -> 18.3 us  [scored(): pl.pallas_call(functools.partial(score_kernel, start, count, wraps, len(e...]
    ppermute x4, starting transfers between devices: 8.36 us -> 6.28 us  [swapped(): far = lax.ppermute(jnp.where(even, first, last), axis, both[1])]
    ppermute x4, starting transfers between devices: 14.3 us -> 12.4 us  [swapped(): near = lax.ppermute(jnp.where(even, last, first), axis, both[0])]
    pallas_call x4 -> x3, Pallas kernels: 14.3 us -> 13.4 us  [forward(): pl.pallas_call(functools.partial(forward_kernel, start, count, wraps, len...]
    ppermute x4 -> x3, starting transfers between devices: 3.12 us -> 2.99 us  [local(): packed.append((own, lax.ppermute(own, 'member', [(0, 1), (1, 0)])))]
  transfers between devices with their start and end apart: 14 -> 13, of which waited for: 3 -> 5; matrix products, arithmetic and copies ran while one was open for 2% -> 2% of each run, Pallas kernels for 29% -> 24%
where the time goes in v5:
time: 123 us; the launch traced here: 122 us
  Pallas kernels  39.4 us (32%)
  starting transfers between devices  38.2 us (31%)
  waiting for transfers between devices  28.3 us (23%)
  local copies, waits for them, and re-layouts  10.4 us (8%)
  other arithmetic  3.16 us (3%)
  between operations  2.76 us (2%)
    all_to_all x2, waiting for transfers between devices, exchange(): return lax.all_to_all(blocks, AXES, 0, 0, tiled=True)  18.8 us
    pallas_call x3, Pallas kernels, scored(): pl.pallas_call(functools.partial(score_kernel, start, count, wraps, len(e...  18.3 us
    all_to_all x2, starting transfers between devices, exchange(): return lax.all_to_all(blocks, AXES, 0, 0, tiled=True)  16.6 us
    pallas_call x3, Pallas kernels, forward(): pl.pallas_call(functools.partial(forward_kernel, start, count, wraps, len...  13.4 us
    ppermute x4, starting transfers between devices, swapped(): near = lax.ppermute(jnp.where(even, last, first), axis, both[0])  12.4 us
    pallas_call x1, Pallas kernels, backward(): pl.pallas_call(functools.partial(backward_kernel, block), grid=(columns /...  7.75 us
    unnamed x18, local copies, waits for them, and re-layouts  6.86 us
    ppermute x4, starting transfers between devices, swapped(): far = lax.ppermute(jnp.where(even, first, last), axis, both[1])  6.28 us
  transfers between devices with their start and end apart: 13, of which 5 were waited for; matrix products, arithmetic and copies ran while one was open for 2% of the time, Pallas kernels for 24%

profile of v5, /device:TPU:1, one launch (start us, length us, event | category | flops | bytes accessed | tf_op | source)
XLA Modules:
  0.0 122.3 jit_solution(1342837444030056762)
XLA Ops:
  0.6 1.0 broadcast_select_fusion.14
  1.6 2.1 %collective-permute-start = (bf16[45,1,128]{2,1,0:T(2,128)(2,1)S(1)}, bf16[45,1,128]{2,1,0:T(2,128)(2,1)S(1)}, u32[]{:S(2)}, u32[]{:S(2)}) collective-permute-start(bf16[45,1,128]{2,1,0:T(2,128)(2,1)S(1)} %get-tuple-element.41), channel_id=1, source_target_pairs={{0,32},{64,96},{32,0},{96,64},{1,33},{65,97},{33,1},{97,65},{2,34}... | collective-permute-start | bytes 34568 | tf_op jit(solution)/shard_map/ppermute | solution.py:33
  3.8 0.7 collective-permute-start.1
  4.4 0.8 fusion.1
  5.2 0.9 slice.90
  6.2 0.1 pad.31.clone
  6.3 0.1 pad.27.clone
  6.5 0.1 maximum_maximum_fusion.refs_1_
  6.6 0.0 copy-start
  6.6 1.6 %copy-done = bf16[1,180,45,128]{3,1,2,0:T(8,128)(2,1)S(1)} copy-done((bf16[1,180,45,128]{3,1,2,0:T(8,128)(2,1)S(1)}, bf16[1,180,45,128]{3,1,2,0:T(8,128)(2,1)}, u32[]{:S(2)}) %copy-start) | copy-done | bytes 2073624
  8.2 1.5 %copy-done.2 = bf16[1,180,45,80]{1,3,2,0:T(8,128)(2,1)S(1)} copy-done((bf16[1,180,45,80]{1,3,2,0:T(8,128)(2,1)S(1)}, bf16[1,180,45,80]{1,3,2,0:T(8,128)(2,1)}, u32[]{:S(2)}) %copy-start.2) | copy-done | bytes 1296024
  9.7 0.9 copy-done.7
  10.6 3.6 %forward.3 = (bf16[45,80,180]{2,1,0:T(8,128)(2,1)}, bf16[18,80,128]{2,1,0:T(8,128)(2,1)S(1)}) custom-call(bf16[45,180,128]{2,1,0:T(8,128)(2,1)S(1)} %bitcast.24, bf16[45,16,128]{2,1,0:T(8,128)(2,1)S(1)} %maximum_maximum_fusion.refs_1_, bf16[45,16,128]{2,1,0:T(8,128)(2,1)S(1)} %concatenate.94.refs_2_, bf16[45,80,180]{2,1,0:T(8,128)(2,1)S(1)} %bitcast.30, ...), custom_call_target="tpu_custom_call" | custom-call | flops 566231040 | bytes 2260992 | tf_op jit(solution)/shard_map/forward/pallas_call | solution.py:155
  14.2 1.4 %collective-permute-start.6 = (bf16[18,80,128]{2,1,0:T(8,128)(2,1)S(1)}, bf16[18,80,128]{2,1,0:T(8,128)(2,1)}, u32[]{:S(2)}, u32[]{:S(2)}) collective-permute-start(bf16[18,80,128]{2,1,0:T(8,128)(2,1)S(1)} %get-tuple-element.24.refs_3_), channel_id=1, source_target_pairs={{0,128},{128,0},{1,129},{129,1},{2,130},{130,2},{3,131},{131,3},{4... | collective-permute-start | bytes 1105928 | tf_op jit(solution)/shard_map/ppermute | solution.py:391
  15.5 0.1 broadcast_select_fusion.6
  15.7 3.8 %collective-permute-start.2 = (bf16[1,256,128]{2,1,0:T(8,128)(2,1)S(1)}, bf16[1,256,128]{2,1,0:T(8,128)(2,1)S(1)}, u32[]{:S(2)}, u32[]{:S(2)}) collective-permute-start(bf16[1,256,128]{2,1,0:T(8,128)(2,1)S(1)} %get-tuple-element.53), channel_id=1, source_target_pairs={{1,2},{3,4},{5,6},{7,8},{9,10},{11,12},{13,14},{15,16},{17,18},{19... | collective-permute-start | bytes 196616 | tf_op jit(solution)/shard_map/ppermute | solution.py:34
  19.5 4.6 %collective-permute-start.3 = (bf16[1,256,128]{2,1,0:T(8,128)(2,1)S(1)}, bf16[1,256,128]{2,1,0:T(8,128)(2,1)S(1)}, u32[]{:S(2)}, u32[]{:S(2)}) collective-permute-start(bf16[1,256,128]{2,1,0:T(8,128)(2,1)S(1)} %get-tuple-element.52), channel_id=1, source_target_pairs={{0,1},{2,3},{4,5},{6,7},{8,9},{10,11},{12,13},{14,15},{16,17},{18,... | collective-permute-start | bytes 196616 | tf_op jit(solution)/shard_map/ppermute | solution.py:33
  24.1 5.0 %forward.4 = (bf16[45,80,180]{2,1,0:T(8,128)(2,1)}, bf16[27,80,128]{2,1,0:T(8,128)(2,1)S(1)}) custom-call(bf16[45,180,128]{2,1,0:T(8,128)(2,1)S(1)} %bitcast.25, bf16[45,16,128]{2,1,0:T(8,128)(2,1)S(1)} %maximum_maximum_fusion.refs_1_, bf16[45,16,128]{2,1,0:T(8,128)(2,1)S(1)} %concatenate.94.refs_2_, ...), custom_call_target="tpu_custom_call", output_to_operand_aliasing={{0}: (5, {})} | custom-call | flops 849346560 | bytes 3391488 | tf_op jit(solution)/shard_map/forward/pallas_call | solution.py:155
  29.1 0.1 collective-permute-start.5
  29.2 0.0 copy-start.1
  29.2 4.8 %forward.5 = (bf16[45,80,180]{2,1,0:T(8,128)(2,1)}, bf16[23,80,128]{2,1,0:T(8,128)(2,1)}) custom-call(bf16[45,180,128]{2,1,0:T(8,128)(2,1)S(1)} %bitcast.26, bf16[45,16,128]{2,1,0:T(8,128)(2,1)S(1)} %maximum_maximum_fusion.refs_1_, bf16[45,16,128]{2,1,0:T(8,128)(2,1)S(1)} %concatenate.94.refs_2_, ...), custom_call_target="tpu_custom_call", output_to_operand_aliasing={{0}: (7, {})} | custom-call | flops 707788800 | bytes 2826240 | tf_op jit(solution)/shard_map/forward/pallas_call | solution.py:155
  34.0 1.5 %collective-permute-start.4 = (bf16[23,80,128]{2,1,0:T(8,128)(2,1)}, bf16[23,80,128]{2,1,0:T(8,128)(2,1)}, u32[]{:S(2)}, u32[]{:S(2)}) collective-permute-start(bf16[23,80,128]{2,1,0:T(8,128)(2,1)} %get-tuple-element.22.refs_3_), channel_id=1, source_target_pairs={{0,128},{128,0},{1,129},{129,1},{2,130},{130,2},{3,131},{131,3},{4... | collective-permute-start | bytes 1413128 | tf_op jit(solution)/shard_map/ppermute | solution.py:391
  35.6 0.1 pad_maximum_fusion.4
  35.7 1.5 %copy-done.3 = bf16[180,45,80]{0,2,1:T(8,128)(2,1)S(1)} copy-done((bf16[180,45,80]{0,2,1:T(8,128)(2,1)S(1)}, bf16[180,45,80]{0,2,1:T(8,128)(2,1)}, u32[]{:S(2)}) %copy-start.3) | copy-done | bytes 1296024
  37.2 4.9 %score.3 = (bf16[45,180,128]{2,1,0:T(8,128)(2,1)S(1)}, f32[768,128]{1,0:T(8,128)S(1)}) custom-call(bf16[45,180,128]{2,1,0:T(8,128)(2,1)S(1)} %bitcast.27, bf16[45,16,128]{2,1,0:T(8,128)(2,1)S(1)} %maximum_maximum_fusion.refs_1_, bf16[45,16,128]{2,1,0:T(8,128)(2,1)S(1)} %concatenate.94.refs_2_, bf16[18,80,128]{2,1,0:T(8,128)(2,1)S(1)} %get-tuple-element.24.refs_3_, ...), custom_call_target="tpu_custom_call" | custom-call | flops 566231040 | bytes 2260992 | tf_op jit(solution)/shard_map/score/pallas_call | solution.py:266
  42.1 1.3 %collective-permute-done.5.refs_4_ = bf16[27,80,128]{2,1,0:T(8,128)(2,1)} collective-permute-done((bf16[27,80,128]{2,1,0:T(8,128)(2,1)S(1)}, bf16[27,80,128]{2,1,0:T(8,128)(2,1)}, u32[]{:S(2)}, u32[]{:S(2)}) %collective-permute-start.5) | collective-permute-done | bytes 552992 | tf_op jit(solution)/shard_map/ppermute | solution.py:391
  43.4 6.7 %score.4 = (bf16[45,180,128]{2,1,0:T(8,128)(2,1)S(1)}, f32[768,128]{1,0:T(8,128)S(1)}) custom-call(bf16[45,180,128]{2,1,0:T(8,128)(2,1)S(1)} %bitcast.28, bf16[45,16,128]{2,1,0:T(8,128)(2,1)S(1)} %maximum_maximum_fusion.refs_1_, bf16[45,16,128]{2,1,0:T(8,128)(2,1)S(1)} %concatenate.94.refs_2_, ...), custom_call_target="tpu_custom_call", output_to_operand_aliasing={{0}: (8, {})} | custom-call | flops 849346560 | bytes 3391488 | tf_op jit(solution)/shard_map/score/pallas_call | solution.py:266
  50.1 3.4 %collective-permute-done.4.refs_4_ = bf16[23,80,128]{2,1,0:T(8,128)(2,1)} collective-permute-done((bf16[23,80,128]{2,1,0:T(8,128)(2,1)}, bf16[23,80,128]{2,1,0:T(8,128)(2,1)}, u32[]{:S(2)}, u32[]{:S(2)}) %collective-permute-start.4) | collective-permute-done | bytes 471072 | tf_op jit(solution)/shard_map/ppermute | solution.py:391
  53.5 6.8 %score.5 = (bf16[45,180,128]{2,1,0:T(8,128)(2,1)S(1)}, f32[768,128]{1,0:T(8,128)}) custom-call(bf16[45,180,128]{2,1,0:T(8,128)(2,1)S(1)} %bitcast.29, bf16[45,16,128]{2,1,0:T(8,128)(2,1)S(1)} %maximum_maximum_fusion.refs_1_, bf16[45,16,128]{2,1,0:T(8,128)(2,1)S(1)} %concatenate.94.refs_2_, ...), custom_call_target="tpu_custom_call", output_to_operand_aliasing={{0}: (10, {})} | custom-call | flops 707788800 | bytes 2826240 | tf_op jit(solution)/shard_map/score/pallas_call | solution.py:266
  60.3 0.1 broadcast_select_fusion.11
  60.3 3.5 %collective-permute-start.7 = (bf16[45,1,128]{2,1,0:T(2,128)(2,1)S(1)}, bf16[45,1,128]{2,1,0:T(2,128)(2,1)S(1)}, u32[]{:S(2)}, u32[]{:S(2)}) collective-permute-start(bf16[45,1,128]{2,1,0:T(2,128)(2,1)S(1)} %get-tuple-element.36), channel_id=1, source_target_pairs={{0,32},{64,96},{32,0},{96,64},{1,33},{65,97},{33,1},{97,65},{2,34}... | collective-permute-start | bytes 34568 | tf_op jit(solution)/shard_map/ppermute | solution.py:33
  63.8 0.7 collective-permute-start.8
  64.5 1.3 %copy-done.5 = bf16[45,180,128]{2,1,0:T(8,128)(2,1)} copy-done((bf16[45,180,128]{2,1,0:T(8,128)(2,1)}, bf16[45,180,128]{2,1,0:T(8,128)(2,1)S(1)}, u32[]{:S(2)}) %copy-start.5) | copy-done | bytes 2073624
  65.8 10.0 %all-to-all-start = ((f32[256,1,384]{2,1,0:T(1,128)}), f32[256,1,384]{2,1,0:T(1,128)S(1)}, u32[]{:S(2)}, u32[]{:S(2)}) async-start(f32[256,1,384]{2,1,0:T(1,128)} %bitcast.11), calls=%async_computation | async-start | bytes 786432 | tf_op jit(solution)/shard_map/all_to_all | solution.py:355
  75.8 0.1 broadcast_select_fusion.9
  75.9 0.1 maximum_maximum_fusion.1.refs_1_
  76.0 0.1 broadcast_select_fusion.2
  76.1 2.2 %collective-permute-start.10 = (bf16[1,256,128]{2,1,0:T(8,128)(2,1)S(1)}, bf16[1,256,128]{2,1,0:T(8,128)(2,1)S(1)}, u32[]{:S(2)}, u32[]{:S(2)}) collective-permute-start(bf16[1,256,128]{2,1,0:T(8,128)(2,1)S(1)} %get-tuple-element.50), channel_id=1, source_target_pairs={{0,1},{2,3},{4,5},{6,7},{8,9},{10,11},{12,13},{14,15},{16,17},{18,... | collective-permute-start | bytes 196616 | tf_op jit(solution)/shard_map/ppermute | solution.py:33
  78.3 1.1 collective-permute-start.9
  79.5 4.8 %collective-permute-done.9 = bf16[1,256,128]{2,1,0:T(8,128)(2,1)S(1)} collective-permute-done((bf16[1,256,128]{2,1,0:T(8,128)(2,1)S(1)}, bf16[1,256,128]{2,1,0:T(8,128)(2,1)S(1)}, u32[]{:S(2)}, u32[]{:S(2)}) %collective-permute-start.9) | collective-permute-done | bytes 65568 | tf_op jit(solution)/shard_map/ppermute | solution.py:34
  84.3 9.2 %all-to-all-done = f32[256,1,384]{2,1,0:T(1,128)S(1)} async-done(((f32[256,1,384]{2,1,0:T(1,128)}), f32[256,1,384]{2,1,0:T(1,128)S(1)}, u32[]{:S(2)}, u32[]{:S(2)}) %all-to-all-start) | async-done | bytes 393248 | tf_op jit(solution)/shard_map/all_to_all | solution.py:355
  93.5 0.3 reduce_sum.9
  93.9 1.0 broadcast_in_dim.20
  94.8 6.6 %all-to-all-start.1 = ((f32[256,1,384]{2,1,0:T(1,128)}), f32[256,1,384]{2,1,0:T(1,128)S(1)}, u32[]{:S(2)}, u32[]{:S(2)}) async-start(f32[256,1,384]{2,1,0:T(1,128)} %broadcast_in_dim.20), calls=%async_computation.1 | async-start | bytes 786432 | tf_op jit(solution)/shard_map/all_to_all | solution.py:355
  101.5 7.7 %backward.1 = bf16[45,180,128]{2,1,0:T(8,128)(2,1)} custom-call(bf16[45,180,128]{2,1,0:T(8,128)(2,1)S(1)} %copy-done.6, bf16[45,16,128]{2,1,0:T(8,128)(2,1)S(1)} %maximum_maximum_fusion.1.refs_1_, bf16[45,16,128]{2,1,0:T(8,128)(2,1)S(1)} %concatenate.100.refs_2_, bf16[1,256,128]{2,1,0:T(8,128)(2,1)S(1)} %get-tuple-element.32.refs_3_, ...), custom_call_target="tpu_custom_call" | custom-call | flops 3397386240 | bytes 5898240 | tf_op jit(solution)/shard_map/backward/pallas_call | solution.py:335
  109.3 9.6 %all-to-all-done.1 = f32[256,1,384]{2,1,0:T(1,128)S(1)} async-done(((f32[256,1,384]{2,1,0:T(1,128)}), f32[256,1,384]{2,1,0:T(1,128)S(1)}, u32[]{:S(2)}, u32[]{:S(2)}) %all-to-all-start.1) | async-done | bytes 393248 | tf_op jit(solution)/shard_map/all_to_all | solution.py:355
  118.8 0.5 slice.99
  120.0 1.1 slice_multiply_fusion
  (37 shorter events, 0.4 us)
Async XLA Ops:
  1.6 4.7 %collective-permute-start = (bf16[45,1,128]{2,1,0:T(2,128)(2,1)S(1)}, bf16[45,1,128]{2,1,0:T(2,128)(2,1)S(1)}, u32[]{:S(2)}, u32[]{:S(2)}) collective-permute-start(bf16[45,1,128]{2,1,0:T(2,128)(2,1)S(1)} %get-tuple-element.41), channel_id=1, source_target_pairs={{0,32},{64,96},{32,0},{96,64},{1,33},{65,97},{33,1},{97,65},{2,34}... | collective-permute-start | bytes 34568 | tf_op jit(solution)/shard_map/ppermute | solution.py:33
  3.8 2.6 %collective-permute-start.1 = (bf16[45,1,128]{2,1,0:T(2,128)(2,1)S(1)}, bf16[45,1,128]{2,1,0:T(2,128)(2,1)S(1)}, u32[]{:S(2)}, u32[]{:S(2)}) collective-permute-start(bf16[45,1,128]{2,1,0:T(2,128)(2,1)S(1)} %get-tuple-element.40), channel_id=1, source_target_pairs={{32,64},{64,32},{33,65},{65,33},{34,66},{66,34},{35,67},{67,35},{3... | collective-permute-start | bytes 34568 | tf_op jit(solution)/shard_map/ppermute | solution.py:34
  6.6 1.6 %copy-start = (bf16[1,180,45,128]{3,1,2,0:T(8,128)(2,1)S(1)}, bf16[1,180,45,128]{3,1,2,0:T(8,128)(2,1)}, u32[]{:S(2)}) copy-start(bf16[1,180,45,128]{3,1,2,0:T(8,128)(2,1)} %param.4) | copy-start | bytes 6220804
  8.2 1.5 %copy-start.2 = (bf16[1,180,45,80]{1,3,2,0:T(8,128)(2,1)S(1)}, bf16[1,180,45,80]{1,3,2,0:T(8,128)(2,1)}, u32[]{:S(2)}) copy-start(bf16[1,180,45,80]{1,3,2,0:T(8,128)(2,1)} %param.5) | copy-start | bytes 3888004
  9.7 0.9 copy-start.7
  14.2 21.5 %collective-permute-start.6 = (bf16[18,80,128]{2,1,0:T(8,128)(2,1)S(1)}, bf16[18,80,128]{2,1,0:T(8,128)(2,1)}, u32[]{:S(2)}, u32[]{:S(2)}) collective-permute-start(bf16[18,80,128]{2,1,0:T(8,128)(2,1)S(1)} %get-tuple-element.24.refs_3_), channel_id=1, source_target_pairs={{0,128},{128,0},{1,129},{129,1},{2,130},{130,2},{3,131},{131,3},{4... | collective-permute-start | bytes 1105928 | tf_op jit(solution)/shard_map/ppermute | solution.py:391
  15.7 13.5 %collective-permute-start.2 = (bf16[1,256,128]{2,1,0:T(8,128)(2,1)S(1)}, bf16[1,256,128]{2,1,0:T(8,128)(2,1)S(1)}, u32[]{:S(2)}, u32[]{:S(2)}) collective-permute-start(bf16[1,256,128]{2,1,0:T(8,128)(2,1)S(1)} %get-tuple-element.53), channel_id=1, source_target_pairs={{1,2},{3,4},{5,6},{7,8},{9,10},{11,12},{13,14},{15,16},{17,18},{19... | collective-permute-start | bytes 196616 | tf_op jit(solution)/shard_map/ppermute | solution.py:34
  19.5 9.7 %collective-permute-start.3 = (bf16[1,256,128]{2,1,0:T(8,128)(2,1)S(1)}, bf16[1,256,128]{2,1,0:T(8,128)(2,1)S(1)}, u32[]{:S(2)}, u32[]{:S(2)}) collective-permute-start(bf16[1,256,128]{2,1,0:T(8,128)(2,1)S(1)} %get-tuple-element.52), channel_id=1, source_target_pairs={{0,1},{2,3},{4,5},{6,7},{8,9},{10,11},{12,13},{14,15},{16,17},{18,... | collective-permute-start | bytes 196616 | tf_op jit(solution)/shard_map/ppermute | solution.py:33
  29.1 14.4 %collective-permute-start.5 = (bf16[27,80,128]{2,1,0:T(8,128)(2,1)S(1)}, bf16[27,80,128]{2,1,0:T(8,128)(2,1)}, u32[]{:S(2)}, u32[]{:S(2)}) collective-permute-start(bf16[27,80,128]{2,1,0:T(8,128)(2,1)S(1)} %get-tuple-element.23.refs_3_), channel_id=1, source_target_pairs={{0,128},{128,0},{1,129},{129,1},{2,130},{130,2},{3,131},{131,3},{4... | collective-permute-start | bytes 1658888 | tf_op jit(solution)/shard_map/ppermute | solution.py:391
  29.2 6.5 %copy-start.1 = (bf16[1,180,45,128]{3,1,2,0:T(8,128)(2,1)S(1)}, bf16[1,180,45,128]{3,1,2,0:T(8,128)(2,1)}, u32[]{:S(2)}) copy-start(bf16[1,180,45,128]{3,1,2,0:T(8,128)(2,1)} %param.4) | copy-start | bytes 6220804
  34.0 19.5 %collective-permute-start.4 = (bf16[23,80,128]{2,1,0:T(8,128)(2,1)}, bf16[23,80,128]{2,1,0:T(8,128)(2,1)}, u32[]{:S(2)}, u32[]{:S(2)}) collective-permute-start(bf16[23,80,128]{2,1,0:T(8,128)(2,1)} %get-tuple-element.22.refs_3_), channel_id=1, source_target_pairs={{0,128},{128,0},{1,129},{129,1},{2,130},{130,2},{3,131},{131,3},{4... | collective-permute-start | bytes 1413128 | tf_op jit(solution)/shard_map/ppermute | solution.py:391
  35.7 1.5 %copy-start.3 = (bf16[180,45,80]{0,2,1:T(8,128)(2,1)S(1)}, bf16[180,45,80]{0,2,1:T(8,128)(2,1)}, u32[]{:S(2)}) copy-start(bf16[180,45,80]{0,2,1:T(8,128)(2,1)} %param.6) | copy-start | bytes 3888004
  37.2 6.2 %copy-start.4 = (bf16[180,45,80]{0,2,1:T(8,128)(2,1)S(1)}, bf16[180,45,80]{0,2,1:T(8,128)(2,1)}, u32[]{:S(2)}) copy-start(bf16[180,45,80]{0,2,1:T(8,128)(2,1)} %param.6) | copy-start | bytes 3888004
  60.3 41.2 %copy-start.8 = (bf16[3,3,128,80]{2,3,1,0:T(8,128)(2,1)S(1)}, bf16[3,3,128,80]{2,3,1,0:T(8,128)(2,1)}, u32[]{:S(2)}) copy-start(bf16[3,3,128,80]{2,3,1,0:T(8,128)(2,1)} %param.7) | copy-start | bytes 552964
  60.3 15.5 %collective-permute-start.7 = (bf16[45,1,128]{2,1,0:T(2,128)(2,1)S(1)}, bf16[45,1,128]{2,1,0:T(2,128)(2,1)S(1)}, u32[]{:S(2)}, u32[]{:S(2)}) collective-permute-start(bf16[45,1,128]{2,1,0:T(2,128)(2,1)S(1)} %get-tuple-element.36), channel_id=1, source_target_pairs={{0,32},{64,96},{32,0},{96,64},{1,33},{65,97},{33,1},{97,65},{2,34}... | collective-permute-start | bytes 34568 | tf_op jit(solution)/shard_map/ppermute | solution.py:33
  63.8 12.0 %collective-permute-start.8 = (bf16[45,1,128]{2,1,0:T(2,128)(2,1)S(1)}, bf16[45,1,128]{2,1,0:T(2,128)(2,1)S(1)}, u32[]{:S(2)}, u32[]{:S(2)}) collective-permute-start(bf16[45,1,128]{2,1,0:T(2,128)(2,1)S(1)} %get-tuple-element.37), channel_id=1, source_target_pairs={{32,64},{64,32},{33,65},{65,33},{34,66},{66,34},{35,67},{67,35},{3... | collective-permute-start | bytes 34568 | tf_op jit(solution)/shard_map/ppermute | solution.py:34
  64.5 1.3 %copy-start.5 = (bf16[45,180,128]{2,1,0:T(8,128)(2,1)}, bf16[45,180,128]{2,1,0:T(8,128)(2,1)S(1)}, u32[]{:S(2)}) copy-start(bf16[45,180,128]{2,1,0:T(8,128)(2,1)S(1)} %get-tuple-element.30.refs_0_) | copy-start | bytes 6220804
  65.8 35.7 %copy-start.6 = (bf16[45,180,128]{2,1,0:T(8,128)(2,1)S(1)}, bf16[45,180,128]{2,1,0:T(8,128)(2,1)}, u32[]{:S(2)}) copy-start(bf16[45,180,128]{2,1,0:T(8,128)(2,1)} %copy-done.5) | copy-start | bytes 6220804
  65.8 27.7 %all-to-all-start = ((f32[256,1,384]{2,1,0:T(1,128)}), f32[256,1,384]{2,1,0:T(1,128)S(1)}, u32[]{:S(2)}, u32[]{:S(2)}) async-start(f32[256,1,384]{2,1,0:T(1,128)} %bitcast.11), calls=%async_computation | async-start | bytes 786432 | tf_op jit(solution)/shard_map/all_to_all | solution.py:355
  76.1 3.4 %collective-permute-start.10 = (bf16[1,256,128]{2,1,0:T(8,128)(2,1)S(1)}, bf16[1,256,128]{2,1,0:T(8,128)(2,1)S(1)}, u32[]{:S(2)}, u32[]{:S(2)}) collective-permute-start(bf16[1,256,128]{2,1,0:T(8,128)(2,1)S(1)} %get-tuple-element.50), channel_id=1, source_target_pairs={{0,1},{2,3},{4,5},{6,7},{8,9},{10,11},{12,13},{14,15},{16,17},{18,... | collective-permute-start | bytes 196616 | tf_op jit(solution)/shard_map/ppermute | solution.py:33
  78.3 5.9 %collective-permute-start.9 = (bf16[1,256,128]{2,1,0:T(8,128)(2,1)S(1)}, bf16[1,256,128]{2,1,0:T(8,128)(2,1)S(1)}, u32[]{:S(2)}, u32[]{:S(2)}) collective-permute-start(bf16[1,256,128]{2,1,0:T(8,128)(2,1)S(1)} %get-tuple-element.51), channel_id=1, source_target_pairs={{1,2},{3,4},{5,6},{7,8},{9,10},{11,12},{13,14},{15,16},{17,18},{19... | collective-permute-start | bytes 196616 | tf_op jit(solution)/shard_map/ppermute | solution.py:34
  94.8 24.0 %all-to-all-start.1 = ((f32[256,1,384]{2,1,0:T(1,128)}), f32[256,1,384]{2,1,0:T(1,128)S(1)}, u32[]{:S(2)}, u32[]{:S(2)}) async-start(f32[256,1,384]{2,1,0:T(1,128)} %broadcast_in_dim.20), calls=%async_computation.1 | async-start | bytes 786432 | tf_op jit(solution)/shard_map/all_to_all | solution.py:355

commit v6 on v5

--- a/solution.py
+++ b/solution.py
@@ -44,14 +44,18 @@
     return low, jnp.concatenate([gap, above], axis=1)
 
 
-def lon_edges(columns, low, high):
+def lon_rings(columns, low, high):
     body = columns.shape[1] - columns.shape[1] % TILE
 
     def ring(part):
         gap = jnp.zeros((1, RING - body - 2 * TILE, columns.shape[2]), columns.dtype)
         return jnp.concatenate([columns[part, :body], low[part], gap, high[part]], axis=1)
 
-    return swapped(ring(slice(0, 1)), ring(slice(-1, None)), "lon", True)
+    return ring(slice(0, 1)), ring(slice(-1, None))
+
+
+def lon_edges(rings):
+    return swapped(*rings, "lon", True)
 
 
 def ring_column(field, edges, column):
@@ -356,7 +360,7 @@
 
 
 def split(columns):
-    shares = (12, 18, 15)
+    shares = (12, 20, 13)
     edges = [1]
     for i in range(len(shares) - 1):
         edges.append(1 + 2 * round(columns * sum(shares[: i + 1]) / sum(shares) / 2))
@@ -381,13 +385,18 @@
     truth = jnp.transpose(target, (1, 2, 0))
 
     field = (columns, *lat_edges(columns))
-    edges = lon_edges(*field)
+    rings = lon_rings(*field)
+    edges = None
     chunks = split(lon_cols)
     pred = None
     packed = []
     for start, count in chunks:
         wraps = int(start + count == lon_cols)
+        if wraps:
+            edges = lon_edges(rings)
         pred, own = forward(start, count, wraps, field, present, taps, edges, pred)
+        if not wraps:
+            rings, own = lax.optimization_barrier((rings, own))
         packed.append((own, lax.ppermute(own, "member", [(0, 1), (1, 0)])))
 
     width = -(-(9 * outputs * inputs + 1) // (devices * LANES)) * LANES
@@ -401,7 +410,7 @@
     turned, sums = carried
     share = jnp.sum(exchange(sums.reshape(devices, width)), axis=0, keepdims=True)
     field = (turned, *lat_edges(turned))
-    share, edges = lax.optimization_barrier((share, lon_edges(*field)))
+    share, edges = lax.optimization_barrier((share, lon_edges(lon_rings(*field))))
     whole = exchange(jnp.broadcast_to(share, (devices, width))).reshape(sum_rows, inputs)
     slope = backward(field, edges, taps)
     objective_mean = whole[9 * outputs, 0] / (total_rows * total_cols)

time: 123 us -> 136 us (1.11)
  waiting for transfers between devices: 28.3 us -> 40.7 us
    ppermute x3, waiting for transfers between devices: 4.69 us -> 17 us  [local(): packed.append((own, lax.ppermute(own, 'member', [(0, 1), (1, 0)])))]
  transfers between devices with their start and end apart: 13 -> 13, of which waited for: 5 -> 4; matrix products, arithmetic and copies ran while one was open for 2% -> 2% of each run, Pallas kernels for 24% -> 18%
where the time goes in v6:
time: 136 us; the launch traced here: 135 us
  waiting for transfers between devices  40.7 us (30%)
  Pallas kernels  40.2 us (30%)
  starting transfers between devices  37.9 us (28%)
  local copies, waits for them, and re-layouts  10.4 us (8%)
  other arithmetic  3.17 us (2%)
  between operations  2.77 us (2%)
    all_to_all x2, waiting for transfers between devices, exchange(): return lax.all_to_all(blocks, AXES, 0, 0, tiled=True)  18.9 us
    pallas_call x3, Pallas kernels, scored(): pl.pallas_call(functools.partial(score_kernel, start, count, wraps, len(e...  18.4 us
    ppermute x3, waiting for transfers between devices, local(): packed.append((own, lax.ppermute(own, 'member', [(0, 1), (1, 0)])))  17 us
    all_to_all x2, starting transfers between devices, exchange(): return lax.all_to_all(blocks, AXES, 0, 0, tiled=True)  17 us
    pallas_call x3, Pallas kernels, forward(): pl.pallas_call(functools.partial(forward_kernel, start, count, wraps, len...  14.1 us
    ppermute x4, starting transfers between devices, swapped(): near = lax.ppermute(jnp.where(even, last, first), axis, both[0])  12.7 us
    pallas_call x1, Pallas kernels, backward(): pl.pallas_call(functools.partial(backward_kernel, block), grid=(columns /...  7.75 us
    unnamed x18, local copies, waits for them, and re-layouts  6.86 us
  transfers between devices with their start and end apart: 13, of which 4 were waited for; matrix products, arithmetic and copies ran while one was open for 2% of the time, Pallas kernels for 18%

profile of v6, /device:TPU:1, one launch (start us, length us, event | category | flops | bytes accessed | tf_op | source)
XLA Modules:
  0.0 135.2 jit_solution(3479141514578747669)
XLA Ops:
  0.6 1.0 broadcast_select_fusion.14
  1.6 2.1 %collective-permute-start = (bf16[45,1,128]{2,1,0:T(2,128)(2,1)S(1)}, bf16[45,1,128]{2,1,0:T(2,128)(2,1)S(1)}, u32[]{:S(2)}, u32[]{:S(2)}) collective-permute-start(bf16[45,1,128]{2,1,0:T(2,128)(2,1)S(1)} %get-tuple-element.53), channel_id=1, source_target_pairs={{0,32},{64,96},{32,0},{96,64},{1,33},{65,97},{33,1},{97,65},{2,34}... | collective-permute-start | bytes 34568 | tf_op jit(solution)/shard_map/ppermute | solution.py:33
  3.8 0.7 collective-permute-start.1
  4.4 0.8 fusion.1
  5.2 0.9 slice.90
  6.2 0.1 pad.31.clone
  6.3 0.1 pad.27.clone
  6.4 0.1 maximum_maximum_fusion.refs_1_
  6.6 0.0 copy-start
  6.6 1.6 %copy-done = bf16[1,180,45,128]{3,1,2,0:T(8,128)(2,1)S(1)} copy-done((bf16[1,180,45,128]{3,1,2,0:T(8,128)(2,1)S(1)}, bf16[1,180,45,128]{3,1,2,0:T(8,128)(2,1)}, u32[]{:S(2)}) %copy-start) | copy-done | bytes 2073624
  8.2 1.5 %copy-done.2 = bf16[1,180,45,80]{1,3,2,0:T(8,128)(2,1)S(1)} copy-done((bf16[1,180,45,80]{1,3,2,0:T(8,128)(2,1)S(1)}, bf16[1,180,45,80]{1,3,2,0:T(8,128)(2,1)}, u32[]{:S(2)}) %copy-start.2) | copy-done | bytes 1296024
  9.7 0.9 copy-done.7
  10.6 4.3 %forward.3 = (bf16[45,80,180]{2,1,0:T(8,128)(2,1)}, bf16[18,80,128]{2,1,0:T(8,128)(2,1)}) custom-call(bf16[45,180,128]{2,1,0:T(8,128)(2,1)S(1)} %bitcast.24, bf16[45,16,128]{2,1,0:T(8,128)(2,1)S(1)} %maximum_maximum_fusion.refs_1_, bf16[45,16,128]{2,1,0:T(8,128)(2,1)S(1)} %concatenate.60.refs_2_, bf16[45,80,180]{2,1,0:T(8,128)(2,1)S(1)} %bitcast.30, ...), custom_call_target="tpu_custom_call" | custom-call | flops 566231040 | bytes 2260992 | tf_op jit(solution)/shard_map/forward/pallas_call | solution.py:159
  14.9 0.1 pad_maximum_fusion.1
  15.0 5.5 %forward.4 = (bf16[45,80,180]{2,1,0:T(8,128)(2,1)}, bf16[30,80,128]{2,1,0:T(8,128)(2,1)S(1)}) custom-call(bf16[45,180,128]{2,1,0:T(8,128)(2,1)S(1)} %bitcast.25, bf16[45,16,128]{2,1,0:T(8,128)(2,1)S(1)} %maximum_maximum_fusion.refs_1_, bf16[45,16,128]{2,1,0:T(8,128)(2,1)S(1)} %concatenate.60.refs_2_, ...), custom_call_target="tpu_custom_call", output_to_operand_aliasing={{0}: (5, {})} | custom-call | flops 943718400 | bytes 3768320 | tf_op jit(solution)/shard_map/forward/pallas_call | solution.py:159
  20.5 3.8 %collective-permute-start.2 = (bf16[1,256,128]{2,1,0:T(8,128)(2,1)S(1)}, bf16[1,256,128]{2,1,0:T(8,128)(2,1)S(1)}, u32[]{:S(2)}, u32[]{:S(2)}) collective-permute-start(bf16[1,256,128]{2,1,0:T(8,128)(2,1)S(1)} %get-tuple-element.63), channel_id=1, source_target_pairs={{1,2},{3,4},{5,6},{7,8},{9,10},{11,12},{13,14},{15,16},{17,18},{19... | collective-permute-start | bytes 196616 | tf_op jit(solution)/shard_map/ppermute | solution.py:34
  24.4 4.8 %collective-permute-start.3 = (bf16[1,256,128]{2,1,0:T(8,128)(2,1)S(1)}, bf16[1,256,128]{2,1,0:T(8,128)(2,1)S(1)}, u32[]{:S(2)}, u32[]{:S(2)}) collective-permute-start(bf16[1,256,128]{2,1,0:T(8,128)(2,1)S(1)} %get-tuple-element.62), channel_id=1, source_target_pairs={{0,1},{2,3},{4,5},{6,7},{8,9},{10,11},{12,13},{14,15},{16,17},{18,... | collective-permute-start | bytes 196616 | tf_op jit(solution)/shard_map/ppermute | solution.py:33
  29.2 0.4 collective-permute-start.5
  29.6 1.1 collective-permute-start.6
  30.7 0.0 copy-start.1
  30.7 4.3 %forward.5 = (bf16[45,80,180]{2,1,0:T(8,128)(2,1)}, bf16[20,80,128]{2,1,0:T(8,128)(2,1)}) custom-call(bf16[45,180,128]{2,1,0:T(8,128)(2,1)S(1)} %bitcast.26, bf16[45,16,128]{2,1,0:T(8,128)(2,1)S(1)} %maximum_maximum_fusion.refs_1_, bf16[45,16,128]{2,1,0:T(8,128)(2,1)S(1)} %concatenate.60.refs_2_, ...), custom_call_target="tpu_custom_call", output_to_operand_aliasing={{0}: (7, {})} | custom-call | flops 613416960 | bytes 2449408 | tf_op jit(solution)/shard_map/forward/pallas_call | solution.py:159
  35.0 0.5 collective-permute-start.4
  35.6 0.1 pad_maximum_fusion.4
  35.7 17.0 %collective-permute-done.6.refs_4_ = bf16[18,80,128]{2,1,0:T(8,128)(2,1)} collective-permute-done((bf16[18,80,128]{2,1,0:T(8,128)(2,1)}, bf16[18,80,128]{2,1,0:T(8,128)(2,1)}, u32[]{:S(2)}, u32[]{:S(2)}) %collective-permute-start.6) | collective-permute-done | bytes 368672 | tf_op jit(solution)/shard_map/ppermute | solution.py:400
  52.7 1.5 %copy-done.3 = bf16[180,45,80]{0,2,1:T(8,128)(2,1)S(1)} copy-done((bf16[180,45,80]{0,2,1:T(8,128)(2,1)S(1)}, bf16[180,45,80]{0,2,1:T(8,128)(2,1)}, u32[]{:S(2)}) %copy-start.3) | copy-done | bytes 1296024
  54.2 5.0 %score.3 = (bf16[45,180,128]{2,1,0:T(8,128)(2,1)S(1)}, f32[768,128]{1,0:T(8,128)S(1)}) custom-call(bf16[45,180,128]{2,1,0:T(8,128)(2,1)S(1)} %bitcast.27, bf16[45,16,128]{2,1,0:T(8,128)(2,1)S(1)} %maximum_maximum_fusion.refs_1_, bf16[45,16,128]{2,1,0:T(8,128)(2,1)S(1)} %concatenate.60.refs_2_, bf16[18,80,128]{2,1,0:T(8,128)(2,1)} %get-tuple-element.36.refs_3_, ...), custom_call_target="tpu_custom_call" | custom-call | flops 566231040 | bytes 2260992 | tf_op jit(solution)/shard_map/score/pallas_call | solution.py:270
  59.3 7.3 %score.4 = (bf16[45,180,128]{2,1,0:T(8,128)(2,1)S(1)}, f32[768,128]{1,0:T(8,128)S(1)}) custom-call(bf16[45,180,128]{2,1,0:T(8,128)(2,1)S(1)} %bitcast.28, bf16[45,16,128]{2,1,0:T(8,128)(2,1)S(1)} %maximum_maximum_fusion.refs_1_, bf16[45,16,128]{2,1,0:T(8,128)(2,1)S(1)} %concatenate.60.refs_2_, ...), custom_call_target="tpu_custom_call", output_to_operand_aliasing={{0}: (8, {})} | custom-call | flops 943718400 | bytes 3768320 | tf_op jit(solution)/shard_map/score/pallas_call | solution.py:270
  66.5 6.1 %score.5 = (bf16[45,180,128]{2,1,0:T(8,128)(2,1)S(1)}, f32[768,128]{1,0:T(8,128)}) custom-call(bf16[45,180,128]{2,1,0:T(8,128)(2,1)S(1)} %bitcast.29, bf16[45,16,128]{2,1,0:T(8,128)(2,1)S(1)} %maximum_maximum_fusion.refs_1_, bf16[45,16,128]{2,1,0:T(8,128)(2,1)S(1)} %concatenate.60.refs_2_, ...), custom_call_target="tpu_custom_call", output_to_operand_aliasing={{0}: (10, {})} | custom-call | flops 613416960 | bytes 2449408 | tf_op jit(solution)/shard_map/score/pallas_call | solution.py:270
  72.7 0.0 copy-start.8
  72.7 0.1 broadcast_select_fusion.11
  72.7 3.5 %collective-permute-start.7 = (bf16[45,1,128]{2,1,0:T(2,128)(2,1)S(1)}, bf16[45,1,128]{2,1,0:T(2,128)(2,1)S(1)}, u32[]{:S(2)}, u32[]{:S(2)}) collective-permute-start(bf16[45,1,128]{2,1,0:T(2,128)(2,1)S(1)} %get-tuple-element.48), channel_id=1, source_target_pairs={{0,32},{64,96},{32,0},{96,64},{1,33},{65,97},{33,1},{97,65},{2,34}... | collective-permute-start | bytes 34568 | tf_op jit(solution)/shard_map/ppermute | solution.py:33
  76.2 0.7 collective-permute-start.8
  76.9 1.3 copy-done.5
  78.2 10.4 %all-to-all-start = ((f32[256,1,384]{2,1,0:T(1,128)}), f32[256,1,384]{2,1,0:T(1,128)S(1)}, u32[]{:S(2)}, u32[]{:S(2)}) async-start(f32[256,1,384]{2,1,0:T(1,128)} %bitcast.11), calls=%async_computation | async-start | bytes 786432 | tf_op jit(solution)/shard_map/all_to_all | solution.py:359
  88.6 0.1 broadcast_select_fusion.9
  88.7 0.1 maximum_maximum_fusion.1.refs_1_
  88.8 0.1 broadcast_select_fusion.2
  88.9 2.2 %collective-permute-start.10 = (bf16[1,256,128]{2,1,0:T(8,128)(2,1)S(1)}, bf16[1,256,128]{2,1,0:T(8,128)(2,1)S(1)}, u32[]{:S(2)}, u32[]{:S(2)}) collective-permute-start(bf16[1,256,128]{2,1,0:T(8,128)(2,1)S(1)} %get-tuple-element.64), channel_id=1, source_target_pairs={{0,1},{2,3},{4,5},{6,7},{8,9},{10,11},{12,13},{14,15},{16,17},{18,... | collective-permute-start | bytes 196616 | tf_op jit(solution)/shard_map/ppermute | solution.py:33
  91.1 1.1 collective-permute-start.9
  92.3 4.8 %collective-permute-done.9 = bf16[1,256,128]{2,1,0:T(8,128)(2,1)S(1)} collective-permute-done((bf16[1,256,128]{2,1,0:T(8,128)(2,1)S(1)}, bf16[1,256,128]{2,1,0:T(8,128)(2,1)S(1)}, u32[]{:S(2)}, u32[]{:S(2)}) %collective-permute-start.9) | collective-permute-done | bytes 65568 | tf_op jit(solution)/shard_map/ppermute | solution.py:34
  97.1 9.2 %all-to-all-done = f32[256,1,384]{2,1,0:T(1,128)S(1)} async-done(((f32[256,1,384]{2,1,0:T(1,128)}), f32[256,1,384]{2,1,0:T(1,128)S(1)}, u32[]{:S(2)}, u32[]{:S(2)}) %all-to-all-start) | async-done | bytes 393248 | tf_op jit(solution)/shard_map/all_to_all | solution.py:359
  106.3 0.3 reduce_sum.9
  106.7 1.0 broadcast_in_dim.20
  107.6 6.7 %all-to-all-start.1 = ((f32[256,1,384]{2,1,0:T(1,128)}), f32[256,1,384]{2,1,0:T(1,128)S(1)}, u32[]{:S(2)}, u32[]{:S(2)}) async-start(f32[256,1,384]{2,1,0:T(1,128)} %broadcast_in_dim.20), calls=%async_computation.1 | async-start | bytes 786432 | tf_op jit(solution)/shard_map/all_to_all | solution.py:359
  114.4 7.8 %backward.1 = bf16[45,180,128]{2,1,0:T(8,128)(2,1)} custom-call(bf16[45,180,128]{2,1,0:T(8,128)(2,1)S(1)} %copy-done.6, bf16[45,16,128]{2,1,0:T(8,128)(2,1)S(1)} %maximum_maximum_fusion.1.refs_1_, bf16[45,16,128]{2,1,0:T(8,128)(2,1)S(1)} %concatenate.65.refs_2_, bf16[1,256,128]{2,1,0:T(8,128)(2,1)S(1)} %get-tuple-element.44.refs_3_, ...), custom_call_target="tpu_custom_call" | custom-call | flops 3397386240 | bytes 5898240 | tf_op jit(solution)/shard_map/backward/pallas_call | solution.py:339
  122.1 9.6 %all-to-all-done.1 = f32[256,1,384]{2,1,0:T(1,128)S(1)} async-done(((f32[256,1,384]{2,1,0:T(1,128)}), f32[256,1,384]{2,1,0:T(1,128)S(1)}, u32[]{:S(2)}, u32[]{:S(2)}) %all-to-all-start.1) | async-done | bytes 393248 | tf_op jit(solution)/shard_map/all_to_all | solution.py:359
  131.7 0.5 slice.99
  132.9 1.1 slice_multiply_fusion
  (38 shorter events, 0.4 us)
Async XLA Ops:
  1.6 4.7 %collective-permute-start = (bf16[45,1,128]{2,1,0:T(2,128)(2,1)S(1)}, bf16[45,1,128]{2,1,0:T(2,128)(2,1)S(1)}, u32[]{:S(2)}, u32[]{:S(2)}) collective-permute-start(bf16[45,1,128]{2,1,0:T(2,128)(2,1)S(1)} %get-tuple-element.53), channel_id=1, source_target_pairs={{0,32},{64,96},{32,0},{96,64},{1,33},{65,97},{33,1},{97,65},{2,34}... | collective-permute-start | bytes 34568 | tf_op jit(solution)/shard_map/ppermute | solution.py:33
  3.8 2.6 %collective-permute-start.1 = (bf16[45,1,128]{2,1,0:T(2,128)(2,1)S(1)}, bf16[45,1,128]{2,1,0:T(2,128)(2,1)S(1)}, u32[]{:S(2)}, u32[]{:S(2)}) collective-permute-start(bf16[45,1,128]{2,1,0:T(2,128)(2,1)S(1)} %get-tuple-element.52), channel_id=1, source_target_pairs={{32,64},{64,32},{33,65},{65,33},{34,66},{66,34},{35,67},{67,35},{3... | collective-permute-start | bytes 34568 | tf_op jit(solution)/shard_map/ppermute | solution.py:34
  6.6 1.6 %copy-start = (bf16[1,180,45,128]{3,1,2,0:T(8,128)(2,1)S(1)}, bf16[1,180,45,128]{3,1,2,0:T(8,128)(2,1)}, u32[]{:S(2)}) copy-start(bf16[1,180,45,128]{3,1,2,0:T(8,128)(2,1)} %param.4) | copy-start | bytes 6220804
  8.2 1.5 %copy-start.2 = (bf16[1,180,45,80]{1,3,2,0:T(8,128)(2,1)S(1)}, bf16[1,180,45,80]{1,3,2,0:T(8,128)(2,1)}, u32[]{:S(2)}) copy-start(bf16[1,180,45,80]{1,3,2,0:T(8,128)(2,1)} %param.5) | copy-start | bytes 3888004
  9.7 0.9 copy-start.7
  20.5 10.2 %collective-permute-start.2 = (bf16[1,256,128]{2,1,0:T(8,128)(2,1)S(1)}, bf16[1,256,128]{2,1,0:T(8,128)(2,1)S(1)}, u32[]{:S(2)}, u32[]{:S(2)}) collective-permute-start(bf16[1,256,128]{2,1,0:T(8,128)(2,1)S(1)} %get-tuple-element.63), channel_id=1, source_target_pairs={{1,2},{3,4},{5,6},{7,8},{9,10},{11,12},{13,14},{15,16},{17,18},{19... | collective-permute-start | bytes 196616 | tf_op jit(solution)/shard_map/ppermute | solution.py:34
  24.4 6.3 %collective-permute-start.3 = (bf16[1,256,128]{2,1,0:T(8,128)(2,1)S(1)}, bf16[1,256,128]{2,1,0:T(8,128)(2,1)S(1)}, u32[]{:S(2)}, u32[]{:S(2)}) collective-permute-start(bf16[1,256,128]{2,1,0:T(8,128)(2,1)S(1)} %get-tuple-element.62), channel_id=1, source_target_pairs={{0,1},{2,3},{4,5},{6,7},{8,9},{10,11},{12,13},{14,15},{16,17},{18,... | collective-permute-start | bytes 196616 | tf_op jit(solution)/shard_map/ppermute | solution.py:33
  29.2 30.0 %collective-permute-start.5 = (bf16[30,80,128]{2,1,0:T(8,128)(2,1)S(1)}, bf16[30,80,128]{2,1,0:T(8,128)(2,1)}, u32[]{:S(2)}, u32[]{:S(2)}) collective-permute-start(bf16[30,80,128]{2,1,0:T(8,128)(2,1)S(1)} %get-tuple-element.35.refs_3_), channel_id=1, source_target_pairs={{0,128},{128,0},{1,129},{129,1},{2,130},{130,2},{3,131},{131,3},{4... | collective-permute-start | bytes 1843208 | tf_op jit(solution)/shard_map/ppermute | solution.py:400
  29.6 23.1 %collective-permute-start.6 = (bf16[18,80,128]{2,1,0:T(8,128)(2,1)}, bf16[18,80,128]{2,1,0:T(8,128)(2,1)}, u32[]{:S(2)}, u32[]{:S(2)}) collective-permute-start(bf16[18,80,128]{2,1,0:T(8,128)(2,1)} %get-tuple-element.36.refs_3_), channel_id=1, source_target_pairs={{0,128},{128,0},{1,129},{129,1},{2,130},{130,2},{3,131},{131,3},{4... | collective-permute-start | bytes 1105928 | tf_op jit(solution)/shard_map/ppermute | solution.py:400
  30.7 22.0 %copy-start.1 = (bf16[1,180,45,128]{3,1,2,0:T(8,128)(2,1)S(1)}, bf16[1,180,45,128]{3,1,2,0:T(8,128)(2,1)}, u32[]{:S(2)}) copy-start(bf16[1,180,45,128]{3,1,2,0:T(8,128)(2,1)} %param.4) | copy-start | bytes 6220804
  35.0 31.5 %collective-permute-start.4 = (bf16[20,80,128]{2,1,0:T(8,128)(2,1)}, bf16[20,80,128]{2,1,0:T(8,128)(2,1)}, u32[]{:S(2)}, u32[]{:S(2)}) collective-permute-start(bf16[20,80,128]{2,1,0:T(8,128)(2,1)} %get-tuple-element.34.refs_3_), channel_id=1, source_target_pairs={{0,128},{128,0},{1,129},{129,1},{2,130},{130,2},{3,131},{131,3},{4... | collective-permute-start | bytes 1228808 | tf_op jit(solution)/shard_map/ppermute | solution.py:400
  52.7 1.5 %copy-start.3 = (bf16[180,45,80]{0,2,1:T(8,128)(2,1)S(1)}, bf16[180,45,80]{0,2,1:T(8,128)(2,1)}, u32[]{:S(2)}) copy-start(bf16[180,45,80]{0,2,1:T(8,128)(2,1)} %param.6) | copy-start | bytes 3888004
  54.2 5.1 %copy-start.4 = (bf16[180,45,80]{0,2,1:T(8,128)(2,1)S(1)}, bf16[180,45,80]{0,2,1:T(8,128)(2,1)}, u32[]{:S(2)}) copy-start(bf16[180,45,80]{0,2,1:T(8,128)(2,1)} %param.6) | copy-start | bytes 3888004
  72.7 41.7 %copy-start.8 = (bf16[3,3,128,80]{2,3,1,0:T(8,128)(2,1)S(1)}, bf16[3,3,128,80]{2,3,1,0:T(8,128)(2,1)}, u32[]{:S(2)}) copy-start(bf16[3,3,128,80]{2,3,1,0:T(8,128)(2,1)} %param.7) | copy-start | bytes 552964
  72.7 15.9 %collective-permute-start.7 = (bf16[45,1,128]{2,1,0:T(2,128)(2,1)S(1)}, bf16[45,1,128]{2,1,0:T(2,128)(2,1)S(1)}, u32[]{:S(2)}, u32[]{:S(2)}) collective-permute-start(bf16[45,1,128]{2,1,0:T(2,128)(2,1)S(1)} %get-tuple-element.48), channel_id=1, source_target_pairs={{0,32},{64,96},{32,0},{96,64},{1,33},{65,97},{33,1},{97,65},{2,34}... | collective-permute-start | bytes 34568 | tf_op jit(solution)/shard_map/ppermute | solution.py:33
  76.2 12.4 %collective-permute-start.8 = (bf16[45,1,128]{2,1,0:T(2,128)(2,1)S(1)}, bf16[45,1,128]{2,1,0:T(2,128)(2,1)S(1)}, u32[]{:S(2)}, u32[]{:S(2)}) collective-permute-start(bf16[45,1,128]{2,1,0:T(2,128)(2,1)S(1)} %get-tuple-element.49), channel_id=1, source_target_pairs={{32,64},{64,32},{33,65},{65,33},{34,66},{66,34},{35,67},{67,35},{3... | collective-permute-start | bytes 34568 | tf_op jit(solution)/shard_map/ppermute | solution.py:34
  76.9 1.3 copy-start.5
  78.2 36.1 %copy-start.6 = (bf16[45,180,128]{2,1,0:T(8,128)(2,1)S(1)}, bf16[45,180,128]{2,1,0:T(8,128)(2,1)}, u32[]{:S(2)}) copy-start(bf16[45,180,128]{2,1,0:T(8,128)(2,1)} %copy-done.5) | copy-start | bytes 6220804
  78.2 28.1 %all-to-all-start = ((f32[256,1,384]{2,1,0:T(1,128)}), f32[256,1,384]{2,1,0:T(1,128)S(1)}, u32[]{:S(2)}, u32[]{:S(2)}) async-start(f32[256,1,384]{2,1,0:T(1,128)} %bitcast.11), calls=%async_computation | async-start | bytes 786432 | tf_op jit(solution)/shard_map/all_to_all | solution.py:359
  88.9 3.4 %collective-permute-start.10 = (bf16[1,256,128]{2,1,0:T(8,128)(2,1)S(1)}, bf16[1,256,128]{2,1,0:T(8,128)(2,1)S(1)}, u32[]{:S(2)}, u32[]{:S(2)}) collective-permute-start(bf16[1,256,128]{2,1,0:T(8,128)(2,1)S(1)} %get-tuple-element.64), channel_id=1, source_target_pairs={{0,1},{2,3},{4,5},{6,7},{8,9},{10,11},{12,13},{14,15},{16,17},{18,... | collective-permute-start | bytes 196616 | tf_op jit(solution)/shard_map/ppermute | solution.py:33
  91.1 5.9 %collective-permute-start.9 = (bf16[1,256,128]{2,1,0:T(8,128)(2,1)S(1)}, bf16[1,256,128]{2,1,0:T(8,128)(2,1)S(1)}, u32[]{:S(2)}, u32[]{:S(2)}) collective-permute-start(bf16[1,256,128]{2,1,0:T(8,128)(2,1)S(1)} %get-tuple-element.65), channel_id=1, source_target_pairs={{1,2},{3,4},{5,6},{7,8},{9,10},{11,12},{13,14},{15,16},{17,18},{19... | collective-permute-start | bytes 196616 | tf_op jit(solution)/shard_map/ppermute | solution.py:34
  107.6 24.1 %all-to-all-start.1 = ((f32[256,1,384]{2,1,0:T(1,128)}), f32[256,1,384]{2,1,0:T(1,128)S(1)}, u32[]{:S(2)}, u32[]{:S(2)}) async-start(f32[256,1,384]{2,1,0:T(1,128)} %broadcast_in_dim.20), calls=%async_computation.1 | async-start | bytes 786432 | tf_op jit(solution)/shard_map/all_to_all | solution.py:359

commit v7 on v6

--- a/solution.py
+++ b/solution.py
@@ -388,25 +388,28 @@
     rings = lon_rings(*field)
     edges = None
     chunks = split(lon_cols)
-    pred = None
+    width = -(-(9 * outputs * inputs + 1) // (devices * LANES)) * LANES
+    sum_rows = devices * width // inputs
+    pred = carried = None
     packed = []
+
+    def score_next(carried, edges):
+        (start, count), (own, other) = packed.pop(0)
+        wraps = int(start + count == lon_cols)
+        return scored(
+            start, count, wraps, field, own, other, truth, weight, edges, carried, sum_rows
+        )
+
     for start, count in chunks:
         wraps = int(start + count == lon_cols)
         if wraps:
             edges = lon_edges(rings)
+            carried = score_next(carried, edges)
+            pred, carried = lax.optimization_barrier((pred, carried))
         pred, own = forward(start, count, wraps, field, present, taps, edges, pred)
-        if not wraps:
-            rings, own = lax.optimization_barrier((rings, own))
-        packed.append((own, lax.ppermute(own, "member", [(0, 1), (1, 0)])))
-
-    width = -(-(9 * outputs * inputs + 1) // (devices * LANES)) * LANES
-    sum_rows = devices * width // inputs
-    carried = None
-    for (start, count), (own, other) in zip(chunks, packed):
-        wraps = int(start + count == lon_cols)
-        carried = scored(
-            start, count, wraps, field, own, other, truth, weight, edges, carried, sum_rows
-        )
+        packed.append(((start, count), (own, lax.ppermute(own, "member", [(0, 1), (1, 0)]))))
+    while packed:
+        carried = score_next(carried, edges)
     turned, sums = carried
     share = jnp.sum(exchange(sums.reshape(devices, width)), axis=0, keepdims=True)
     field = (turned, *lat_edges(turned))

time: 136 us -> 120 us (0.88)
  waiting for transfers between devices: 40.7 us -> 32.7 us
  Pallas kernels: 40.2 us -> 35.3 us
  local copies, waits for them, and re-layouts: 10.4 us -> 7.53 us
    ppermute x3, waiting for transfers between devices: 17 us -> 9.03 us  [local(): lax.ppermute(own, 'member', [(0, 1), (1, 0)])]
    pallas_call x3, Pallas kernels: 18.4 us -> 15 us  [scored(): pl.pallas_call(functools.partial(score_kernel, start, count, wraps, len(e...]
    unnamed x18 -> x12, local copies, waits for them, and re-layouts: 6.86 us -> 4.03 us
    pallas_call x3, Pallas kernels: 14.1 us -> 12.6 us  [forward(): pl.pallas_call(functools.partial(forward_kernel, start, count, wraps, len...]
  transfers between devices with their start and end apart: 13 -> 13, of which waited for: 4 -> 5; matrix products, arithmetic and copies ran while one was open for 2% -> 2% of each run, Pallas kernels for 18% -> 22%
where the time goes in v7:
time: 120 us; the launch traced here: 119 us
  starting transfers between devices  37.7 us (31%)
  Pallas kernels  35.3 us (29%)
  waiting for transfers between devices  32.7 us (27%)
  local copies, waits for them, and re-layouts  7.53 us (6%)
  other arithmetic  3.16 us (3%)
  between operations  2.77 us (2%)
    all_to_all x2, waiting for transfers between devices, exchange(): return lax.all_to_all(blocks, AXES, 0, 0, tiled=True)  18.9 us
    all_to_all x2, starting transfers between devices, exchange(): return lax.all_to_all(blocks, AXES, 0, 0, tiled=True)  16 us
    pallas_call x3, Pallas kernels, scored(): pl.pallas_call(functools.partial(score_kernel, start, count, wraps, len(e...  15 us
    pallas_call x3, Pallas kernels, forward(): pl.pallas_call(functools.partial(forward_kernel, start, count, wraps, len...  12.6 us
    ppermute x4, starting transfers between devices, swapped(): near = lax.ppermute(jnp.where(even, last, first), axis, both[0])  12.4 us
    ppermute x3, waiting for transfers between devices, local(): lax.ppermute(own, 'member', [(0, 1), (1, 0)])  9.03 us
    pallas_call x1, Pallas kernels, backward(): pl.pallas_call(functools.partial(backward_kernel, block), grid=(columns /...  7.75 us
    ppermute x4, starting transfers between devices, swapped(): far = lax.ppermute(jnp.where(even, first, last), axis, both[1])  6.27 us
  transfers between devices with their start and end apart: 13, of which 5 were waited for; matrix products, arithmetic and copies ran while one was open for 2% of the time, Pallas kernels for 22%

profile of v7, /device:TPU:1, one launch (start us, length us, event | category | flops | bytes accessed | tf_op | source)
XLA Modules:
  0.0 119.2 jit_solution(18133886578868580651)
XLA Ops:
  0.6 1.0 broadcast_select_fusion.14
  1.6 2.1 %collective-permute-start = (bf16[45,1,128]{2,1,0:T(2,128)(2,1)S(1)}, bf16[45,1,128]{2,1,0:T(2,128)(2,1)S(1)}, u32[]{:S(2)}, u32[]{:S(2)}) collective-permute-start(bf16[45,1,128]{2,1,0:T(2,128)(2,1)S(1)} %get-tuple-element.47), channel_id=1, source_target_pairs={{0,32},{64,96},{32,0},{96,64},{1,33},{65,97},{33,1},{97,65},{2,34}... | collective-permute-start | bytes 34568 | tf_op jit(solution)/shard_map/ppermute | solution.py:33
  3.8 0.7 collective-permute-start.1
  4.5 0.8 fusion.1
  5.3 0.1 pad_maximum_fusion.4
  5.4 0.9 slice.90
  6.3 0.1 pad.31.clone
  6.4 0.1 pad.27.clone
  6.5 0.0 collective-permute-done
  6.6 0.1 maximum_maximum_fusion.refs_1_
  6.7 0.0 copy-start
  6.8 1.6 %copy-done = bf16[1,180,45,128]{3,1,2,0:T(8,128)(2,1)S(1)} copy-done((bf16[1,180,45,128]{3,1,2,0:T(8,128)(2,1)S(1)}, bf16[1,180,45,128]{3,1,2,0:T(8,128)(2,1)}, u32[]{:S(2)}) %copy-start) | copy-done | bytes 2073624
  8.3 1.5 %copy-done.1 = bf16[1,180,45,80]{1,3,2,0:T(8,128)(2,1)S(1)} copy-done((bf16[1,180,45,80]{1,3,2,0:T(8,128)(2,1)S(1)}, bf16[1,180,45,80]{1,3,2,0:T(8,128)(2,1)}, u32[]{:S(2)}) %copy-start.1) | copy-done | bytes 1296024
  9.8 0.9 copy-done.4
  10.8 3.6 %forward.3 = (bf16[45,80,180]{2,1,0:T(8,128)(2,1)}, bf16[18,80,128]{2,1,0:T(8,128)(2,1)S(1)}) custom-call(bf16[45,180,128]{2,1,0:T(8,128)(2,1)S(1)} %bitcast.24, bf16[45,16,128]{2,1,0:T(8,128)(2,1)S(1)} %maximum_maximum_fusion.refs_1_, bf16[45,16,128]{2,1,0:T(8,128)(2,1)S(1)} %concatenate.94.refs_2_, bf16[45,80,180]{2,1,0:T(8,128)(2,1)S(1)} %bitcast.30, ...), custom_call_target="tpu_custom_call" | custom-call | flops 566231040 | bytes 2260992 | tf_op jit(solution)/shard_map/forward/pallas_call | solution.py:159
  14.3 1.4 %collective-permute-start.4 = (bf16[18,80,128]{2,1,0:T(8,128)(2,1)S(1)}, bf16[18,80,128]{2,1,0:T(8,128)(2,1)S(1)}, u32[]{:S(2)}, u32[]{:S(2)}) collective-permute-start(bf16[18,80,128]{2,1,0:T(8,128)(2,1)S(1)} %get-tuple-element.24.refs_3_), channel_id=1, source_target_pairs={{0,128},{128,0},{1,129},{129,1},{2,130},{130,2},{3,131},{131,3},{4... | collective-permute-start | bytes 1105928 | tf_op jit(solution)/shard_map/ppermute | solution.py:410
  15.7 0.1 broadcast_select_fusion.6
  15.8 3.8 %collective-permute-start.2 = (bf16[1,256,128]{2,1,0:T(8,128)(2,1)S(1)}, bf16[1,256,128]{2,1,0:T(8,128)(2,1)S(1)}, u32[]{:S(2)}, u32[]{:S(2)}) collective-permute-start(bf16[1,256,128]{2,1,0:T(8,128)(2,1)S(1)} %get-tuple-element.59), channel_id=1, source_target_pairs={{1,2},{3,4},{5,6},{7,8},{9,10},{11,12},{13,14},{15,16},{17,18},{19... | collective-permute-start | bytes 196616 | tf_op jit(solution)/shard_map/ppermute | solution.py:34
  19.6 4.6 %collective-permute-start.3 = (bf16[1,256,128]{2,1,0:T(8,128)(2,1)S(1)}, bf16[1,256,128]{2,1,0:T(8,128)(2,1)S(1)}, u32[]{:S(2)}, u32[]{:S(2)}) collective-permute-start(bf16[1,256,128]{2,1,0:T(8,128)(2,1)S(1)} %get-tuple-element.58), channel_id=1, source_target_pairs={{0,1},{2,3},{4,5},{6,7},{8,9},{10,11},{12,13},{14,15},{16,17},{18,... | collective-permute-start | bytes 196616 | tf_op jit(solution)/shard_map/ppermute | solution.py:33
  24.2 5.5 %forward.4 = (bf16[45,80,180]{2,1,0:T(8,128)(2,1)}, bf16[30,80,128]{2,1,0:T(8,128)(2,1)S(1)}) custom-call(bf16[45,180,128]{2,1,0:T(8,128)(2,1)S(1)} %bitcast.25, bf16[45,16,128]{2,1,0:T(8,128)(2,1)S(1)} %maximum_maximum_fusion.refs_1_, bf16[45,16,128]{2,1,0:T(8,128)(2,1)S(1)} %concatenate.94.refs_2_, ...), custom_call_target="tpu_custom_call", output_to_operand_aliasing={{0}: (5, {})} | custom-call | flops 943718400 | bytes 3768320 | tf_op jit(solution)/shard_map/forward/pallas_call | solution.py:159
  29.7 0.1 collective-permute-start.6
  29.9 0.0 copy-start.2
  29.9 3.8 %score.3 = (bf16[45,180,128]{2,1,0:T(8,128)(2,1)S(1)}, f32[768,128]{1,0:T(8,128)S(1)}) custom-call(bf16[45,180,128]{2,1,0:T(8,128)(2,1)S(1)} %bitcast.26, bf16[45,16,128]{2,1,0:T(8,128)(2,1)S(1)} %maximum_maximum_fusion.refs_1_, bf16[45,16,128]{2,1,0:T(8,128)(2,1)S(1)} %concatenate.94.refs_2_, bf16[18,80,128]{2,1,0:T(8,128)(2,1)S(1)} %get-tuple-element.24.refs_3_, ...), custom_call_target="tpu_custom_call" | custom-call | flops 566231040 | bytes 2260992 | tf_op jit(solution)/shard_map/score/pallas_call | solution.py:270
  33.7 3.6 %forward.5 = (bf16[45,80,180]{2,1,0:T(8,128)(2,1)}, bf16[20,80,128]{2,1,0:T(8,128)(2,1)S(1)}) custom-call(bf16[45,180,128]{2,1,0:T(8,128)(2,1)S(1)} %bitcast.27, bf16[45,16,128]{2,1,0:T(8,128)(2,1)S(1)} %maximum_maximum_fusion.refs_1_, bf16[45,16,128]{2,1,0:T(8,128)(2,1)S(1)} %concatenate.94.refs_2_, ...), custom_call_target="tpu_custom_call", output_to_operand_aliasing={{0}: (7, {})} | custom-call | flops 613416960 | bytes 2449408 | tf_op jit(solution)/shard_map/forward/pallas_call | solution.py:159
  37.3 1.5 %collective-permute-start.5 = (bf16[20,80,128]{2,1,0:T(8,128)(2,1)S(1)}, bf16[20,80,128]{2,1,0:T(8,128)(2,1)S(1)}, u32[]{:S(2)}, u32[]{:S(2)}) collective-permute-start(bf16[20,80,128]{2,1,0:T(8,128)(2,1)S(1)} %get-tuple-element.29.refs_3_), channel_id=1, source_target_pairs={{0,128},{128,0},{1,129},{129,1},{2,130},{130,2},{3,131},{131,3},{4... | collective-permute-start | bytes 1228808 | tf_op jit(solution)/shard_map/ppermute | solution.py:410
  38.8 6.5 %collective-permute-done.6.refs_4_ = bf16[30,80,128]{2,1,0:T(8,128)(2,1)S(1)} collective-permute-done((bf16[30,80,128]{2,1,0:T(8,128)(2,1)S(1)}, bf16[30,80,128]{2,1,0:T(8,128)(2,1)S(1)}, u32[]{:S(2)}, u32[]{:S(2)}) %collective-permute-start.6) | collective-permute-done | bytes 614432 | tf_op jit(solution)/shard_map/ppermute | solution.py:410
  45.3 6.2 %score.4 = (bf16[45,180,128]{2,1,0:T(8,128)(2,1)S(1)}, f32[768,128]{1,0:T(8,128)S(1)}) custom-call(bf16[45,180,128]{2,1,0:T(8,128)(2,1)S(1)} %bitcast.28, bf16[45,16,128]{2,1,0:T(8,128)(2,1)S(1)} %maximum_maximum_fusion.refs_1_, bf16[45,16,128]{2,1,0:T(8,128)(2,1)S(1)} %concatenate.94.refs_2_, ...), custom_call_target="tpu_custom_call", output_to_operand_aliasing={{0}: (8, {})} | custom-call | flops 943718400 | bytes 3768320 | tf_op jit(solution)/shard_map/score/pallas_call | solution.py:270
  51.5 2.5 %collective-permute-done.5.refs_4_ = bf16[20,80,128]{2,1,0:T(8,128)(2,1)S(1)} collective-permute-done((bf16[20,80,128]{2,1,0:T(8,128)(2,1)S(1)}, bf16[20,80,128]{2,1,0:T(8,128)(2,1)S(1)}, u32[]{:S(2)}, u32[]{:S(2)}) %collective-permute-start.5) | collective-permute-done | bytes 409632 | tf_op jit(solution)/shard_map/ppermute | solution.py:410
  54.1 5.0 %score.5 = (bf16[45,180,128]{2,1,0:T(8,128)(2,1)S(1)}, f32[768,128]{1,0:T(8,128)}) custom-call(bf16[45,180,128]{2,1,0:T(8,128)(2,1)S(1)} %bitcast.29, bf16[45,16,128]{2,1,0:T(8,128)(2,1)S(1)} %maximum_maximum_fusion.refs_1_, bf16[45,16,128]{2,1,0:T(8,128)(2,1)S(1)} %concatenate.94.refs_2_, ...), custom_call_target="tpu_custom_call", output_to_operand_aliasing={{0}: (10, {})} | custom-call | flops 613416960 | bytes 2449408 | tf_op jit(solution)/shard_map/score/pallas_call | solution.py:270
  59.0 0.0 copy-start.5
  59.0 0.1 broadcast_select_fusion.11
  59.1 3.5 %collective-permute-start.7 = (bf16[45,1,128]{2,1,0:T(2,128)(2,1)S(1)}, bf16[45,1,128]{2,1,0:T(2,128)(2,1)S(1)}, u32[]{:S(2)}, u32[]{:S(2)}) collective-permute-start(bf16[45,1,128]{2,1,0:T(2,128)(2,1)S(1)} %get-tuple-element.42), channel_id=1, source_target_pairs={{0,32},{64,96},{32,0},{96,64},{1,33},{65,97},{33,1},{97,65},{2,34}... | collective-permute-start | bytes 34568 | tf_op jit(solution)/shard_map/ppermute | solution.py:33
  62.6 0.7 collective-permute-start.8
  63.3 9.5 %all-to-all-start = ((f32[256,1,384]{2,1,0:T(1,128)}), f32[256,1,384]{2,1,0:T(1,128)S(1)}, u32[]{:S(2)}, u32[]{:S(2)}) async-start(f32[256,1,384]{2,1,0:T(1,128)} %bitcast.11), calls=%async_computation | async-start | bytes 786432 | tf_op jit(solution)/shard_map/all_to_all | solution.py:359
  72.8 0.1 broadcast_select_fusion.9
  72.8 0.1 maximum_maximum_fusion.1.refs_1_
  72.9 0.1 broadcast_select_fusion.2
  73.1 2.2 %collective-permute-start.10 = (bf16[1,256,128]{2,1,0:T(8,128)(2,1)S(1)}, bf16[1,256,128]{2,1,0:T(8,128)(2,1)S(1)}, u32[]{:S(2)}, u32[]{:S(2)}) collective-permute-start(bf16[1,256,128]{2,1,0:T(8,128)(2,1)S(1)} %get-tuple-element.56), channel_id=1, source_target_pairs={{0,1},{2,3},{4,5},{6,7},{8,9},{10,11},{12,13},{14,15},{16,17},{18,... | collective-permute-start | bytes 196616 | tf_op jit(solution)/shard_map/ppermute | solution.py:33
  75.3 1.1 collective-permute-start.9
  76.4 4.8 %collective-permute-done.9 = bf16[1,256,128]{2,1,0:T(8,128)(2,1)S(1)} collective-permute-done((bf16[1,256,128]{2,1,0:T(8,128)(2,1)S(1)}, bf16[1,256,128]{2,1,0:T(8,128)(2,1)S(1)}, u32[]{:S(2)}, u32[]{:S(2)}) %collective-permute-start.9) | collective-permute-done | bytes 65568 | tf_op jit(solution)/shard_map/ppermute | solution.py:34
  81.2 9.3 %all-to-all-done = f32[256,1,384]{2,1,0:T(1,128)S(1)} async-done(((f32[256,1,384]{2,1,0:T(1,128)}), f32[256,1,384]{2,1,0:T(1,128)S(1)}, u32[]{:S(2)}, u32[]{:S(2)}) %all-to-all-start) | async-done | bytes 393248 | tf_op jit(solution)/shard_map/all_to_all | solution.py:359
  90.5 0.3 reduce_sum.9
  90.8 0.9 broadcast_in_dim.20
  91.8 6.6 %all-to-all-start.1 = ((f32[256,1,384]{2,1,0:T(1,128)}), f32[256,1,384]{2,1,0:T(1,128)S(1)}, u32[]{:S(2)}, u32[]{:S(2)}) async-start(f32[256,1,384]{2,1,0:T(1,128)} %broadcast_in_dim.20), calls=%async_computation.1 | async-start | bytes 786432 | tf_op jit(solution)/shard_map/all_to_all | solution.py:359
  98.4 7.7 %backward.1 = bf16[45,180,128]{2,1,0:T(8,128)(2,1)} custom-call(bf16[45,180,128]{2,1,0:T(8,128)(2,1)S(1)} %get-tuple-element.36.refs_0_, bf16[45,16,128]{2,1,0:T(8,128)(2,1)S(1)} %maximum_maximum_fusion.1.refs_1_, bf16[45,16,128]{2,1,0:T(8,128)(2,1)S(1)} %concatenate.100.refs_2_, bf16[1,256,128]{2,1,0:T(8,128)(2,1)S(1)} %get-tuple-element.38.refs_3_, ...), custom_call_target="tpu_custom_call" | custom-call | flops 3397386240 | bytes 5898240 | tf_op jit(solution)/shard_map/backward/pallas_call | solution.py:339
  106.2 9.7 %all-to-all-done.1 = f32[256,1,384]{2,1,0:T(1,128)S(1)} async-done(((f32[256,1,384]{2,1,0:T(1,128)}), f32[256,1,384]{2,1,0:T(1,128)S(1)}, u32[]{:S(2)}, u32[]{:S(2)}) %all-to-all-start.1) | async-done | bytes 393248 | tf_op jit(solution)/shard_map/all_to_all | solution.py:359
  115.8 0.5 slice.99
  117.0 1.1 slice_multiply_fusion
  (31 shorter events, 0.3 us)
Async XLA Ops:
  1.6 4.9 %collective-permute-start = (bf16[45,1,128]{2,1,0:T(2,128)(2,1)S(1)}, bf16[45,1,128]{2,1,0:T(2,128)(2,1)S(1)}, u32[]{:S(2)}, u32[]{:S(2)}) collective-permute-start(bf16[45,1,128]{2,1,0:T(2,128)(2,1)S(1)} %get-tuple-element.47), channel_id=1, source_target_pairs={{0,32},{64,96},{32,0},{96,64},{1,33},{65,97},{33,1},{97,65},{2,34}... | collective-permute-start | bytes 34568 | tf_op jit(solution)/shard_map/ppermute | solution.py:33
  3.8 2.7 %collective-permute-start.1 = (bf16[45,1,128]{2,1,0:T(2,128)(2,1)S(1)}, bf16[45,1,128]{2,1,0:T(2,128)(2,1)S(1)}, u32[]{:S(2)}, u32[]{:S(2)}) collective-permute-start(bf16[45,1,128]{2,1,0:T(2,128)(2,1)S(1)} %get-tuple-element.46), channel_id=1, source_target_pairs={{32,64},{64,32},{33,65},{65,33},{34,66},{66,34},{35,67},{67,35},{3... | collective-permute-start | bytes 34568 | tf_op jit(solution)/shard_map/ppermute | solution.py:34
  6.7 1.6 %copy-start = (bf16[1,180,45,128]{3,1,2,0:T(8,128)(2,1)S(1)}, bf16[1,180,45,128]{3,1,2,0:T(8,128)(2,1)}, u32[]{:S(2)}) copy-start(bf16[1,180,45,128]{3,1,2,0:T(8,128)(2,1)} %param.4) | copy-start | bytes 6220804
  8.3 1.5 %copy-start.1 = (bf16[1,180,45,80]{1,3,2,0:T(8,128)(2,1)S(1)}, bf16[1,180,45,80]{1,3,2,0:T(8,128)(2,1)}, u32[]{:S(2)}) copy-start(bf16[1,180,45,80]{1,3,2,0:T(8,128)(2,1)} %param.5) | copy-start | bytes 3888004
  9.8 0.9 copy-start.4
  14.3 15.5 %collective-permute-start.4 = (bf16[18,80,128]{2,1,0:T(8,128)(2,1)S(1)}, bf16[18,80,128]{2,1,0:T(8,128)(2,1)S(1)}, u32[]{:S(2)}, u32[]{:S(2)}) collective-permute-start(bf16[18,80,128]{2,1,0:T(8,128)(2,1)S(1)} %get-tuple-element.24.refs_3_), channel_id=1, source_target_pairs={{0,128},{128,0},{1,129},{129,1},{2,130},{130,2},{3,131},{131,3},{4... | collective-permute-start | bytes 1105928 | tf_op jit(solution)/shard_map/ppermute | solution.py:410
  15.8 14.0 %collective-permute-start.2 = (bf16[1,256,128]{2,1,0:T(8,128)(2,1)S(1)}, bf16[1,256,128]{2,1,0:T(8,128)(2,1)S(1)}, u32[]{:S(2)}, u32[]{:S(2)}) collective-permute-start(bf16[1,256,128]{2,1,0:T(8,128)(2,1)S(1)} %get-tuple-element.59), channel_id=1, source_target_pairs={{1,2},{3,4},{5,6},{7,8},{9,10},{11,12},{13,14},{15,16},{17,18},{19... | collective-permute-start | bytes 196616 | tf_op jit(solution)/shard_map/ppermute | solution.py:34
  19.6 10.2 %collective-permute-start.3 = (bf16[1,256,128]{2,1,0:T(8,128)(2,1)S(1)}, bf16[1,256,128]{2,1,0:T(8,128)(2,1)S(1)}, u32[]{:S(2)}, u32[]{:S(2)}) collective-permute-start(bf16[1,256,128]{2,1,0:T(8,128)(2,1)S(1)} %get-tuple-element.58), channel_id=1, source_target_pairs={{0,1},{2,3},{4,5},{6,7},{8,9},{10,11},{12,13},{14,15},{16,17},{18,... | collective-permute-start | bytes 196616 | tf_op jit(solution)/shard_map/ppermute | solution.py:33
  24.2 5.6 %copy-start.3 = (bf16[180,45,80]{0,2,1:T(8,128)(2,1)S(1)}, bf16[180,45,80]{0,2,1:T(8,128)(2,1)}, u32[]{:S(2)}) copy-start(bf16[180,45,80]{0,2,1:T(8,128)(2,1)} %param.6) | copy-start | bytes 3888004
  29.7 15.6 %collective-permute-start.6 = (bf16[30,80,128]{2,1,0:T(8,128)(2,1)S(1)}, bf16[30,80,128]{2,1,0:T(8,128)(2,1)S(1)}, u32[]{:S(2)}, u32[]{:S(2)}) collective-permute-start(bf16[30,80,128]{2,1,0:T(8,128)(2,1)S(1)} %get-tuple-element.30.refs_3_), channel_id=1, source_target_pairs={{0,128},{128,0},{1,129},{129,1},{2,130},{130,2},{3,131},{131,3},{4... | collective-permute-start | bytes 1843208 | tf_op jit(solution)/shard_map/ppermute | solution.py:410
  29.9 3.8 %copy-start.2 = (bf16[1,180,45,80]{1,3,2,0:T(8,128)(2,1)S(1)}, bf16[1,180,45,80]{1,3,2,0:T(8,128)(2,1)}, u32[]{:S(2)}) copy-start(bf16[1,180,45,80]{1,3,2,0:T(8,128)(2,1)} %param.5) | copy-start | bytes 3888004
  37.3 16.8 %collective-permute-start.5 = (bf16[20,80,128]{2,1,0:T(8,128)(2,1)S(1)}, bf16[20,80,128]{2,1,0:T(8,128)(2,1)S(1)}, u32[]{:S(2)}, u32[]{:S(2)}) collective-permute-start(bf16[20,80,128]{2,1,0:T(8,128)(2,1)S(1)} %get-tuple-element.29.refs_3_), channel_id=1, source_target_pairs={{0,128},{128,0},{1,129},{129,1},{2,130},{130,2},{3,131},{131,3},{4... | collective-permute-start | bytes 1228808 | tf_op jit(solution)/shard_map/ppermute | solution.py:410
  59.0 39.4 %copy-start.5 = (bf16[3,3,128,80]{2,3,1,0:T(8,128)(2,1)S(1)}, bf16[3,3,128,80]{2,3,1,0:T(8,128)(2,1)}, u32[]{:S(2)}) copy-start(bf16[3,3,128,80]{2,3,1,0:T(8,128)(2,1)} %param.7) | copy-start | bytes 552964
  59.1 13.6 %collective-permute-start.7 = (bf16[45,1,128]{2,1,0:T(2,128)(2,1)S(1)}, bf16[45,1,128]{2,1,0:T(2,128)(2,1)S(1)}, u32[]{:S(2)}, u32[]{:S(2)}) collective-permute-start(bf16[45,1,128]{2,1,0:T(2,128)(2,1)S(1)} %get-tuple-element.42), channel_id=1, source_target_pairs={{0,32},{64,96},{32,0},{96,64},{1,33},{65,97},{33,1},{97,65},{2,34}... | collective-permute-start | bytes 34568 | tf_op jit(solution)/shard_map/ppermute | solution.py:33
  62.6 10.2 %collective-permute-start.8 = (bf16[45,1,128]{2,1,0:T(2,128)(2,1)S(1)}, bf16[45,1,128]{2,1,0:T(2,128)(2,1)S(1)}, u32[]{:S(2)}, u32[]{:S(2)}) collective-permute-start(bf16[45,1,128]{2,1,0:T(2,128)(2,1)S(1)} %get-tuple-element.43), channel_id=1, source_target_pairs={{32,64},{64,32},{33,65},{65,33},{34,66},{66,34},{35,67},{67,35},{3... | collective-permute-start | bytes 34568 | tf_op jit(solution)/shard_map/ppermute | solution.py:34
  63.3 27.2 %all-to-all-start = ((f32[256,1,384]{2,1,0:T(1,128)}), f32[256,1,384]{2,1,0:T(1,128)S(1)}, u32[]{:S(2)}, u32[]{:S(2)}) async-start(f32[256,1,384]{2,1,0:T(1,128)} %bitcast.11), calls=%async_computation | async-start | bytes 786432 | tf_op jit(solution)/shard_map/all_to_all | solution.py:359
  73.1 3.4 %collective-permute-start.10 = (bf16[1,256,128]{2,1,0:T(8,128)(2,1)S(1)}, bf16[1,256,128]{2,1,0:T(8,128)(2,1)S(1)}, u32[]{:S(2)}, u32[]{:S(2)}) collective-permute-start(bf16[1,256,128]{2,1,0:T(8,128)(2,1)S(1)} %get-tuple-element.56), channel_id=1, source_target_pairs={{0,1},{2,3},{4,5},{6,7},{8,9},{10,11},{12,13},{14,15},{16,17},{18,... | collective-permute-start | bytes 196616 | tf_op jit(solution)/shard_map/ppermute | solution.py:33
  75.3 5.9 %collective-permute-start.9 = (bf16[1,256,128]{2,1,0:T(8,128)(2,1)S(1)}, bf16[1,256,128]{2,1,0:T(8,128)(2,1)S(1)}, u32[]{:S(2)}, u32[]{:S(2)}) collective-permute-start(bf16[1,256,128]{2,1,0:T(8,128)(2,1)S(1)} %get-tuple-element.57), channel_id=1, source_target_pairs={{1,2},{3,4},{5,6},{7,8},{9,10},{11,12},{13,14},{15,16},{17,18},{19... | collective-permute-start | bytes 196616 | tf_op jit(solution)/shard_map/ppermute | solution.py:34
  91.8 24.0 %all-to-all-start.1 = ((f32[256,1,384]{2,1,0:T(1,128)}), f32[256,1,384]{2,1,0:T(1,128)S(1)}, u32[]{:S(2)}, u32[]{:S(2)}) async-start(f32[256,1,384]{2,1,0:T(1,128)} %broadcast_in_dim.20), calls=%async_computation.1 | async-start | bytes 786432 | tf_op jit(solution)/shard_map/all_to_all | solution.py:359

commit v8 on v7

--- a/solution.py
+++ b/solution.py
@@ -360,7 +360,7 @@
 
 
 def split(columns):
-    shares = (12, 20, 13)
+    shares = (18, 16, 11)
     edges = [1]
     for i in range(len(shares) - 1):
         edges.append(1 + 2 * round(columns * sum(shares[: i + 1]) / sum(shares) / 2))

time: 120 us -> 121 us (level)
  starting transfers between devices: 37.7 us -> 40.8 us
  waiting for transfers between devices: 32.7 us -> 30.9 us
    ppermute x3, waiting for transfers between devices: 9.03 us -> 1.32 us  [local(): lax.ppermute(own, 'member', [(0, 1), (1, 0)])]
    ppermute x4, waiting for transfers between devices: 4.79 us -> 10.6 us  [swapped(): far = lax.ppermute(jnp.where(even, first, last), axis, both[1])]
    all_to_all x2, starting transfers between devices: 16 us -> 20.5 us  [exchange(): return lax.all_to_all(blocks, AXES, 0, 0, tiled=True)]
    ppermute x3, starting transfers between devices: 3 us -> 1.57 us  [local(): lax.ppermute(own, 'member', [(0, 1), (1, 0)])]
where the time goes in v8:
time: 121 us; the launch traced here: 120 us
  starting transfers between devices  40.8 us (34%)
  Pallas kernels  35.3 us (29%)
  waiting for transfers between devices  30.9 us (26%)
  local copies, waits for them, and re-layouts  7.53 us (6%)
  other arithmetic  3.16 us (3%)
  between operations  2.76 us (2%)
    all_to_all x2, starting transfers between devices, exchange(): return lax.all_to_all(blocks, AXES, 0, 0, tiled=True)  20.5 us
    all_to_all x2, waiting for transfers between devices, exchange(): return lax.all_to_all(blocks, AXES, 0, 0, tiled=True)  18.9 us
    pallas_call x3, Pallas kernels, scored(): pl.pallas_call(functools.partial(score_kernel, start, count, wraps, len(e...  15 us
    pallas_call x3, Pallas kernels, forward(): pl.pallas_call(functools.partial(forward_kernel, start, count, wraps, len...  12.6 us
    ppermute x4, starting transfers between devices, swapped(): near = lax.ppermute(jnp.where(even, last, first), axis, both[0])  12.5 us
    ppermute x4, waiting for transfers between devices, swapped(): far = lax.ppermute(jnp.where(even, first, last), axis, both[1])  10.6 us
    pallas_call x1, Pallas kernels, backward(): pl.pallas_call(functools.partial(backward_kernel, block), grid=(columns /...  7.75 us
    ppermute x4, starting transfers between devices, swapped(): far = lax.ppermute(jnp.where(even, first, last), axis, both[1])  6.28 us
  transfers between devices with their start and end apart: 13, of which 5 were waited for; matrix products, arithmetic and copies ran while one was open for 2% of the time, Pallas kernels for 22%

profile of v8, /device:TPU:1, one launch (start us, length us, event | category | flops | bytes accessed | tf_op | source)
XLA Modules:
  0.0 120.5 jit_solution(3040308255834268382)
XLA Ops:
  0.6 1.0 broadcast_select_fusion.14
  1.6 2.1 %collective-permute-start = (bf16[45,1,128]{2,1,0:T(2,128)(2,1)S(1)}, bf16[45,1,128]{2,1,0:T(2,128)(2,1)S(1)}, u32[]{:S(2)}, u32[]{:S(2)}) collective-permute-start(bf16[45,1,128]{2,1,0:T(2,128)(2,1)S(1)} %get-tuple-element.47), channel_id=1, source_target_pairs={{0,32},{64,96},{32,0},{96,64},{1,33},{65,97},{33,1},{97,65},{2,34}... | collective-permute-start | bytes 34568 | tf_op jit(solution)/shard_map/ppermute | solution.py:33
  3.8 0.7 collective-permute-start.1
  4.5 0.8 fusion.1
  5.3 0.1 pad_maximum_fusion.4
  5.4 0.9 slice.90
  6.3 0.1 pad.31.clone
  6.4 0.1 pad.27.clone
  6.5 0.0 collective-permute-done
  6.6 0.1 maximum_maximum_fusion.refs_1_
  6.7 0.0 copy-start
  6.7 1.6 %copy-done = bf16[1,180,45,128]{3,1,2,0:T(8,128)(2,1)S(1)} copy-done((bf16[1,180,45,128]{3,1,2,0:T(8,128)(2,1)S(1)}, bf16[1,180,45,128]{3,1,2,0:T(8,128)(2,1)}, u32[]{:S(2)}) %copy-start) | copy-done | bytes 2073624
  8.3 1.5 %copy-done.2 = bf16[1,180,45,80]{1,3,2,0:T(8,128)(2,1)S(1)} copy-done((bf16[1,180,45,80]{1,3,2,0:T(8,128)(2,1)S(1)}, bf16[1,180,45,80]{1,3,2,0:T(8,128)(2,1)}, u32[]{:S(2)}) %copy-start.2) | copy-done | bytes 1296024
  9.8 0.9 copy-done.4
  10.8 5.0 %forward.3 = (bf16[45,80,180]{2,1,0:T(8,128)(2,1)}, bf16[27,80,128]{2,1,0:T(8,128)(2,1)S(1)}) custom-call(bf16[45,180,128]{2,1,0:T(8,128)(2,1)S(1)} %bitcast.24, bf16[45,16,128]{2,1,0:T(8,128)(2,1)S(1)} %maximum_maximum_fusion.refs_1_, bf16[45,16,128]{2,1,0:T(8,128)(2,1)S(1)} %concatenate.94.refs_2_, bf16[45,80,180]{2,1,0:T(8,128)(2,1)S(1)} %bitcast.33, ...), custom_call_target="tpu_custom_call" | custom-call | flops 849346560 | bytes 3391488 | tf_op jit(solution)/shard_map/forward/pallas_call | solution.py:159
  15.8 1.4 %collective-permute-start.4 = (bf16[27,80,128]{2,1,0:T(8,128)(2,1)S(1)}, bf16[27,80,128]{2,1,0:T(8,128)(2,1)S(1)}, u32[]{:S(2)}, u32[]{:S(2)}) collective-permute-start(bf16[27,80,128]{2,1,0:T(8,128)(2,1)S(1)} %get-tuple-element.24.refs_3_), channel_id=1, source_target_pairs={{0,128},{128,0},{1,129},{129,1},{2,130},{130,2},{3,131},{131,3},{4... | collective-permute-start | bytes 1658888 | tf_op jit(solution)/shard_map/ppermute | solution.py:410
  17.1 0.1 broadcast_select_fusion.6
  17.3 3.8 %collective-permute-start.2 = (bf16[1,256,128]{2,1,0:T(8,128)(2,1)S(1)}, bf16[1,256,128]{2,1,0:T(8,128)(2,1)S(1)}, u32[]{:S(2)}, u32[]{:S(2)}) collective-permute-start(bf16[1,256,128]{2,1,0:T(8,128)(2,1)S(1)} %get-tuple-element.59), channel_id=1, source_target_pairs={{1,2},{3,4},{5,6},{7,8},{9,10},{11,12},{13,14},{15,16},{17,18},{19... | collective-permute-start | bytes 196616 | tf_op jit(solution)/shard_map/ppermute | solution.py:34
  21.1 4.6 %collective-permute-start.3 = (bf16[1,256,128]{2,1,0:T(8,128)(2,1)S(1)}, bf16[1,256,128]{2,1,0:T(8,128)(2,1)S(1)}, u32[]{:S(2)}, u32[]{:S(2)}) collective-permute-start(bf16[1,256,128]{2,1,0:T(8,128)(2,1)S(1)} %get-tuple-element.58), channel_id=1, source_target_pairs={{0,1},{2,3},{4,5},{6,7},{8,9},{10,11},{12,13},{14,15},{16,17},{18,... | collective-permute-start | bytes 196616 | tf_op jit(solution)/shard_map/ppermute | solution.py:33
  25.6 4.5 %forward.4 = (bf16[45,80,180]{2,1,0:T(8,128)(2,1)}, bf16[24,80,128]{2,1,0:T(8,128)(2,1)S(1)}) custom-call(bf16[45,180,128]{2,1,0:T(8,128)(2,1)S(1)} %bitcast.25, bf16[45,16,128]{2,1,0:T(8,128)(2,1)S(1)} %maximum_maximum_fusion.refs_1_, bf16[45,16,128]{2,1,0:T(8,128)(2,1)S(1)} %concatenate.94.refs_2_, ...), custom_call_target="tpu_custom_call", output_to_operand_aliasing={{0}: (5, {})} | custom-call | flops 754974720 | bytes 3014656 | tf_op jit(solution)/shard_map/forward/pallas_call | solution.py:159
  30.2 0.1 collective-permute-start.6
  30.3 5.9 %collective-permute-done.2 = bf16[1,256,128]{2,1,0:T(8,128)(2,1)S(1)} collective-permute-done((bf16[1,256,128]{2,1,0:T(8,128)(2,1)S(1)}, bf16[1,256,128]{2,1,0:T(8,128)(2,1)S(1)}, u32[]{:S(2)}, u32[]{:S(2)}) %collective-permute-start.2) | collective-permute-done | bytes 65568 | tf_op jit(solution)/shard_map/ppermute | solution.py:34
  36.2 0.0 copy-start.3
  36.2 5.6 %score.3 = (bf16[45,180,128]{2,1,0:T(8,128)(2,1)S(1)}, f32[768,128]{1,0:T(8,128)S(1)}) custom-call(bf16[45,180,128]{2,1,0:T(8,128)(2,1)S(1)} %bitcast.26, bf16[45,16,128]{2,1,0:T(8,128)(2,1)S(1)} %maximum_maximum_fusion.refs_1_, bf16[45,16,128]{2,1,0:T(8,128)(2,1)S(1)} %concatenate.94.refs_2_, bf16[27,80,128]{2,1,0:T(8,128)(2,1)S(1)} %get-tuple-element.24.refs_3_, ...), custom_call_target="tpu_custom_call" | custom-call | flops 849346560 | bytes 3391488 | tf_op jit(solution)/shard_map/score/pallas_call | solution.py:270
  41.8 3.1 %forward.5 = (bf16[45,80,180]{2,1,0:T(8,128)(2,1)}, bf16[17,80,128]{2,1,0:T(8,128)(2,1)S(1)}) custom-call(bf16[45,180,128]{2,1,0:T(8,128)(2,1)S(1)} %bitcast.27, bf16[45,16,128]{2,1,0:T(8,128)(2,1)S(1)} %maximum_maximum_fusion.refs_1_, bf16[45,16,128]{2,1,0:T(8,128)(2,1)S(1)} %concatenate.94.refs_2_, ...), custom_call_target="tpu_custom_call", output_to_operand_aliasing={{0}: (7, {})} | custom-call | flops 519045120 | bytes 2072576 | tf_op jit(solution)/shard_map/forward/pallas_call | solution.py:159
  44.9 0.1 collective-permute-start.5
  45.0 5.0 %score.4 = (bf16[45,180,128]{2,1,0:T(8,128)(2,1)S(1)}, f32[768,128]{1,0:T(8,128)S(1)}) custom-call(bf16[45,180,128]{2,1,0:T(8,128)(2,1)S(1)} %bitcast.28, bf16[45,16,128]{2,1,0:T(8,128)(2,1)S(1)} %maximum_maximum_fusion.refs_1_, bf16[45,16,128]{2,1,0:T(8,128)(2,1)S(1)} %concatenate.94.refs_2_, ...), custom_call_target="tpu_custom_call", output_to_operand_aliasing={{0}: (8, {})} | custom-call | flops 754974720 | bytes 3014656 | tf_op jit(solution)/shard_map/score/pallas_call | solution.py:270
  50.0 1.3 %collective-permute-done.5.refs_4_ = bf16[17,80,128]{2,1,0:T(8,128)(2,1)S(1)} collective-permute-done((bf16[17,80,128]{2,1,0:T(8,128)(2,1)S(1)}, bf16[17,80,128]{2,1,0:T(8,128)(2,1)S(1)}, u32[]{:S(2)}, u32[]{:S(2)}) %collective-permute-start.5) | collective-permute-done | bytes 348192 | tf_op jit(solution)/shard_map/ppermute | solution.py:410
  51.3 4.4 %score.5 = (bf16[45,180,128]{2,1,0:T(8,128)(2,1)S(1)}, f32[768,128]{1,0:T(8,128)}) custom-call(bf16[45,180,128]{2,1,0:T(8,128)(2,1)S(1)} %bitcast.29, bf16[45,16,128]{2,1,0:T(8,128)(2,1)S(1)} %maximum_maximum_fusion.refs_1_, bf16[45,16,128]{2,1,0:T(8,128)(2,1)S(1)} %concatenate.94.refs_2_, ...), custom_call_target="tpu_custom_call", output_to_operand_aliasing={{0}: (10, {})} | custom-call | flops 519045120 | bytes 2072576 | tf_op jit(solution)/shard_map/score/pallas_call | solution.py:270
  55.7 0.0 copy-start.5
  55.7 0.1 broadcast_select_fusion.11
  55.8 3.5 %collective-permute-start.7 = (bf16[45,1,128]{2,1,0:T(2,128)(2,1)S(1)}, bf16[45,1,128]{2,1,0:T(2,128)(2,1)S(1)}, u32[]{:S(2)}, u32[]{:S(2)}) collective-permute-start(bf16[45,1,128]{2,1,0:T(2,128)(2,1)S(1)} %get-tuple-element.42), channel_id=1, source_target_pairs={{0,32},{64,96},{32,0},{96,64},{1,33},{65,97},{33,1},{97,65},{2,34}... | collective-permute-start | bytes 34568 | tf_op jit(solution)/shard_map/ppermute | solution.py:33
  59.3 0.7 collective-permute-start.8
  60.0 14.0 %all-to-all-start = ((f32[256,1,384]{2,1,0:T(1,128)}), f32[256,1,384]{2,1,0:T(1,128)S(1)}, u32[]{:S(2)}, u32[]{:S(2)}) async-start(f32[256,1,384]{2,1,0:T(1,128)} %bitcast.11), calls=%async_computation | async-start | bytes 786432 | tf_op jit(solution)/shard_map/all_to_all | solution.py:359
  74.0 0.1 broadcast_select_fusion.9
  74.1 0.1 maximum_maximum_fusion.1.refs_1_
  74.2 0.1 broadcast_select_fusion.2
  74.3 2.2 %collective-permute-start.10 = (bf16[1,256,128]{2,1,0:T(8,128)(2,1)S(1)}, bf16[1,256,128]{2,1,0:T(8,128)(2,1)S(1)}, u32[]{:S(2)}, u32[]{:S(2)}) collective-permute-start(bf16[1,256,128]{2,1,0:T(8,128)(2,1)S(1)} %get-tuple-element.56), channel_id=1, source_target_pairs={{0,1},{2,3},{4,5},{6,7},{8,9},{10,11},{12,13},{14,15},{16,17},{18,... | collective-permute-start | bytes 196616 | tf_op jit(solution)/shard_map/ppermute | solution.py:33
  76.5 1.1 collective-permute-start.9
  77.7 4.8 %collective-permute-done.9 = bf16[1,256,128]{2,1,0:T(8,128)(2,1)S(1)} collective-permute-done((bf16[1,256,128]{2,1,0:T(8,128)(2,1)S(1)}, bf16[1,256,128]{2,1,0:T(8,128)(2,1)S(1)}, u32[]{:S(2)}, u32[]{:S(2)}) %collective-permute-start.9) | collective-permute-done | bytes 65568 | tf_op jit(solution)/shard_map/ppermute | solution.py:34
  82.5 9.3 %all-to-all-done = f32[256,1,384]{2,1,0:T(1,128)S(1)} async-done(((f32[256,1,384]{2,1,0:T(1,128)}), f32[256,1,384]{2,1,0:T(1,128)S(1)}, u32[]{:S(2)}, u32[]{:S(2)}) %all-to-all-start) | async-done | bytes 393248 | tf_op jit(solution)/shard_map/all_to_all | solution.py:359
  91.7 0.3 reduce_sum.9
  92.1 0.9 broadcast_in_dim.20
  93.0 6.6 %all-to-all-start.1 = ((f32[256,1,384]{2,1,0:T(1,128)}), f32[256,1,384]{2,1,0:T(1,128)S(1)}, u32[]{:S(2)}, u32[]{:S(2)}) async-start(f32[256,1,384]{2,1,0:T(1,128)} %broadcast_in_dim.20), calls=%async_computation.1 | async-start | bytes 786432 | tf_op jit(solution)/shard_map/all_to_all | solution.py:359
  99.6 7.7 %backward.1 = bf16[45,180,128]{2,1,0:T(8,128)(2,1)} custom-call(bf16[45,180,128]{2,1,0:T(8,128)(2,1)S(1)} %get-tuple-element.36.refs_0_, bf16[45,16,128]{2,1,0:T(8,128)(2,1)S(1)} %maximum_maximum_fusion.1.refs_1_, bf16[45,16,128]{2,1,0:T(8,128)(2,1)S(1)} %concatenate.100.refs_2_, bf16[1,256,128]{2,1,0:T(8,128)(2,1)S(1)} %get-tuple-element.38.refs_3_, ...), custom_call_target="tpu_custom_call" | custom-call | flops 3397386240 | bytes 5898240 | tf_op jit(solution)/shard_map/backward/pallas_call | solution.py:339
  107.4 9.7 %all-to-all-done.1 = f32[256,1,384]{2,1,0:T(1,128)S(1)} async-done(((f32[256,1,384]{2,1,0:T(1,128)}), f32[256,1,384]{2,1,0:T(1,128)S(1)}, u32[]{:S(2)}, u32[]{:S(2)}) %all-to-all-start.1) | async-done | bytes 393248 | tf_op jit(solution)/shard_map/all_to_all | solution.py:359
  117.0 0.5 slice.99
  118.2 1.1 slice_multiply_fusion
  (31 shorter events, 0.3 us)
Async XLA Ops:
  1.6 4.9 %collective-permute-start = (bf16[45,1,128]{2,1,0:T(2,128)(2,1)S(1)}, bf16[45,1,128]{2,1,0:T(2,128)(2,1)S(1)}, u32[]{:S(2)}, u32[]{:S(2)}) collective-permute-start(bf16[45,1,128]{2,1,0:T(2,128)(2,1)S(1)} %get-tuple-element.47), channel_id=1, source_target_pairs={{0,32},{64,96},{32,0},{96,64},{1,33},{65,97},{33,1},{97,65},{2,34}... | collective-permute-start | bytes 34568 | tf_op jit(solution)/shard_map/ppermute | solution.py:33
  3.8 2.7 %collective-permute-start.1 = (bf16[45,1,128]{2,1,0:T(2,128)(2,1)S(1)}, bf16[45,1,128]{2,1,0:T(2,128)(2,1)S(1)}, u32[]{:S(2)}, u32[]{:S(2)}) collective-permute-start(bf16[45,1,128]{2,1,0:T(2,128)(2,1)S(1)} %get-tuple-element.46), channel_id=1, source_target_pairs={{32,64},{64,32},{33,65},{65,33},{34,66},{66,34},{35,67},{67,35},{3... | collective-permute-start | bytes 34568 | tf_op jit(solution)/shard_map/ppermute | solution.py:34
  6.7 1.6 %copy-start = (bf16[1,180,45,128]{3,1,2,0:T(8,128)(2,1)S(1)}, bf16[1,180,45,128]{3,1,2,0:T(8,128)(2,1)}, u32[]{:S(2)}) copy-start(bf16[1,180,45,128]{3,1,2,0:T(8,128)(2,1)} %param.4) | copy-start | bytes 6220804
  8.3 1.5 %copy-start.2 = (bf16[1,180,45,80]{1,3,2,0:T(8,128)(2,1)S(1)}, bf16[1,180,45,80]{1,3,2,0:T(8,128)(2,1)}, u32[]{:S(2)}) copy-start(bf16[1,180,45,80]{1,3,2,0:T(8,128)(2,1)} %param.5) | copy-start | bytes 3888004
  9.8 0.9 copy-start.4
  15.8 20.4 %collective-permute-start.4 = (bf16[27,80,128]{2,1,0:T(8,128)(2,1)S(1)}, bf16[27,80,128]{2,1,0:T(8,128)(2,1)S(1)}, u32[]{:S(2)}, u32[]{:S(2)}) collective-permute-start(bf16[27,80,128]{2,1,0:T(8,128)(2,1)S(1)} %get-tuple-element.24.refs_3_), channel_id=1, source_target_pairs={{0,128},{128,0},{1,129},{129,1},{2,130},{130,2},{3,131},{131,3},{4... | collective-permute-start | bytes 1658888 | tf_op jit(solution)/shard_map/ppermute | solution.py:410
  17.3 18.9 %collective-permute-start.2 = (bf16[1,256,128]{2,1,0:T(8,128)(2,1)S(1)}, bf16[1,256,128]{2,1,0:T(8,128)(2,1)S(1)}, u32[]{:S(2)}, u32[]{:S(2)}) collective-permute-start(bf16[1,256,128]{2,1,0:T(8,128)(2,1)S(1)} %get-tuple-element.59), channel_id=1, source_target_pairs={{1,2},{3,4},{5,6},{7,8},{9,10},{11,12},{13,14},{15,16},{17,18},{19... | collective-permute-start | bytes 196616 | tf_op jit(solution)/shard_map/ppermute | solution.py:34
  21.1 15.0 %collective-permute-start.3 = (bf16[1,256,128]{2,1,0:T(8,128)(2,1)S(1)}, bf16[1,256,128]{2,1,0:T(8,128)(2,1)S(1)}, u32[]{:S(2)}, u32[]{:S(2)}) collective-permute-start(bf16[1,256,128]{2,1,0:T(8,128)(2,1)S(1)} %get-tuple-element.58), channel_id=1, source_target_pairs={{0,1},{2,3},{4,5},{6,7},{8,9},{10,11},{12,13},{14,15},{16,17},{18,... | collective-permute-start | bytes 196616 | tf_op jit(solution)/shard_map/ppermute | solution.py:33
  25.6 10.5 %copy-start.1 = (bf16[180,45,80]{0,2,1:T(8,128)(2,1)S(1)}, bf16[180,45,80]{0,2,1:T(8,128)(2,1)}, u32[]{:S(2)}) copy-start(bf16[180,45,80]{0,2,1:T(8,128)(2,1)} %param.6) | copy-start | bytes 3888004
  30.2 14.8 %collective-permute-start.6 = (bf16[24,80,128]{2,1,0:T(8,128)(2,1)S(1)}, bf16[24,80,128]{2,1,0:T(8,128)(2,1)S(1)}, u32[]{:S(2)}, u32[]{:S(2)}) collective-permute-start(bf16[24,80,128]{2,1,0:T(8,128)(2,1)S(1)} %get-tuple-element.30.refs_3_), channel_id=1, source_target_pairs={{0,128},{128,0},{1,129},{129,1},{2,130},{130,2},{3,131},{131,3},{4... | collective-permute-start | bytes 1474568 | tf_op jit(solution)/shard_map/ppermute | solution.py:410
  36.2 5.6 %copy-start.3 = (bf16[1,180,45,80]{1,3,2,0:T(8,128)(2,1)S(1)}, bf16[1,180,45,80]{1,3,2,0:T(8,128)(2,1)}, u32[]{:S(2)}) copy-start(bf16[1,180,45,80]{1,3,2,0:T(8,128)(2,1)} %param.5) | copy-start | bytes 3888004
  44.9 6.4 %collective-permute-start.5 = (bf16[17,80,128]{2,1,0:T(8,128)(2,1)S(1)}, bf16[17,80,128]{2,1,0:T(8,128)(2,1)S(1)}, u32[]{:S(2)}, u32[]{:S(2)}) collective-permute-start(bf16[17,80,128]{2,1,0:T(8,128)(2,1)S(1)} %get-tuple-element.29.refs_3_), channel_id=1, source_target_pairs={{0,128},{128,0},{1,129},{129,1},{2,130},{130,2},{3,131},{131,3},{4... | collective-permute-start | bytes 1044488 | tf_op jit(solution)/shard_map/ppermute | solution.py:410
  55.7 43.9 %copy-start.5 = (bf16[3,3,128,80]{2,3,1,0:T(8,128)(2,1)S(1)}, bf16[3,3,128,80]{2,3,1,0:T(8,128)(2,1)}, u32[]{:S(2)}) copy-start(bf16[3,3,128,80]{2,3,1,0:T(8,128)(2,1)} %param.7) | copy-start | bytes 552964
  55.8 18.2 %collective-permute-start.7 = (bf16[45,1,128]{2,1,0:T(2,128)(2,1)S(1)}, bf16[45,1,128]{2,1,0:T(2,128)(2,1)S(1)}, u32[]{:S(2)}, u32[]{:S(2)}) collective-permute-start(bf16[45,1,128]{2,1,0:T(2,128)(2,1)S(1)} %get-tuple-element.42), channel_id=1, source_target_pairs={{0,32},{64,96},{32,0},{96,64},{1,33},{65,97},{33,1},{97,65},{2,34}... | collective-permute-start | bytes 34568 | tf_op jit(solution)/shard_map/ppermute | solution.py:33
  59.3 14.7 %collective-permute-start.8 = (bf16[45,1,128]{2,1,0:T(2,128)(2,1)S(1)}, bf16[45,1,128]{2,1,0:T(2,128)(2,1)S(1)}, u32[]{:S(2)}, u32[]{:S(2)}) collective-permute-start(bf16[45,1,128]{2,1,0:T(2,128)(2,1)S(1)} %get-tuple-element.43), channel_id=1, source_target_pairs={{32,64},{64,32},{33,65},{65,33},{34,66},{66,34},{35,67},{67,35},{3... | collective-permute-start | bytes 34568 | tf_op jit(solution)/shard_map/ppermute | solution.py:34
  60.0 31.7 %all-to-all-start = ((f32[256,1,384]{2,1,0:T(1,128)}), f32[256,1,384]{2,1,0:T(1,128)S(1)}, u32[]{:S(2)}, u32[]{:S(2)}) async-start(f32[256,1,384]{2,1,0:T(1,128)} %bitcast.11), calls=%async_computation | async-start | bytes 786432 | tf_op jit(solution)/shard_map/all_to_all | solution.py:359
  74.3 3.4 %collective-permute-start.10 = (bf16[1,256,128]{2,1,0:T(8,128)(2,1)S(1)}, bf16[1,256,128]{2,1,0:T(8,128)(2,1)S(1)}, u32[]{:S(2)}, u32[]{:S(2)}) collective-permute-start(bf16[1,256,128]{2,1,0:T(8,128)(2,1)S(1)} %get-tuple-element.56), channel_id=1, source_target_pairs={{0,1},{2,3},{4,5},{6,7},{8,9},{10,11},{12,13},{14,15},{16,17},{18,... | collective-permute-start | bytes 196616 | tf_op jit(solution)/shard_map/ppermute | solution.py:33
  76.5 5.9 %collective-permute-start.9 = (bf16[1,256,128]{2,1,0:T(8,128)(2,1)S(1)}, bf16[1,256,128]{2,1,0:T(8,128)(2,1)S(1)}, u32[]{:S(2)}, u32[]{:S(2)}) collective-permute-start(bf16[1,256,128]{2,1,0:T(8,128)(2,1)S(1)} %get-tuple-element.57), channel_id=1, source_target_pairs={{1,2},{3,4},{5,6},{7,8},{9,10},{11,12},{13,14},{15,16},{17,18},{19... | collective-permute-start | bytes 196616 | tf_op jit(solution)/shard_map/ppermute | solution.py:34
  93.0 24.0 %all-to-all-start.1 = ((f32[256,1,384]{2,1,0:T(1,128)}), f32[256,1,384]{2,1,0:T(1,128)S(1)}, u32[]{:S(2)}, u32[]{:S(2)}) async-start(f32[256,1,384]{2,1,0:T(1,128)} %broadcast_in_dim.20), calls=%async_computation.1 | async-start | bytes 786432 | tf_op jit(solution)/shard_map/all_to_all | solution.py:359
